TPU v7x, 256 devices: a whole 4x4x8 slice. The times are simulated.
256 devices in a mesh: blk: 64 (over x_hi, y, z), row: 4 (over x_lo, core).
Axes of the slice: x: 4 (x_hi: 2, x_lo: 2; x = x_hi * 2 + x_lo), y: 4, z: 8, core: 2. Of those that a mesh axis runs over, the one named last changes fastest.
Arguments:
- pool_embeds: bfloat16 [65536, 768], P('blk'), may hold values from -24 to 24
- target_samples: bfloat16 [16384, 768], P(('blk', 'row')), may hold values from -6 to 6
- reference_samples: bfloat16 [16384, 768], P(('blk', 'row')), may hold values from -6 to 6
Outputs:
- log_ratio: float32 [65536], P('blk')
- standardized: float32 [65536], P('blk')
All inputs are finite; a program needn't handle non-finite values.
Results may differ from a plain program's by a relative error of at most 0.0003.
Values may be sent and summed in bfloat16 or wider, within the bound.
No kernel may reach another device: no remote copies, remote signals or barrier semaphores. Data moves between devices by JAX's collectives and lax.ppermute only.
A program may use at most 128 MiB of HBM per device.

v0:
```python
import functools

import jax
import jax.numpy as jnp
from jax import lax
from jax.experimental import pallas as pl
from jax.experimental.pallas import tpu as pltpu
from jax.sharding import Mesh, PartitionSpec as P


KERNEL_GAIN = 30.0
TILE = 256
CHUNK = 256
SIZES = {"xh": 2, "y": 4, "z": 8, "xl": 2, "core": 2}
ROW_GROUP = ("y", "xl", "core")
BLK = ("xh", "y", "z")
VMEM = pl.BlockSpec(memory_space=pltpu.VMEM)


def lse_tiles(pools, samples, each, scale, out_ref, joined, half_norm, pool_all, bufs, tops):
    rows = joined.shape[0]
    member = rows // 2
    i = 0
    for ref in samples:
        for unit in range(0, ref.shape[0], 2 * each):
            joined[i * each : (i + 1) * each, :] = ref[unit : unit + each, :]
            joined[member + i * each : member + (i + 1) * each, :] = ref[unit + each : unit + 2 * each, :]
            i += 1
    count = 0
    for ref in pools:
        pool_all[count : count + ref.shape[0], :] = ref[...]
        count += ref.shape[0]

    def norms(i, _):
        at = pl.ds(pl.multiple_of(i * 128, 128), 128)
        wide = joined[at, :].astype(jnp.float32)
        half_norm[at, :] = jnp.broadcast_to(jnp.sum(wide * wide, axis=1, keepdims=True) * 0.5, (128, 128))
        return 0

    lax.fori_loop(0, rows // 128, norms, 0)
    tiles = count // TILE

    def step(tile, buf, top, done, done_buf, done_top):
        if tile is not None:
            weights = pool_all[pl.ds(pl.multiple_of(tile * TILE, TILE), TILE), :]
        if done is not None:
            high = [jnp.max(done_top[8 * m : 8 * m + 8, :], axis=0, keepdims=True) for m in range(2)]
        highs, totals = [None, None], [None, None]
        for c in range(rows // CHUNK):
            m = c * CHUNK // member
            at = slice(c * CHUNK, (c + 1) * CHUNK)
            if tile is not None:
                products = lax.dot_general(
                    joined[at, :], weights, (((1,), (1,)), ((), ())), preferred_element_type=jnp.float32
                )
                values = products - jnp.concatenate([half_norm[at, :]] * (TILE // 128), axis=1)
                buf[at, :] = values
                top_of = jnp.max(values.reshape(CHUNK // 8, 8, TILE), axis=0)
                highs[m] = top_of if highs[m] is None else jnp.maximum(highs[m], top_of)
            if done is not None:
                powers = jnp.exp((done_buf[at, :] - high[m]) * scale)
                total = jnp.sum(powers.reshape(CHUNK // 8, 8, TILE), axis=0)
                totals[m] = total if totals[m] is None else totals[m] + total
        if tile is not None:
            for m in range(2):
                top[8 * m : 8 * m + 8, :] = highs[m]
        if done is not None:
            for m in range(2):
                value = high[m] * scale + jnp.log(jnp.sum(totals[m], axis=0, keepdims=True))
                for k in range(TILE // 128):
                    out_ref[m, pl.ds(done * (TILE // 128) + k, 1), :] = value[:, k * 128 : (k + 1) * 128]

    step(0, bufs[0], tops[0], None, None, None)

    def pair(i, _):
        step(2 * i + 1, bufs[1], tops[1], 2 * i, bufs[0], tops[0])
        step(2 * i + 2, bufs[0], tops[0], 2 * i + 1, bufs[1], tops[1])
        return 0

    lax.fori_loop(0, tiles // 2 - 1, pair, 0)
    step(tiles - 1, bufs[1], tops[1], tiles - 2, bufs[0], tops[0])
    step(None, None, None, tiles - 1, bufs[1], tops[1])


def partial_kernel(n_pools, n_samples, each, scale, *refs):
    pools, samples, out_ref = refs[:n_pools], refs[n_pools : n_pools + n_samples], refs[n_pools + n_samples]
    joined, half_norm, pool_all, buf0, buf1, top0, top1 = refs[n_pools + n_samples + 1 :]
    lse_tiles(pools, samples, each, scale, out_ref, joined, half_norm, pool_all, (buf0, buf1), (top0, top1))


def add_exp(a, b):
    high = jnp.maximum(a, b)
    return high + jnp.log(jnp.exp(a - high) + jnp.exp(b - high))


def last_kernel(n_pools, n_samples, each, scale, place, *refs):
    pools, samples = refs[:n_pools], refs[n_pools : n_pools + n_samples]
    first, second, out_ref, across = refs[n_pools + n_samples : n_pools + n_samples + 4]
    joined, half_norm, pool_all, buf0, buf1, top0, top1 = refs[n_pools + n_samples + 4 :]
    lse_tiles(pools, samples, each, scale, across, joined, half_norm, pool_all, (buf0, buf1), (top0, top1))
    y, core = place[0], place[1]
    near = add_exp(first[...], second[...])
    n = near.shape[1] // 3
    far = across[...]

    def put(owner, value, swapped):
        half = n // 2
        for j in range(4):
            at = lax.rem(owner, 4) * 4 + j
            if swapped:
                out_ref[at, :, pl.ds(core * half, half), :] = value[:, :half, :]
                out_ref[at, :, pl.ds((1 - core) * half, half), :] = value[:, half:, :]
            else:
                out_ref[at, :, :, :] = value

    put(y, near[:, :n, :], False)
    put(y + 3 - 2 * core, near[:, n : 2 * n, :], False)
    put(y + 1 + 2 * core, near[:, 2 * n :, :], False)
    put(y + 2, far, True)


def lse_call(pools, samples, each, scale, earlier=None, place=None):
    count = sum(p.shape[0] for p in pools)
    rows = sum(s.shape[0] for s in samples)
    depth = pools[0].shape[1]
    scratch = [
        pltpu.VMEM((rows, depth), jnp.bfloat16),
        pltpu.VMEM((rows, 128), jnp.float32),
        pltpu.VMEM((count, depth), jnp.bfloat16),
        pltpu.VMEM((rows, TILE), jnp.float32),
        pltpu.VMEM((rows, TILE), jnp.float32),
        pltpu.VMEM((16, TILE), jnp.float32),
        pltpu.VMEM((16, TILE), jnp.float32),
    ]
    partial = jax.ShapeDtypeStruct((2, count // 128, 128), jnp.float32)
    common = dict(
        out_specs=VMEM,
        compiler_params=pltpu.CompilerParams(vmem_limit_bytes=14 * 1024 * 1024),
        cost_estimate=pl.CostEstimate(
            flops=2 * rows * count * depth, bytes_accessed=2 * (rows + count) * depth, transcendentals=rows * count
        ),
    )
    inputs = [VMEM] * (len(pools) + len(samples))
    if earlier is None:
        kernel = functools.partial(partial_kernel, len(pools), len(samples), each, scale)
        return pl.pallas_call(kernel, out_shape=partial, in_specs=inputs, scratch_shapes=scratch, **common)(*pools, *samples)
    kernel = functools.partial(last_kernel, len(pools), len(samples), each, scale)
    return pl.pallas_call(
        kernel,
        out_shape=jax.ShapeDtypeStruct((16,) + partial.shape, jnp.float32),
        in_specs=[pl.BlockSpec(memory_space=pltpu.SMEM)] + inputs + [VMEM] * 2,
        scratch_shapes=[pltpu.VMEM(partial.shape, jnp.float32)] + scratch,
        **common,
    )(place, *pools, *samples, *earlier)


def merge_kernel(got, norms, ratio_ref, stats_ref):
    value = got[...]
    high = jnp.max(value, axis=0)
    total = high + jnp.log(jnp.sum(jnp.exp(value - high[None]), axis=0))
    log_target = total[0] - norms[...]
    log_ref = total[1] - norms[...]
    ratio = log_target - log_ref
    ratio_ref[...] = ratio
    count = ratio.shape[0] * ratio.shape[1]
    mean = jnp.sum(ratio, axis=(0, 1), keepdims=True) / count
    square = jnp.sum(jnp.square(ratio - mean), axis=(0, 1), keepdims=True) / count
    lane = lax.broadcasted_iota(jnp.int32, stats_ref.shape, 1)
    stats_ref[...] = jnp.where(lane == 0, mean, jnp.where(lane == 1, square, 0.0))


def finish_kernel(ratio, stats, out_ref):
    blocks = stats.shape[0]
    value = stats[...]
    mean = jnp.sum(value[:, 0:1], axis=0, keepdims=True) / blocks
    variance = jnp.sum(value[:, 1:2] + jnp.square(value[:, 0:1] - mean), axis=0, keepdims=True) / blocks
    out_ref[...] = (ratio[...] - mean) / jnp.sqrt(variance + 1e-05)


def swap_core(value):
    return lax.ppermute(value, "core", [(0, 1), (1, 0)])


def swap_x(value):
    return lax.ppermute(value, ("xh", "xl"), [(0, 3), (3, 0), (1, 2), (2, 1)])


def both_ways(value, axis):
    n = SIZES[axis]
    pairs = [(2 * i, 2 * ((i + 1) % n)) for i in range(n)] + [(2 * i + 1, 2 * ((i - 1) % n) + 1) for i in range(n)]
    return lax.ppermute(value, (axis, "core"), pairs)


def body(pool_embeds, target_samples, reference_samples):
    count, depth = pool_embeds.shape
    half = count // 2
    core = lax.axis_index("core")
    each = target_samples.shape[0]
    scale = 2.0 * KERNEL_GAIN / depth
    place = jnp.stack([lax.axis_index("y"), core]).astype(jnp.int32)

    own = jnp.concatenate([target_samples, reference_samples], axis=0)
    beside = both_ways(pool_embeds, "y")
    other = swap_x(own)
    block = jnp.concatenate([own, swap_core(own)], axis=0)
    z1 = both_ways(block, "z")
    other_block = jnp.concatenate([other, swap_core(other)], axis=0)
    zx1 = both_ways(other_block, "z")
    z2 = both_ways(z1, "z")
    zx2 = both_ways(zx1, "z")
    z3 = both_ways(z2, "z")
    zx3 = both_ways(zx2, "z")
    z4 = both_ways(z3[: 2 * each], "z")
    across = both_ways(lax.dynamic_slice_in_dim(beside, core * half, half, 0), "y")
    near = [pool_embeds, beside, swap_core(beside)]
    far = [across, swap_core(across)]
    early = [own, other, z1, zx1, z2]
    late = [zx2, z3, zx3, z4, swap_x(z4)]
    first = lse_call(near, early, each, scale)
    second = lse_call(near, late, each, scale)
    send = lse_call(far, early + late, each, scale, (first, second), place)

    got = lax.all_to_all(send, ROW_GROUP, 0, 0)
    pool_norms = jnp.sum(jnp.square(pool_embeds.astype(jnp.float32)), axis=1) * (KERNEL_GAIN / depth)
    dense = (count // 128, 128)
    blocks = lax.axis_size(BLK)
    log_ratio, stats = pl.pallas_call(
        merge_kernel,
        out_shape=(jax.ShapeDtypeStruct(dense, jnp.float32), jax.ShapeDtypeStruct((blocks, 128), jnp.float32)),
        in_specs=[VMEM, VMEM],
        out_specs=(VMEM, VMEM),
    )(got, pool_norms.reshape(dense))
    stats = lax.all_to_all(stats, BLK, 0, 0, tiled=True)
    standardized = pl.pallas_call(
        finish_kernel, out_shape=jax.ShapeDtypeStruct(dense, jnp.float32), in_specs=[VMEM, VMEM], out_specs=VMEM
    )(log_ratio, stats)
    return (log_ratio.reshape(count), standardized.reshape(count))


def solution(mesh):
    fine = Mesh(mesh.devices.reshape(2, 4, 8, 2, 2), ("xh", "y", "z", "xl", "core"))
    rows = P(BLK, None)
    samples = P(("xh", "y", "z", "xl", "core"), None)
    return jax.shard_map(
        body, mesh=fine, in_specs=(rows, samples, samples), out_specs=(P(BLK), P(BLK)), check_vma=False
    )
```

profile of v0, /device:TPU:32, one launch (start us, length us, event | category | flops | bytes accessed | tf_op | source)
XLA Modules:
  0.0 127.2 jit_solution(7258762607499408461)
XLA Ops:
  0.6 1.7 %collective-permute-start = (bf16[1024,768]{1,0:T(8,128)(2,1)}, bf16[1024,768]{1,0:T(8,128)(2,1)S(1)}, u32[]{:S(2)}, u32[]{:S(2)}) collective-permute-start(bf16[1024,768]{1,0:T(8,128)(2,1)} %refs_0_.3), channel_id=1, source_target_pairs={{0,32},{32,64},{64,96},{96,0},{1,97},{33,1},{65,33},{97,65},{2,34}... | collective-permute-start | bytes 4718600 | tf_op jit(solution)/shard_map/ppermute | solution.py:191
  2.3 0.9 constant_dynamic-update-slice_fusion.1
  3.2 0.9 constant_dynamic-update-slice_fusion.refs_3_.refs_2_
  4.1 1.0 collective-permute-start.4
  5.1 17.5 %collective-permute-done.refs_1_ = bf16[1024,768]{1,0:T(8,128)(2,1)S(1)} collective-permute-done((bf16[1024,768]{1,0:T(8,128)(2,1)}, bf16[1024,768]{1,0:T(8,128)(2,1)S(1)}, u32[]{:S(2)}, u32[]{:S(2)}) %collective-permute-start) | collective-permute-done | bytes 1572896 | tf_op jit(solution)/shard_map/ppermute | solution.py:191
  22.5 0.0 collective-permute-start.14
  22.5 0.0 collective-permute-done.4
  22.6 1.7 %pad_maximum_fusion = bf16[256,768]{1,0:T(8,128)(2,1)} fusion(bf16[128,768]{1,0:T(8,128)(2,1)S(1)} %collective-permute-done.4, bf16[64,768]{1,0:T(8,128)(2,1)} %param.5, bf16[64,768]{1,0:T(8,128)(2,1)} %param.4), kind=kLoop, calls=%fused_computation.1 | loop fusion | flops 1179648 | bytes 786432 | tf_op jit(solution)/shard_map/concatenate | solution.py:205
  24.3 1.9 %collective-permute-start.5 = (bf16[256,768]{1,0:T(8,128)(2,1)}, bf16[256,768]{1,0:T(8,128)(2,1)}, u32[]{:S(2)}, u32[]{:S(2)}) collective-permute-start(bf16[256,768]{1,0:T(8,128)(2,1)} %pad_maximum_fusion), channel_id=1, source_target_pairs={{0,4},{4,8},{8,12},{12,16},{16,20},{20,24},{24,28},{28,0},{1,29},{... | collective-permute-start | bytes 1179656 | tf_op jit(solution)/shard_map/ppermute | solution.py:191
  26.2 2.8 %collective-permute-start.3 = (bf16[128,768]{1,0:T(8,128)(2,1)S(1)}, bf16[128,768]{1,0:T(8,128)(2,1)S(1)}, u32[]{:S(2)}, u32[]{:S(2)}) collective-permute-start(bf16[128,768]{1,0:T(8,128)(2,1)S(1)} %constant_dynamic-update-slice_fusion.refs_3_.refs_2_), channel_id=1, source_target_pairs={{0,130},{130,0},{2,128},{128,2},{1,131},{131,1},{3,129},{129,3},{4... | collective-permute-start | bytes 589832 | tf_op jit(solution)/shard_map/ppermute | solution.py:185
  28.9 5.4 %collective-permute-done.3.refs_4_.refs_3_ = bf16[128,768]{1,0:T(8,128)(2,1)S(1)} collective-permute-done((bf16[128,768]{1,0:T(8,128)(2,1)S(1)}, bf16[128,768]{1,0:T(8,128)(2,1)S(1)}, u32[]{:S(2)}, u32[]{:S(2)}) %collective-permute-start.3) | collective-permute-done | bytes 196640 | tf_op jit(solution)/shard_map/ppermute | solution.py:185
  34.3 0.0 collective-permute-start.6
  34.3 0.0 collective-permute-done.5.refs_5_.refs_4_
  34.3 0.7 collective-permute-start.8
  35.0 0.9 collective-permute-done.6
  35.9 1.0 pad_maximum_fusion.1
  36.9 2.3 %collective-permute-start.7 = (bf16[256,768]{1,0:T(8,128)(2,1)S(1)}, bf16[256,768]{1,0:T(8,128)(2,1)}, u32[]{:S(2)}, u32[]{:S(2)}) collective-permute-start(bf16[256,768]{1,0:T(8,128)(2,1)S(1)} %pad_maximum_fusion.1), channel_id=1, source_target_pairs={{0,4},{4,8},{8,12},{12,16},{16,20},{20,24},{24,28},{28,0},{1,29},{... | collective-permute-start | bytes 1179656 | tf_op jit(solution)/shard_map/ppermute | solution.py:191
  39.2 0.9 constant_dynamic-slice_fusion
  40.1 0.4 collective-permute-start.1
  40.5 2.0 %collective-permute-done.8.refs_7_.refs_6_ = bf16[256,768]{1,0:T(8,128)(2,1)} collective-permute-done((bf16[256,768]{1,0:T(8,128)(2,1)}, bf16[256,768]{1,0:T(8,128)(2,1)}, u32[]{:S(2)}, u32[]{:S(2)}) %collective-permute-start.8) | collective-permute-done | bytes 393248 | tf_op jit(solution)/shard_map/ppermute | solution.py:191
  42.5 1.2 collective-permute-start.10
  43.7 3.0 %collective-permute-done.7.refs_6_.refs_5_ = bf16[256,768]{1,0:T(8,128)(2,1)} collective-permute-done((bf16[256,768]{1,0:T(8,128)(2,1)S(1)}, bf16[256,768]{1,0:T(8,128)(2,1)}, u32[]{:S(2)}, u32[]{:S(2)}) %collective-permute-start.7) | collective-permute-done | bytes 393248 | tf_op jit(solution)/shard_map/ppermute | solution.py:191
  46.7 1.1 collective-permute-start.9
  47.8 0.1 pad_add_fusion.place
  47.9 3.9 %collective-permute-done.10.refs_4_.refs_8_ = bf16[256,768]{1,0:T(8,128)(2,1)} collective-permute-done((bf16[256,768]{1,0:T(8,128)(2,1)}, bf16[256,768]{1,0:T(8,128)(2,1)}, u32[]{:S(2)}, u32[]{:S(2)}) %collective-permute-start.10) | collective-permute-done | bytes 393248 | tf_op jit(solution)/shard_map/ppermute | solution.py:191
  51.8 0.9 slice.4
  52.7 0.4 collective-permute-start.12
  53.2 0.4 multiply_reduce_fusion
  53.6 2.4 %collective-permute-done.9.refs_3_.refs_7_ = bf16[256,768]{1,0:T(8,128)(2,1)} collective-permute-done((bf16[256,768]{1,0:T(8,128)(2,1)}, bf16[256,768]{1,0:T(8,128)(2,1)}, u32[]{:S(2)}, u32[]{:S(2)}) %collective-permute-start.9) | collective-permute-done | bytes 393248 | tf_op jit(solution)/shard_map/ppermute | solution.py:191
  56.0 0.9 collective-permute-start.11
  56.9 2.8 %collective-permute-done.12.refs_6_.refs_10_ = bf16[128,768]{1,0:T(8,128)(2,1)S(1)} collective-permute-done((bf16[128,768]{1,0:T(8,128)(2,1)S(1)}, bf16[128,768]{1,0:T(8,128)(2,1)S(1)}, u32[]{:S(2)}, u32[]{:S(2)}) %collective-permute-start.12) | collective-permute-done | bytes 196640 | tf_op jit(solution)/shard_map/ppermute | solution.py:191
  59.7 2.8 %collective-permute-start.13 = (bf16[128,768]{1,0:T(8,128)(2,1)S(1)}, bf16[128,768]{1,0:T(8,128)(2,1)S(1)}, u32[]{:S(2)}, u32[]{:S(2)}) collective-permute-start(bf16[128,768]{1,0:T(8,128)(2,1)S(1)} %collective-permute-done.12.refs_6_.refs_10_), channel_id=1, source_target_pairs={{0,130},{130,0},{2,128},{128,2},{1,131},{131,1},{3,129},{129,3},{4... | collective-permute-start | bytes 589832 | tf_op jit(solution)/shard_map/ppermute | solution.py:185
  62.5 0.0 collective-permute-done.1.refs_0_
  62.5 0.0 collective-permute-start.2
  62.5 0.0 collective-permute-done.14.refs_2_
  62.5 9.9 %shard_map.50.refs_12_ = f32[2,24,128]{2,1,0:T(8,128)S(1)} custom-call(bf16[1024,768]{1,0:T(8,128)(2,1)S(1)} %copy-done, bf16[1024,768]{1,0:T(8,128)(2,1)S(1)} %collective-permute-done.refs_1_, bf16[1024,768]{1,0:T(8,128)(2,1)} %collective-permute-done.14.refs_2_, bf16[128,768]{1,0:T(8,128)(2,1)S(1)} %constant_dynamic-update-slice_fusion.refs_3_.refs_2_, ...), custom_call_target="tpu_custom_call" | custom-call | flops 4831838208 | bytes 6291456 | tf_op jit(solution)/shard_map/pallas_call | solution.py:146
  72.4 0.0 collective-permute-done.11.refs_5_.refs_9_
  72.4 0.0 collective-permute-done.13.refs_7_.refs_11_
  72.4 9.8 %shard_map.51.refs_13_ = f32[2,24,128]{2,1,0:T(8,128)S(1)} custom-call(bf16[1024,768]{1,0:T(8,128)(2,1)S(1)} %copy-done, bf16[1024,768]{1,0:T(8,128)(2,1)S(1)} %collective-permute-done.refs_1_, bf16[1024,768]{1,0:T(8,128)(2,1)} %collective-permute-done.14.refs_2_, bf16[256,768]{1,0:T(8,128)(2,1)} %collective-permute-done.9.refs_3_.refs_7_, ...), custom_call_target="tpu_custom_call" | custom-call | flops 4831838208 | bytes 6291456 | tf_op jit(solution)/shard_map/pallas_call | solution.py:146
  82.2 0.0 collective-permute-done.2.refs_1_
  82.2 9.0 %shard_map.52 = f32[16,2,8,128]{3,2,1,0:T(8,128)} custom-call(s32[2]{0:T(128)S(1)} %pad_add_fusion.place, bf16[512,768]{1,0:T(8,128)(2,1)} %collective-permute-done.1.refs_0_, bf16[512,768]{1,0:T(8,128)(2,1)S(1)} %collective-permute-done.2.refs_1_, bf16[128,768]{1,0:T(8,128)(2,1)S(1)} %constant_dynamic-update-slice_fusion.refs_3_.refs_2_, ...), custom_call_target="tpu_custom_call" | custom-call | flops 3221225472 | bytes 4718592 | tf_op jit(solution)/shard_map/pallas_call | solution.py:148
  91.2 3.5 %all-to-all-start = ((f32[16,2,8,128]{3,2,1,0:T(8,128)}), f32[16,2,8,128]{3,2,1,0:T(8,128)S(1)}, u32[]{:S(2)}, u32[]{:S(2)}) async-start(f32[16,2,8,128]{3,2,1,0:T(8,128)} %shard_map.52), calls=%async_computation | async-start | bytes 262144 | tf_op jit(solution)/shard_map/all_to_all | solution.py:223
  94.7 0.6 multiply_bitcast_fusion.norms
  95.3 6.0 %all-to-all-done.got = f32[16,2,8,128]{3,2,1,0:T(8,128)S(1)} async-done(((f32[16,2,8,128]{3,2,1,0:T(8,128)}), f32[16,2,8,128]{3,2,1,0:T(8,128)S(1)}, u32[]{:S(2)}, u32[]{:S(2)}) %all-to-all-start) | async-done | bytes 131104 | tf_op jit(solution)/shard_map/all_to_all | solution.py:223
  101.4 0.7 copy-done.1
  102.0 1.8 %shard_map.53 = (f32[8,128]{1,0:T(8,128)}, f32[64,128]{1,0:T(8,128)}) custom-call(f32[16,2,8,128]{3,2,1,0:T(8,128)} %copy-done.1, f32[8,128]{1,0:T(8,128)} %multiply_bitcast_fusion.norms), custom_call_target="tpu_custom_call" | custom-call | tf_op jit(solution)/shard_map/pallas_call | solution.py:227
  103.8 21.9 %all_to_all.16 = f32[64,1,128]{2,1,0:T(1,128)} all-to-all(f32[64,1,128]{2,1,0:T(1,128)} %bitcast.11), channel_id=1, replica_groups=mesh['xh'=2,'y'=4,'z'=8,'xl'=2,'core'=2] {'xh','y','z'}, dimensions={0} | all-to-all | bytes 65536 | tf_op jit(solution)/shard_map/all_to_all | solution.py:233
  125.7 1.6 %shard_map.54 = f32[8,128]{1,0:T(8,128)} custom-call(f32[8,128]{1,0:T(8,128)} %get-tuple-element.4.ratio, f32[64,128]{1,0:T(8,128)} %bitcast.10), custom_call_target="tpu_custom_call" | custom-call | tf_op jit(solution)/shard_map/pallas_call | solution.py:234
  (3 shorter events, 0.0 us)
Async XLA Ops:
  0.6 21.9 %collective-permute-start = (bf16[1024,768]{1,0:T(8,128)(2,1)}, bf16[1024,768]{1,0:T(8,128)(2,1)S(1)}, u32[]{:S(2)}, u32[]{:S(2)}) collective-permute-start(bf16[1024,768]{1,0:T(8,128)(2,1)} %refs_0_.3), channel_id=1, source_target_pairs={{0,32},{32,64},{64,96},{96,0},{1,97},{33,1},{65,33},{97,65},{2,34}... | collective-permute-start | bytes 4718600 | tf_op jit(solution)/shard_map/ppermute | solution.py:191
  4.1 18.5 %collective-permute-start.4 = (bf16[128,768]{1,0:T(8,128)(2,1)S(1)}, bf16[128,768]{1,0:T(8,128)(2,1)S(1)}, u32[]{:S(2)}, u32[]{:S(2)}) collective-permute-start(bf16[128,768]{1,0:T(8,128)(2,1)S(1)} %constant_dynamic-update-slice_fusion.refs_3_.refs_2_), channel_id=1, source_target_pairs={{0,1},{1,0},{2,3},{3,2},{4,5},{5,4},{6,7},{7,6},{8,9},{9,8},{10,11... | collective-permute-start | bytes 589832 | tf_op jit(solution)/shard_map/ppermute | solution.py:181
  22.5 39.9 %collective-permute-start.14 = (bf16[1024,768]{1,0:T(8,128)(2,1)S(1)}, bf16[1024,768]{1,0:T(8,128)(2,1)}, u32[]{:S(2)}, u32[]{:S(2)}) collective-permute-start(bf16[1024,768]{1,0:T(8,128)(2,1)S(1)} %collective-permute-done.refs_1_), channel_id=1, source_target_pairs={{0,1},{1,0},{2,3},{3,2},{4,5},{5,4},{6,7},{7,6},{8,9},{9,8},{10,11... | collective-permute-start | bytes 4718600 | tf_op jit(solution)/shard_map/ppermute | solution.py:181
  24.3 28.9 %copy-start = (bf16[1024,768]{1,0:T(8,128)(2,1)S(1)}, bf16[1024,768]{1,0:T(8,128)(2,1)}, u32[]{:S(2)}) copy-start(bf16[1024,768]{1,0:T(8,128)(2,1)} %refs_0_.3) | copy-start | bytes 4718596
  24.3 10.1 %collective-permute-start.5 = (bf16[256,768]{1,0:T(8,128)(2,1)}, bf16[256,768]{1,0:T(8,128)(2,1)}, u32[]{:S(2)}, u32[]{:S(2)}) collective-permute-start(bf16[256,768]{1,0:T(8,128)(2,1)} %pad_maximum_fusion), channel_id=1, source_target_pairs={{0,4},{4,8},{8,12},{12,16},{16,20},{20,24},{24,28},{28,0},{1,29},{... | collective-permute-start | bytes 1179656 | tf_op jit(solution)/shard_map/ppermute | solution.py:191
  26.2 8.1 %collective-permute-start.3 = (bf16[128,768]{1,0:T(8,128)(2,1)S(1)}, bf16[128,768]{1,0:T(8,128)(2,1)S(1)}, u32[]{:S(2)}, u32[]{:S(2)}) collective-permute-start(bf16[128,768]{1,0:T(8,128)(2,1)S(1)} %constant_dynamic-update-slice_fusion.refs_3_.refs_2_), channel_id=1, source_target_pairs={{0,130},{130,0},{2,128},{128,2},{1,131},{131,1},{3,129},{129,3},{4... | collective-permute-start | bytes 589832 | tf_op jit(solution)/shard_map/ppermute | solution.py:185
  34.3 1.6 %collective-permute-start.6 = (bf16[128,768]{1,0:T(8,128)(2,1)S(1)}, bf16[128,768]{1,0:T(8,128)(2,1)}, u32[]{:S(2)}, u32[]{:S(2)}) collective-permute-start(bf16[128,768]{1,0:T(8,128)(2,1)S(1)} %collective-permute-done.3.refs_4_.refs_3_), channel_id=1, source_target_pairs={{0,1},{1,0},{2,3},{3,2},{4,5},{5,4},{6,7},{7,6},{8,9},{9,8},{10,11... | collective-permute-start | bytes 589832 | tf_op jit(solution)/shard_map/ppermute | solution.py:181
  34.3 8.2 %collective-permute-start.8 = (bf16[256,768]{1,0:T(8,128)(2,1)}, bf16[256,768]{1,0:T(8,128)(2,1)}, u32[]{:S(2)}, u32[]{:S(2)}) collective-permute-start(bf16[256,768]{1,0:T(8,128)(2,1)} %collective-permute-done.5.refs_5_.refs_4_), channel_id=1, source_target_pairs={{0,4},{4,8},{8,12},{12,16},{16,20},{20,24},{24,28},{28,0},{1,29},{... | collective-permute-start | bytes 1179656 | tf_op jit(solution)/shard_map/ppermute | solution.py:191
  36.9 9.8 %collective-permute-start.7 = (bf16[256,768]{1,0:T(8,128)(2,1)S(1)}, bf16[256,768]{1,0:T(8,128)(2,1)}, u32[]{:S(2)}, u32[]{:S(2)}) collective-permute-start(bf16[256,768]{1,0:T(8,128)(2,1)S(1)} %pad_maximum_fusion.1), channel_id=1, source_target_pairs={{0,4},{4,8},{8,12},{12,16},{16,20},{20,24},{24,28},{28,0},{1,29},{... | collective-permute-start | bytes 1179656 | tf_op jit(solution)/shard_map/ppermute | solution.py:191
  40.1 22.4 %collective-permute-start.1 = (bf16[512,768]{1,0:T(8,128)(2,1)}, bf16[512,768]{1,0:T(8,128)(2,1)}, u32[]{:S(2)}, u32[]{:S(2)}) collective-permute-start(bf16[512,768]{1,0:T(8,128)(2,1)} %constant_dynamic-slice_fusion), channel_id=1, source_target_pairs={{0,32},{32,64},{64,96},{96,0},{1,97},{33,1},{65,33},{97,65},{2,34}... | collective-permute-start | bytes 2359304 | tf_op jit(solution)/shard_map/ppermute | solution.py:191
  42.5 9.3 %collective-permute-start.10 = (bf16[256,768]{1,0:T(8,128)(2,1)}, bf16[256,768]{1,0:T(8,128)(2,1)}, u32[]{:S(2)}, u32[]{:S(2)}) collective-permute-start(bf16[256,768]{1,0:T(8,128)(2,1)} %collective-permute-done.8.refs_7_.refs_6_), channel_id=1, source_target_pairs={{0,4},{4,8},{8,12},{12,16},{16,20},{20,24},{24,28},{28,0},{1,29},{... | collective-permute-start | bytes 1179656 | tf_op jit(solution)/shard_map/ppermute | solution.py:191
  46.7 9.3 %collective-permute-start.9 = (bf16[256,768]{1,0:T(8,128)(2,1)}, bf16[256,768]{1,0:T(8,128)(2,1)}, u32[]{:S(2)}, u32[]{:S(2)}) collective-permute-start(bf16[256,768]{1,0:T(8,128)(2,1)} %collective-permute-done.7.refs_6_.refs_5_), channel_id=1, source_target_pairs={{0,4},{4,8},{8,12},{12,16},{16,20},{20,24},{24,28},{28,0},{1,29},{... | collective-permute-start | bytes 1179656 | tf_op jit(solution)/shard_map/ppermute | solution.py:191
  52.7 7.0 %collective-permute-start.12 = (bf16[128,768]{1,0:T(8,128)(2,1)S(1)}, bf16[128,768]{1,0:T(8,128)(2,1)S(1)}, u32[]{:S(2)}, u32[]{:S(2)}) collective-permute-start(bf16[128,768]{1,0:T(8,128)(2,1)S(1)} %slice.4), channel_id=1, source_target_pairs={{0,4},{4,8},{8,12},{12,16},{16,20},{20,24},{24,28},{28,0},{1,29},{... | collective-permute-start | bytes 589832 | tf_op jit(solution)/shard_map/ppermute | solution.py:191
  56.0 16.4 %collective-permute-start.11 = (bf16[256,768]{1,0:T(8,128)(2,1)}, bf16[256,768]{1,0:T(8,128)(2,1)S(1)}, u32[]{:S(2)}, u32[]{:S(2)}) collective-permute-start(bf16[256,768]{1,0:T(8,128)(2,1)} %collective-permute-done.9.refs_3_.refs_7_), channel_id=1, source_target_pairs={{0,4},{4,8},{8,12},{12,16},{16,20},{20,24},{24,28},{28,0},{1,29},{... | collective-permute-start | bytes 1179656 | tf_op jit(solution)/shard_map/ppermute | solution.py:191
  59.7 12.7 %collective-permute-start.13 = (bf16[128,768]{1,0:T(8,128)(2,1)S(1)}, bf16[128,768]{1,0:T(8,128)(2,1)S(1)}, u32[]{:S(2)}, u32[]{:S(2)}) collective-permute-start(bf16[128,768]{1,0:T(8,128)(2,1)S(1)} %collective-permute-done.12.refs_6_.refs_10_), channel_id=1, source_target_pairs={{0,130},{130,0},{2,128},{128,2},{1,131},{131,1},{3,129},{129,3},{4... | collective-permute-start | bytes 589832 | tf_op jit(solution)/shard_map/ppermute | solution.py:185
  62.5 19.8 %collective-permute-start.2 = (bf16[512,768]{1,0:T(8,128)(2,1)}, bf16[512,768]{1,0:T(8,128)(2,1)S(1)}, u32[]{:S(2)}, u32[]{:S(2)}) collective-permute-start(bf16[512,768]{1,0:T(8,128)(2,1)} %collective-permute-done.1.refs_0_), channel_id=1, source_target_pairs={{0,1},{1,0},{2,3},{3,2},{4,5},{5,4},{6,7},{7,6},{8,9},{9,8},{10,11... | collective-permute-start | bytes 2359304 | tf_op jit(solution)/shard_map/ppermute | solution.py:181
  91.2 10.2 %all-to-all-start = ((f32[16,2,8,128]{3,2,1,0:T(8,128)}), f32[16,2,8,128]{3,2,1,0:T(8,128)S(1)}, u32[]{:S(2)}, u32[]{:S(2)}) async-start(f32[16,2,8,128]{3,2,1,0:T(8,128)} %shard_map.52), calls=%async_computation | async-start | bytes 262144 | tf_op jit(solution)/shard_map/all_to_all | solution.py:223
  101.4 0.7 copy-start.1
where the time goes:
time: 129 us; the launch traced here: 127 us
  waiting for transfers between devices  43.9 us (34%)
  Pallas kernels  32 us (25%)
  blocking collectives  21.9 us (17%)
  starting transfers between devices  20.7 us (16%)
  local copies, waits for them, and re-layouts  4.33 us (3%)
  other arithmetic  3.71 us (3%)
    ppermute x9, waiting for transfers between devices, both_ways(): return lax.ppermute(value, (axis, 'core'), pairs)  31.6 us
    all_to_all x1, blocking collectives, body(): stats = lax.all_to_all(stats, BLK, 0, 0, tiled=True)  21.9 us
    pallas_call x2, Pallas kernels, lse_call(): pl.pallas_call(kernel, out_shape=partial, in_specs=inputs, scratch_shapes...  19.7 us
    ppermute x9, starting transfers between devices, both_ways(): return lax.ppermute(value, (axis, 'core'), pairs)  10.6 us
    pallas_call x1, Pallas kernels, lse_call(): pl.pallas_call(kernel, out_shape=jax.ShapeDtypeStruct((16,) + partial.sha...  9 us
    all_to_all x1, waiting for transfers between devices, body(): got = lax.all_to_all(send, ROW_GROUP, 0, 0)  6.04 us
    ppermute x2, starting transfers between devices, swap_x(): return lax.ppermute(value, ('xh', 'xl'), [(0, 3), (3, 0), (1, 2), (2, 1)])  5.52 us
    ppermute x2, waiting for transfers between devices, swap_x(): return lax.ppermute(value, ('xh', 'xl'), [(0, 3), (3, 0), (1, 2), (2, 1)])  5.39 us
  transfers between devices with their start and end apart: 16, of which 9 were waited for; matrix products, arithmetic and copies ran while one was open for 6% of the time, Pallas kernels for 15%

commit v1 on v0

--- a/solution.py
+++ b/solution.py
@@ -10,7 +10,7 @@
 
 KERNEL_GAIN = 30.0
 TILE = 256
-CHUNK = 256
+CHUNK = 384
 SIZES = {"xh": 2, "y": 4, "z": 8, "xl": 2, "core": 2}
 ROW_GROUP = ("y", "xl", "core")
 BLK = ("xh", "y", "z")
@@ -39,6 +39,7 @@
 
     lax.fori_loop(0, rows // 128, norms, 0)
     tiles = count // TILE
+    chunk = member // -(-member // CHUNK)
 
     def step(tile, buf, top, done, done_buf, done_top):
         if tile is not None:
@@ -46,20 +47,20 @@
         if done is not None:
             high = [jnp.max(done_top[8 * m : 8 * m + 8, :], axis=0, keepdims=True) for m in range(2)]
         highs, totals = [None, None], [None, None]
-        for c in range(rows // CHUNK):
-            m = c * CHUNK // member
-            at = slice(c * CHUNK, (c + 1) * CHUNK)
+        for c in range(rows // chunk):
+            m = c * chunk // member
+            at = slice(c * chunk, (c + 1) * chunk)
             if tile is not None:
                 products = lax.dot_general(
                     joined[at, :], weights, (((1,), (1,)), ((), ())), preferred_element_type=jnp.float32
                 )
                 values = products - jnp.concatenate([half_norm[at, :]] * (TILE // 128), axis=1)
                 buf[at, :] = values
-                top_of = jnp.max(values.reshape(CHUNK // 8, 8, TILE), axis=0)
+                top_of = jnp.max(values.reshape(chunk // 8, 8, TILE), axis=0)
                 highs[m] = top_of if highs[m] is None else jnp.maximum(highs[m], top_of)
             if done is not None:
                 powers = jnp.exp((done_buf[at, :] - high[m]) * scale)
-                total = jnp.sum(powers.reshape(CHUNK // 8, 8, TILE), axis=0)
+                total = jnp.sum(powers.reshape(chunk // 8, 8, TILE), axis=0)
                 totals[m] = total if totals[m] is None else totals[m] + total
         if tile is not None:
             for m in range(2):
@@ -95,13 +96,13 @@
 
 def last_kernel(n_pools, n_samples, each, scale, place, *refs):
     pools, samples = refs[:n_pools], refs[n_pools : n_pools + n_samples]
-    first, second, out_ref, across = refs[n_pools + n_samples : n_pools + n_samples + 4]
-    joined, half_norm, pool_all, buf0, buf1, top0, top1 = refs[n_pools + n_samples + 4 :]
-    lse_tiles(pools, samples, each, scale, across, joined, half_norm, pool_all, (buf0, buf1), (top0, top1))
+    first, second, third, out_ref, last = refs[n_pools + n_samples : n_pools + n_samples + 5]
+    joined, half_norm, pool_all, buf0, buf1, top0, top1 = refs[n_pools + n_samples + 5 :]
+    lse_tiles(pools, samples, each, scale, last, joined, half_norm, pool_all, (buf0, buf1), (top0, top1))
     y, core = place[0], place[1]
-    near = add_exp(first[...], second[...])
-    n = near.shape[1] // 3
-    far = across[...]
+    n = first.shape[1] // 3
+    near = add_exp(add_exp(first[...], second[...]), last[:, : 3 * n, :])
+    far = add_exp(third[...], last[:, 3 * n :, :])
 
     def put(owner, value, swapped):
         half = n // 2
@@ -147,8 +148,8 @@
     kernel = functools.partial(last_kernel, len(pools), len(samples), each, scale)
     return pl.pallas_call(
         kernel,
-        out_shape=jax.ShapeDtypeStruct((16,) + partial.shape, jnp.float32),
-        in_specs=[pl.BlockSpec(memory_space=pltpu.SMEM)] + inputs + [VMEM] * 2,
+        out_shape=jax.ShapeDtypeStruct((16, 2, pools[0].shape[0] // 128, 128), jnp.float32),
+        in_specs=[pl.BlockSpec(memory_space=pltpu.SMEM)] + inputs + [VMEM] * len(earlier),
         scratch_shapes=[pltpu.VMEM(partial.shape, jnp.float32)] + scratch,
         **common,
     )(place, *pools, *samples, *earlier)
@@ -199,7 +200,11 @@
     scale = 2.0 * KERNEL_GAIN / depth
     place = jnp.stack([lax.axis_index("y"), core]).astype(jnp.int32)
 
-    own = jnp.concatenate([target_samples, reference_samples], axis=0)
+    own = jnp.where(
+        lax.broadcasted_iota(jnp.int32, (2 * each, depth), 0) < each,
+        jnp.pad(target_samples, ((0, each), (0, 0))),
+        jnp.pad(reference_samples, ((each, 0), (0, 0))),
+    )
     beside = both_ways(pool_embeds, "y")
     other = swap_x(own)
     block = jnp.concatenate([own, swap_core(own)], axis=0)
@@ -214,11 +219,12 @@
     across = both_ways(lax.dynamic_slice_in_dim(beside, core * half, half, 0), "y")
     near = [pool_embeds, beside, swap_core(beside)]
     far = [across, swap_core(across)]
-    early = [own, other, z1, zx1, z2]
-    late = [zx2, z3, zx3, z4, swap_x(z4)]
-    first = lse_call(near, early, each, scale)
-    second = lse_call(near, late, each, scale)
-    send = lse_call(far, early + late, each, scale, (first, second), place)
+    earliest, early = [own, other, z1, zx1], [z2, zx2]
+    late = [z3, zx3, z4, swap_x(z4)]
+    first = lse_call(near, earliest, each, scale)
+    second = lse_call(near, early, each, scale)
+    third = lse_call(far, earliest + early, each, scale)
+    send = lse_call(near + far, late, each, scale, (first, second, third), place)
 
     got = lax.all_to_all(send, ROW_GROUP, 0, 0)
     pool_norms = jnp.sum(jnp.square(pool_embeds.astype(jnp.float32)), axis=1) * (KERNEL_GAIN / depth)

time: 129 us -> 131 us (1.016)
  Pallas kernels: 32 us -> 35.4 us
  waiting for transfers between devices: 43.9 us -> 46 us
  local copies, waits for them, and re-layouts: 4.33 us -> 2.53 us
    ppermute x9, waiting for transfers between devices: 31.6 us -> 35.1 us  [both_ways(): return lax.ppermute(value, (axis, 'core'), pairs)]
    pallas_call x1, Pallas kernels: 9 us -> 11.3 us  [lse_call(): pl.pallas_call(kernel, out_shape=jax.ShapeDtypeStruct((16, 2, pools[0].sh...]
    pallas_call x2 -> x3, Pallas kernels: 19.7 us -> 20.8 us  [lse_call(): pl.pallas_call(kernel, out_shape=partial, in_specs=inputs, scratch_shapes...]
  transfers between devices with their start and end apart: 16 -> 16, of which waited for: 9 -> 9; matrix products, arithmetic and copies ran while one was open for 6% -> 4% of each run, Pallas kernels for 15% -> 16%
where the time goes in v1:
time: 131 us; the launch traced here: 130 us
  waiting for transfers between devices  46 us (35%)
  Pallas kernels  35.4 us (27%)
  blocking collectives  21.6 us (16%)
  starting transfers between devices  20.4 us (16%)
  other arithmetic  2.9 us (2%)
  local copies, waits for them, and re-layouts  2.53 us (2%)
    ppermute x9, waiting for transfers between devices, both_ways(): return lax.ppermute(value, (axis, 'core'), pairs)  35.1 us
    all_to_all x1, blocking collectives, body(): stats = lax.all_to_all(stats, BLK, 0, 0, tiled=True)  21.6 us
    pallas_call x3, Pallas kernels, lse_call(): pl.pallas_call(kernel, out_shape=partial, in_specs=inputs, scratch_shapes...  20.8 us
    pallas_call x1, Pallas kernels, lse_call(): pl.pallas_call(kernel, out_shape=jax.ShapeDtypeStruct((16, 2, pools[0].sh...  11.3 us
    ppermute x9, starting transfers between devices, both_ways(): return lax.ppermute(value, (axis, 'core'), pairs)  10.1 us
    all_to_all x1, waiting for transfers between devices, body(): got = lax.all_to_all(send, ROW_GROUP, 0, 0)  6.07 us
    ppermute x2, starting transfers between devices, swap_x(): return lax.ppermute(value, ('xh', 'xl'), [(0, 3), (3, 0), (1, 2), (2, 1)])  5.52 us
    ppermute x2, waiting for transfers between devices, swap_x(): return lax.ppermute(value, ('xh', 'xl'), [(0, 3), (3, 0), (1, 2), (2, 1)])  4.09 us
  transfers between devices with their start and end apart: 16, of which 9 were waited for; matrix products, arithmetic and copies ran while one was open for 4% of the time, Pallas kernels for 16%

profile of v1, /device:TPU:32, one launch (start us, length us, event | category | flops | bytes accessed | tf_op | source)
XLA Modules:
  0.0 129.6 jit_solution(15766337379763340340)
XLA Ops:
  0.6 1.7 %collective-permute-start = (bf16[1024,768]{1,0:T(8,128)(2,1)}, bf16[1024,768]{1,0:T(8,128)(2,1)S(1)}, u32[]{:S(2)}, u32[]{:S(2)}) collective-permute-start(bf16[1024,768]{1,0:T(8,128)(2,1)} %refs_0_.5), channel_id=1, source_target_pairs={{0,32},{32,64},{64,96},{96,0},{1,97},{33,1},{65,33},{97,65},{2,34}... | collective-permute-start | bytes 4718600 | tf_op jit(solution)/shard_map/ppermute | solution.py:192
  2.3 1.0 pad_select_fusion.refs_3_.refs_2_
  3.3 1.1 collective-permute-start.4
  4.4 18.1 %collective-permute-done.refs_1_ = bf16[1024,768]{1,0:T(8,128)(2,1)S(1)} collective-permute-done((bf16[1024,768]{1,0:T(8,128)(2,1)}, bf16[1024,768]{1,0:T(8,128)(2,1)S(1)}, u32[]{:S(2)}, u32[]{:S(2)}) %collective-permute-start) | collective-permute-done | bytes 1572896 | tf_op jit(solution)/shard_map/ppermute | solution.py:192
  22.5 0.0 collective-permute-start.1
  22.5 0.0 collective-permute-done.4
  22.6 0.8 pad_maximum_fusion
  23.3 1.9 %collective-permute-start.5 = (bf16[256,768]{1,0:T(8,128)(2,1)}, bf16[256,768]{1,0:T(8,128)(2,1)}, u32[]{:S(2)}, u32[]{:S(2)}) collective-permute-start(bf16[256,768]{1,0:T(8,128)(2,1)} %pad_maximum_fusion), channel_id=1, source_target_pairs={{0,4},{4,8},{8,12},{12,16},{16,20},{20,24},{24,28},{28,0},{1,29},{... | collective-permute-start | bytes 1179656 | tf_op jit(solution)/shard_map/ppermute | solution.py:192
  25.3 2.8 %collective-permute-start.8 = (bf16[128,768]{1,0:T(8,128)(2,1)S(1)}, bf16[128,768]{1,0:T(8,128)(2,1)S(1)}, u32[]{:S(2)}, u32[]{:S(2)}) collective-permute-start(bf16[128,768]{1,0:T(8,128)(2,1)S(1)} %pad_select_fusion.refs_3_.refs_2_), channel_id=1, source_target_pairs={{0,130},{130,0},{2,128},{128,2},{1,131},{131,1},{3,129},{129,3},{4... | collective-permute-start | bytes 589832 | tf_op jit(solution)/shard_map/ppermute | solution.py:186
  28.0 0.9 constant_dynamic-slice_fusion
  28.9 0.4 collective-permute-start.2
  29.3 4.1 %collective-permute-done.8.refs_4_.refs_3_ = bf16[128,768]{1,0:T(8,128)(2,1)S(1)} collective-permute-done((bf16[128,768]{1,0:T(8,128)(2,1)S(1)}, bf16[128,768]{1,0:T(8,128)(2,1)S(1)}, u32[]{:S(2)}, u32[]{:S(2)}) %collective-permute-start.8) | collective-permute-done | bytes 196640 | tf_op jit(solution)/shard_map/ppermute | solution.py:186
  33.4 0.0 collective-permute-start.9
  33.4 0.0 collective-permute-done.5.refs_5_.refs_4_
  33.4 0.7 collective-permute-start.6
  34.1 0.8 collective-permute-done.9
  34.9 2.4 %collective-permute-start.10 = (bf16[256,768]{1,0:T(8,128)(2,1)S(1)}, bf16[256,768]{1,0:T(8,128)(2,1)}, u32[]{:S(2)}, u32[]{:S(2)}) collective-permute-start(bf16[256,768]{1,0:T(8,128)(2,1)S(1)} %pad_maximum_fusion.1), channel_id=1, source_target_pairs={{0,4},{4,8},{8,12},{12,16},{16,20},{20,24},{24,28},{28,0},{1,29},{... | collective-permute-start | bytes 1179656 | tf_op jit(solution)/shard_map/ppermute | solution.py:192
  37.3 4.4 %collective-permute-done.6.refs_3_.refs_6_ = bf16[256,768]{1,0:T(8,128)(2,1)} collective-permute-done((bf16[256,768]{1,0:T(8,128)(2,1)}, bf16[256,768]{1,0:T(8,128)(2,1)}, u32[]{:S(2)}, u32[]{:S(2)}) %collective-permute-start.6) | collective-permute-done | bytes 393248 | tf_op jit(solution)/shard_map/ppermute | solution.py:192
  41.7 1.1 collective-permute-start.7
  42.8 3.1 %collective-permute-done.10.refs_6_.refs_5_ = bf16[256,768]{1,0:T(8,128)(2,1)} collective-permute-done((bf16[256,768]{1,0:T(8,128)(2,1)S(1)}, bf16[256,768]{1,0:T(8,128)(2,1)}, u32[]{:S(2)}, u32[]{:S(2)}) %collective-permute-start.10) | collective-permute-done | bytes 393248 | tf_op jit(solution)/shard_map/ppermute | solution.py:192
  45.9 1.0 collective-permute-start.11
  46.9 0.0 collective-permute-done.2.refs_0_.refs_3_
  46.9 0.2 collective-permute-start.3
  47.1 0.1 pad_add_fusion.place
  47.2 3.8 %collective-permute-done.7.refs_5_ = bf16[256,768]{1,0:T(8,128)(2,1)} collective-permute-done((bf16[256,768]{1,0:T(8,128)(2,1)}, bf16[256,768]{1,0:T(8,128)(2,1)}, u32[]{:S(2)}, u32[]{:S(2)}) %collective-permute-start.7) | collective-permute-done | bytes 393248 | tf_op jit(solution)/shard_map/ppermute | solution.py:192
  51.0 0.9 slice.4
  52.0 0.3 collective-permute-start.13
  52.2 0.0 copy-done
  52.3 0.4 multiply_reduce_fusion
  52.6 2.6 %collective-permute-done.11.refs_4_.refs_7_ = bf16[256,768]{1,0:T(8,128)(2,1)} collective-permute-done((bf16[256,768]{1,0:T(8,128)(2,1)}, bf16[256,768]{1,0:T(8,128)(2,1)}, u32[]{:S(2)}, u32[]{:S(2)}) %collective-permute-start.11) | collective-permute-done | bytes 393248 | tf_op jit(solution)/shard_map/ppermute | solution.py:192
  55.3 0.8 collective-permute-start.12
  56.0 2.9 %collective-permute-done.13.refs_7_ = bf16[128,768]{1,0:T(8,128)(2,1)S(1)} collective-permute-done((bf16[128,768]{1,0:T(8,128)(2,1)S(1)}, bf16[128,768]{1,0:T(8,128)(2,1)S(1)}, u32[]{:S(2)}, u32[]{:S(2)}) %collective-permute-start.13) | collective-permute-done | bytes 196640 | tf_op jit(solution)/shard_map/ppermute | solution.py:192
  58.9 2.8 %collective-permute-start.14 = (bf16[128,768]{1,0:T(8,128)(2,1)S(1)}, bf16[128,768]{1,0:T(8,128)(2,1)S(1)}, u32[]{:S(2)}, u32[]{:S(2)}) collective-permute-start(bf16[128,768]{1,0:T(8,128)(2,1)S(1)} %collective-permute-done.13.refs_7_), channel_id=1, source_target_pairs={{0,130},{130,0},{2,128},{128,2},{1,131},{131,1},{3,129},{129,3},{4... | collective-permute-start | bytes 589832 | tf_op jit(solution)/shard_map/ppermute | solution.py:186
  61.7 0.0 collective-permute-done.1.refs_2_
  61.7 8.4 %shard_map.50.refs_9_ = f32[2,24,128]{2,1,0:T(8,128)S(1)} custom-call(bf16[1024,768]{1,0:T(8,128)(2,1)S(1)} %copy-done, bf16[1024,768]{1,0:T(8,128)(2,1)S(1)} %collective-permute-done.refs_1_, bf16[1024,768]{1,0:T(8,128)(2,1)} %collective-permute-done.1.refs_2_, bf16[128,768]{1,0:T(8,128)(2,1)S(1)} %pad_select_fusion.refs_3_.refs_2_, ...), custom_call_target="tpu_custom_call" | custom-call | flops 3623878656 | bytes 5898240 | tf_op jit(solution)/shard_map/pallas_call | solution.py:147
  70.2 6.7 %shard_map.51.refs_10_ = f32[2,24,128]{2,1,0:T(8,128)S(1)} custom-call(bf16[1024,768]{1,0:T(8,128)(2,1)S(1)} %copy-done, bf16[1024,768]{1,0:T(8,128)(2,1)S(1)} %collective-permute-done.refs_1_, bf16[1024,768]{1,0:T(8,128)(2,1)} %collective-permute-done.1.refs_2_, bf16[256,768]{1,0:T(8,128)(2,1)} %collective-permute-done.6.refs_3_.refs_6_, ...), custom_call_target="tpu_custom_call" | custom-call | flops 2415919104 | bytes 5505024 | tf_op jit(solution)/shard_map/pallas_call | solution.py:147
  76.8 0.0 collective-permute-done.3.refs_1_.refs_4_
  76.8 5.7 %shard_map.52.refs_11_ = f32[2,8,128]{2,1,0:T(8,128)S(1)} custom-call(bf16[512,768]{1,0:T(8,128)(2,1)} %collective-permute-done.2.refs_0_.refs_3_, bf16[512,768]{1,0:T(8,128)(2,1)S(1)} %collective-permute-done.3.refs_1_.refs_4_, bf16[128,768]{1,0:T(8,128)(2,1)S(1)} %pad_select_fusion.refs_3_.refs_2_, ...), custom_call_target="tpu_custom_call" | custom-call | flops 2013265920 | bytes 3538944 | tf_op jit(solution)/shard_map/pallas_call | solution.py:147
  82.5 0.0 collective-permute-done.12.refs_6_
  82.5 0.0 collective-permute-done.14.refs_8_
  82.5 11.3 %shard_map.53 = f32[16,2,8,128]{3,2,1,0:T(8,128)} custom-call(s32[2]{0:T(128)S(1)} %pad_add_fusion.place, bf16[1024,768]{1,0:T(8,128)(2,1)S(1)} %copy-done, bf16[1024,768]{1,0:T(8,128)(2,1)S(1)} %collective-permute-done.refs_1_, bf16[1024,768]{1,0:T(8,128)(2,1)} %collective-permute-done.1.refs_2_, bf16[512,768]{1,0:T(8,128)(2,1)} %collective-permute-done.2.refs_0_.refs_3_, ...), custom_call_target="tpu_custom_call" | custom-call | flops 4831838208 | bytes 7471104 | tf_op jit(solution)/shard_map/pallas_call | solution.py:149
  93.8 3.5 %all-to-all-start = ((f32[16,2,8,128]{3,2,1,0:T(8,128)}), f32[16,2,8,128]{3,2,1,0:T(8,128)S(1)}, u32[]{:S(2)}, u32[]{:S(2)}) async-start(f32[16,2,8,128]{3,2,1,0:T(8,128)} %shard_map.53), calls=%async_computation | async-start | bytes 262144 | tf_op jit(solution)/shard_map/all_to_all | solution.py:229
  97.3 0.6 multiply_bitcast_fusion.norms
  97.9 6.1 %all-to-all-done.got = f32[16,2,8,128]{3,2,1,0:T(8,128)S(1)} async-done(((f32[16,2,8,128]{3,2,1,0:T(8,128)}), f32[16,2,8,128]{3,2,1,0:T(8,128)S(1)}, u32[]{:S(2)}, u32[]{:S(2)}) %all-to-all-start) | async-done | bytes 131104 | tf_op jit(solution)/shard_map/all_to_all | solution.py:229
  104.0 0.7 copy-done.1
  104.7 1.8 %shard_map.54 = (f32[8,128]{1,0:T(8,128)}, f32[64,128]{1,0:T(8,128)}) custom-call(f32[16,2,8,128]{3,2,1,0:T(8,128)} %copy-done.1, f32[8,128]{1,0:T(8,128)} %multiply_bitcast_fusion.norms), custom_call_target="tpu_custom_call" | custom-call | tf_op jit(solution)/shard_map/pallas_call | solution.py:233
  106.4 21.6 %all_to_all.16 = f32[64,1,128]{2,1,0:T(1,128)} all-to-all(f32[64,1,128]{2,1,0:T(1,128)} %bitcast.11), channel_id=1, replica_groups=mesh['xh'=2,'y'=4,'z'=8,'xl'=2,'core'=2] {'xh','y','z'}, dimensions={0} | all-to-all | bytes 65536 | tf_op jit(solution)/shard_map/all_to_all | solution.py:239
  128.0 1.6 %shard_map.55 = f32[8,128]{1,0:T(8,128)} custom-call(f32[8,128]{1,0:T(8,128)} %get-tuple-element.4.ratio, f32[64,128]{1,0:T(8,128)} %bitcast.10), custom_call_target="tpu_custom_call" | custom-call | tf_op jit(solution)/shard_map/pallas_call | solution.py:240
  (4 shorter events, 0.0 us)
Async XLA Ops:
  0.6 21.9 %collective-permute-start = (bf16[1024,768]{1,0:T(8,128)(2,1)}, bf16[1024,768]{1,0:T(8,128)(2,1)S(1)}, u32[]{:S(2)}, u32[]{:S(2)}) collective-permute-start(bf16[1024,768]{1,0:T(8,128)(2,1)} %refs_0_.5), channel_id=1, source_target_pairs={{0,32},{32,64},{64,96},{96,0},{1,97},{33,1},{65,33},{97,65},{2,34}... | collective-permute-start | bytes 4718600 | tf_op jit(solution)/shard_map/ppermute | solution.py:192
  3.3 19.2 %collective-permute-start.4 = (bf16[128,768]{1,0:T(8,128)(2,1)S(1)}, bf16[128,768]{1,0:T(8,128)(2,1)S(1)}, u32[]{:S(2)}, u32[]{:S(2)}) collective-permute-start(bf16[128,768]{1,0:T(8,128)(2,1)S(1)} %pad_select_fusion.refs_3_.refs_2_), channel_id=1, source_target_pairs={{0,1},{1,0},{2,3},{3,2},{4,5},{5,4},{6,7},{7,6},{8,9},{9,8},{10,11... | collective-permute-start | bytes 589832 | tf_op jit(solution)/shard_map/ppermute | solution.py:182
  22.5 39.2 %collective-permute-start.1 = (bf16[1024,768]{1,0:T(8,128)(2,1)S(1)}, bf16[1024,768]{1,0:T(8,128)(2,1)}, u32[]{:S(2)}, u32[]{:S(2)}) collective-permute-start(bf16[1024,768]{1,0:T(8,128)(2,1)S(1)} %collective-permute-done.refs_1_), channel_id=1, source_target_pairs={{0,1},{1,0},{2,3},{3,2},{4,5},{5,4},{6,7},{7,6},{8,9},{9,8},{10,11... | collective-permute-start | bytes 4718600 | tf_op jit(solution)/shard_map/ppermute | solution.py:182
  23.3 28.9 %copy-start = (bf16[1024,768]{1,0:T(8,128)(2,1)S(1)}, bf16[1024,768]{1,0:T(8,128)(2,1)}, u32[]{:S(2)}) copy-start(bf16[1024,768]{1,0:T(8,128)(2,1)} %refs_0_.5) | copy-start | bytes 4718596
  23.3 10.1 %collective-permute-start.5 = (bf16[256,768]{1,0:T(8,128)(2,1)}, bf16[256,768]{1,0:T(8,128)(2,1)}, u32[]{:S(2)}, u32[]{:S(2)}) collective-permute-start(bf16[256,768]{1,0:T(8,128)(2,1)} %pad_maximum_fusion), channel_id=1, source_target_pairs={{0,4},{4,8},{8,12},{12,16},{16,20},{20,24},{24,28},{28,0},{1,29},{... | collective-permute-start | bytes 1179656 | tf_op jit(solution)/shard_map/ppermute | solution.py:192
  25.3 8.1 %collective-permute-start.8 = (bf16[128,768]{1,0:T(8,128)(2,1)S(1)}, bf16[128,768]{1,0:T(8,128)(2,1)S(1)}, u32[]{:S(2)}, u32[]{:S(2)}) collective-permute-start(bf16[128,768]{1,0:T(8,128)(2,1)S(1)} %pad_select_fusion.refs_3_.refs_2_), channel_id=1, source_target_pairs={{0,130},{130,0},{2,128},{128,2},{1,131},{131,1},{3,129},{129,3},{4... | collective-permute-start | bytes 589832 | tf_op jit(solution)/shard_map/ppermute | solution.py:186
  28.9 18.0 %collective-permute-start.2 = (bf16[512,768]{1,0:T(8,128)(2,1)}, bf16[512,768]{1,0:T(8,128)(2,1)}, u32[]{:S(2)}, u32[]{:S(2)}) collective-permute-start(bf16[512,768]{1,0:T(8,128)(2,1)} %constant_dynamic-slice_fusion), channel_id=1, source_target_pairs={{0,32},{32,64},{64,96},{96,0},{1,97},{33,1},{65,33},{97,65},{2,34}... | collective-permute-start | bytes 2359304 | tf_op jit(solution)/shard_map/ppermute | solution.py:192
  33.4 1.4 %collective-permute-start.9 = (bf16[128,768]{1,0:T(8,128)(2,1)S(1)}, bf16[128,768]{1,0:T(8,128)(2,1)S(1)}, u32[]{:S(2)}, u32[]{:S(2)}) collective-permute-start(bf16[128,768]{1,0:T(8,128)(2,1)S(1)} %collective-permute-done.8.refs_4_.refs_3_), channel_id=1, source_target_pairs={{0,1},{1,0},{2,3},{3,2},{4,5},{5,4},{6,7},{7,6},{8,9},{9,8},{10,11... | collective-permute-start | bytes 589832 | tf_op jit(solution)/shard_map/ppermute | solution.py:182
  33.4 8.3 %collective-permute-start.6 = (bf16[256,768]{1,0:T(8,128)(2,1)}, bf16[256,768]{1,0:T(8,128)(2,1)}, u32[]{:S(2)}, u32[]{:S(2)}) collective-permute-start(bf16[256,768]{1,0:T(8,128)(2,1)} %collective-permute-done.5.refs_5_.refs_4_), channel_id=1, source_target_pairs={{0,4},{4,8},{8,12},{12,16},{16,20},{20,24},{24,28},{28,0},{1,29},{... | collective-permute-start | bytes 1179656 | tf_op jit(solution)/shard_map/ppermute | solution.py:192
  34.9 11.1 %collective-permute-start.10 = (bf16[256,768]{1,0:T(8,128)(2,1)S(1)}, bf16[256,768]{1,0:T(8,128)(2,1)}, u32[]{:S(2)}, u32[]{:S(2)}) collective-permute-start(bf16[256,768]{1,0:T(8,128)(2,1)S(1)} %pad_maximum_fusion.1), channel_id=1, source_target_pairs={{0,4},{4,8},{8,12},{12,16},{16,20},{20,24},{24,28},{28,0},{1,29},{... | collective-permute-start | bytes 1179656 | tf_op jit(solution)/shard_map/ppermute | solution.py:192
  41.7 9.3 %collective-permute-start.7 = (bf16[256,768]{1,0:T(8,128)(2,1)}, bf16[256,768]{1,0:T(8,128)(2,1)}, u32[]{:S(2)}, u32[]{:S(2)}) collective-permute-start(bf16[256,768]{1,0:T(8,128)(2,1)} %collective-permute-done.6.refs_3_.refs_6_), channel_id=1, source_target_pairs={{0,4},{4,8},{8,12},{12,16},{16,20},{20,24},{24,28},{28,0},{1,29},{... | collective-permute-start | bytes 1179656 | tf_op jit(solution)/shard_map/ppermute | solution.py:192
  45.9 9.3 %collective-permute-start.11 = (bf16[256,768]{1,0:T(8,128)(2,1)}, bf16[256,768]{1,0:T(8,128)(2,1)}, u32[]{:S(2)}, u32[]{:S(2)}) collective-permute-start(bf16[256,768]{1,0:T(8,128)(2,1)} %collective-permute-done.10.refs_6_.refs_5_), channel_id=1, source_target_pairs={{0,4},{4,8},{8,12},{12,16},{16,20},{20,24},{24,28},{28,0},{1,29},{... | collective-permute-start | bytes 1179656 | tf_op jit(solution)/shard_map/ppermute | solution.py:192
  46.9 29.9 %collective-permute-start.3 = (bf16[512,768]{1,0:T(8,128)(2,1)}, bf16[512,768]{1,0:T(8,128)(2,1)S(1)}, u32[]{:S(2)}, u32[]{:S(2)}) collective-permute-start(bf16[512,768]{1,0:T(8,128)(2,1)} %collective-permute-done.2.refs_0_.refs_3_), channel_id=1, source_target_pairs={{0,1},{1,0},{2,3},{3,2},{4,5},{5,4},{6,7},{7,6},{8,9},{9,8},{10,11... | collective-permute-start | bytes 2359304 | tf_op jit(solution)/shard_map/ppermute | solution.py:182
  52.0 7.0 %collective-permute-start.13 = (bf16[128,768]{1,0:T(8,128)(2,1)S(1)}, bf16[128,768]{1,0:T(8,128)(2,1)S(1)}, u32[]{:S(2)}, u32[]{:S(2)}) collective-permute-start(bf16[128,768]{1,0:T(8,128)(2,1)S(1)} %slice.4), channel_id=1, source_target_pairs={{0,4},{4,8},{8,12},{12,16},{16,20},{20,24},{24,28},{28,0},{1,29},{... | collective-permute-start | bytes 589832 | tf_op jit(solution)/shard_map/ppermute | solution.py:192
  55.3 27.2 %collective-permute-start.12 = (bf16[256,768]{1,0:T(8,128)(2,1)}, bf16[256,768]{1,0:T(8,128)(2,1)S(1)}, u32[]{:S(2)}, u32[]{:S(2)}) collective-permute-start(bf16[256,768]{1,0:T(8,128)(2,1)} %collective-permute-done.11.refs_4_.refs_7_), channel_id=1, source_target_pairs={{0,4},{4,8},{8,12},{12,16},{16,20},{20,24},{24,28},{28,0},{1,29},{... | collective-permute-start | bytes 1179656 | tf_op jit(solution)/shard_map/ppermute | solution.py:192
  58.9 23.6 %collective-permute-start.14 = (bf16[128,768]{1,0:T(8,128)(2,1)S(1)}, bf16[128,768]{1,0:T(8,128)(2,1)S(1)}, u32[]{:S(2)}, u32[]{:S(2)}) collective-permute-start(bf16[128,768]{1,0:T(8,128)(2,1)S(1)} %collective-permute-done.13.refs_7_), channel_id=1, source_target_pairs={{0,130},{130,0},{2,128},{128,2},{1,131},{131,1},{3,129},{129,3},{4... | collective-permute-start | bytes 589832 | tf_op jit(solution)/shard_map/ppermute | solution.py:186
  93.8 10.2 %all-to-all-start = ((f32[16,2,8,128]{3,2,1,0:T(8,128)}), f32[16,2,8,128]{3,2,1,0:T(8,128)S(1)}, u32[]{:S(2)}, u32[]{:S(2)}) async-start(f32[16,2,8,128]{3,2,1,0:T(8,128)} %shard_map.53), calls=%async_computation | async-start | bytes 262144 | tf_op jit(solution)/shard_map/all_to_all | solution.py:229
  104.0 0.7 copy-start.1

commit v2 on v1

--- a/solution.py
+++ b/solution.py
@@ -17,19 +17,29 @@
 VMEM = pl.BlockSpec(memory_space=pltpu.VMEM)
 
 
-def lse_tiles(pools, samples, each, scale, out_ref, joined, half_norm, pool_all, bufs, tops):
+def lse_tiles(pools, samples, each, scale, out_ref, joined, half_norm, pool_all, bufs, tops, sems):
     rows = joined.shape[0]
     member = rows // 2
-    i = 0
+    sample_copies, pool_copies = [], []
     for ref in samples:
         for unit in range(0, ref.shape[0], 2 * each):
-            joined[i * each : (i + 1) * each, :] = ref[unit : unit + each, :]
-            joined[member + i * each : member + (i + 1) * each, :] = ref[unit + each : unit + 2 * each, :]
-            i += 1
+            n = len(sample_copies)
+            at = n // 2 * each
+            for m in range(2):
+                sample_copies.append(
+                    pltpu.make_async_copy(
+                        ref.at[pl.ds(unit + m * each, each), :], joined.at[pl.ds(at + m * member, each), :], sems.at[n + m]
+                    )
+                )
     count = 0
     for ref in pools:
-        pool_all[count : count + ref.shape[0], :] = ref[...]
+        sem = sems.at[len(sample_copies) + len(pool_copies)]
+        pool_copies.append(pltpu.make_async_copy(ref, pool_all.at[pl.ds(count, ref.shape[0]), :], sem))
         count += ref.shape[0]
+    for copy in sample_copies + pool_copies:
+        copy.start()
+    for copy in sample_copies:
+        copy.wait()
 
     def norms(i, _):
         at = pl.ds(pl.multiple_of(i * 128, 128), 128)
@@ -37,7 +47,8 @@
         half_norm[at, :] = jnp.broadcast_to(jnp.sum(wide * wide, axis=1, keepdims=True) * 0.5, (128, 128))
         return 0
 
-    lax.fori_loop(0, rows // 128, norms, 0)
+    lax.fori_loop(0, rows // 128, norms, 0, unroll=True)
+    pool_copies[0].wait()
     tiles = count // TILE
     chunk = member // -(-member // CHUNK)
 
@@ -72,6 +83,8 @@
                     out_ref[m, pl.ds(done * (TILE // 128) + k, 1), :] = value[:, k * 128 : (k + 1) * 128]
 
     step(0, bufs[0], tops[0], None, None, None)
+    for copy in pool_copies[1:]:
+        copy.wait()
 
     def pair(i, _):
         step(2 * i + 1, bufs[1], tops[1], 2 * i, bufs[0], tops[0])
@@ -85,8 +98,8 @@
 
 def partial_kernel(n_pools, n_samples, each, scale, *refs):
     pools, samples, out_ref = refs[:n_pools], refs[n_pools : n_pools + n_samples], refs[n_pools + n_samples]
-    joined, half_norm, pool_all, buf0, buf1, top0, top1 = refs[n_pools + n_samples + 1 :]
-    lse_tiles(pools, samples, each, scale, out_ref, joined, half_norm, pool_all, (buf0, buf1), (top0, top1))
+    joined, half_norm, pool_all, buf0, buf1, top0, top1, sems = refs[n_pools + n_samples + 1 :]
+    lse_tiles(pools, samples, each, scale, out_ref, joined, half_norm, pool_all, (buf0, buf1), (top0, top1), sems)
 
 
 def add_exp(a, b):
@@ -96,12 +109,14 @@
 
 def last_kernel(n_pools, n_samples, each, scale, place, *refs):
     pools, samples = refs[:n_pools], refs[n_pools : n_pools + n_samples]
-    first, second, third, out_ref, last = refs[n_pools + n_samples : n_pools + n_samples + 5]
-    joined, half_norm, pool_all, buf0, buf1, top0, top1 = refs[n_pools + n_samples + 5 :]
-    lse_tiles(pools, samples, each, scale, last, joined, half_norm, pool_all, (buf0, buf1), (top0, top1))
+    alone, first, second, third, out_ref, last = refs[n_pools + n_samples : n_pools + n_samples + 6]
+    joined, half_norm, pool_all, buf0, buf1, top0, top1, sems = refs[n_pools + n_samples + 6 :]
+    lse_tiles(pools, samples, each, scale, last, joined, half_norm, pool_all, (buf0, buf1), (top0, top1), sems)
     y, core = place[0], place[1]
-    n = first.shape[1] // 3
-    near = add_exp(add_exp(first[...], second[...]), last[:, : 3 * n, :])
+    n = alone.shape[1]
+    rest = add_exp(second[...], last[:, : 3 * n, :])
+    own = add_exp(alone[...], rest[:, :n, :])
+    near = add_exp(first[...], rest[:, n:, :])
     far = add_exp(third[...], last[:, 3 * n :, :])
 
     def put(owner, value, swapped):
@@ -114,9 +129,9 @@
             else:
                 out_ref[at, :, :, :] = value
 
-    put(y, near[:, :n, :], False)
-    put(y + 3 - 2 * core, near[:, n : 2 * n, :], False)
-    put(y + 1 + 2 * core, near[:, 2 * n :, :], False)
+    put(y, own, False)
+    put(y + 3 - 2 * core, near[:, :n, :], False)
+    put(y + 1 + 2 * core, near[:, n:, :], False)
     put(y + 2, far, True)
 
 
@@ -132,6 +147,7 @@
         pltpu.VMEM((rows, TILE), jnp.float32),
         pltpu.VMEM((16, TILE), jnp.float32),
         pltpu.VMEM((16, TILE), jnp.float32),
+        pltpu.SemaphoreType.DMA((rows // each + len(pools),)),
     ]
     partial = jax.ShapeDtypeStruct((2, count // 128, 128), jnp.float32)
     common = dict(
@@ -141,7 +157,7 @@
             flops=2 * rows * count * depth, bytes_accessed=2 * (rows + count) * depth, transcendentals=rows * count
         ),
     )
-    inputs = [VMEM] * (len(pools) + len(samples))
+    inputs = [pl.BlockSpec(memory_space=pl.ANY)] * (len(pools) + len(samples))
     if earlier is None:
         kernel = functools.partial(partial_kernel, len(pools), len(samples), each, scale)
         return pl.pallas_call(kernel, out_shape=partial, in_specs=inputs, scratch_shapes=scratch, **common)(*pools, *samples)
@@ -217,14 +233,15 @@
     zx3 = both_ways(zx2, "z")
     z4 = both_ways(z3[: 2 * each], "z")
     across = both_ways(lax.dynamic_slice_in_dim(beside, core * half, half, 0), "y")
-    near = [pool_embeds, beside, swap_core(beside)]
+    near = [beside, swap_core(beside)]
     far = [across, swap_core(across)]
-    earliest, early = [own, other, z1, zx1], [z2, zx2]
+    earliest, early = [own, other, z1], [zx1, z2, zx2]
     late = [z3, zx3, z4, swap_x(z4)]
+    alone = lse_call([pool_embeds], earliest, each, scale)
     first = lse_call(near, earliest, each, scale)
-    second = lse_call(near, early, each, scale)
+    second = lse_call([pool_embeds] + near, early, each, scale)
     third = lse_call(far, earliest + early, each, scale)
-    send = lse_call(near + far, late, each, scale, (first, second, third), place)
+    send = lse_call([pool_embeds] + near + far, late, each, scale, (alone, first, second, third), place)
 
     got = lax.all_to_all(send, ROW_GROUP, 0, 0)
     pool_norms = jnp.sum(jnp.square(pool_embeds.astype(jnp.float32)), axis=1) * (KERNEL_GAIN / depth)

time: 131 us -> 125 us (0.954)
  waiting for transfers between devices: 46 us -> 32.5 us
  starting transfers between devices: 20.4 us -> 26.8 us
  Pallas kernels: 35.4 us -> 36.8 us
    ppermute x9, waiting for transfers between devices: 35.1 us -> 20.6 us  [both_ways(): return lax.ppermute(value, (axis, 'core'), pairs)]
    ppermute x9, starting transfers between devices: 10.1 us -> 15.8 us  [both_ways(): return lax.ppermute(value, (axis, 'core'), pairs)]
    ppermute x4, waiting for transfers between devices: 0.79 us -> 2.51 us  [swap_core(): return lax.ppermute(value, 'core', [(0, 1), (1, 0)])]
    pallas_call x3 -> x4, Pallas kernels: 20.8 us -> 21.5 us  [lse_call(): pl.pallas_call(kernel, out_shape=partial, in_specs=inputs, scratch_shapes...]
  transfers between devices with their start and end apart: 16 -> 16, of which waited for: 9 -> 7; matrix products, arithmetic and copies ran while one was open for 4% -> 3% of each run, Pallas kernels for 16% -> 17%
where the time goes in v2:
time: 125 us; the launch traced here: 123 us
  Pallas kernels  36.8 us (29%)
  waiting for transfers between devices  32.5 us (26%)
  starting transfers between devices  26.8 us (21%)
  blocking collectives  21.2 us (17%)
  other arithmetic  2.91 us (2%)
  local copies, waits for them, and re-layouts  2.15 us (2%)
    pallas_call x4, Pallas kernels, lse_call(): pl.pallas_call(kernel, out_shape=partial, in_specs=inputs, scratch_shapes...  21.5 us
    all_to_all x1, blocking collectives, body(): stats = lax.all_to_all(stats, BLK, 0, 0, tiled=True)  21.2 us
    ppermute x9, waiting for transfers between devices, both_ways(): return lax.ppermute(value, (axis, 'core'), pairs)  20.6 us
    ppermute x9, starting transfers between devices, both_ways(): return lax.ppermute(value, (axis, 'core'), pairs)  15.8 us
    pallas_call x1, Pallas kernels, lse_call(): pl.pallas_call(kernel, out_shape=jax.ShapeDtypeStruct((16, 2, pools[0].sh...  12 us
    all_to_all x1, waiting for transfers between devices, body(): got = lax.all_to_all(send, ROW_GROUP, 0, 0)  6.07 us
    ppermute x2, starting transfers between devices, swap_x(): return lax.ppermute(value, ('xh', 'xl'), [(0, 3), (3, 0), (1, 2), (2, 1)])  5.52 us
    all_to_all x1, starting transfers between devices, body(): got = lax.all_to_all(send, ROW_GROUP, 0, 0)  3.83 us
  transfers between devices with their start and end apart: 16, of which 7 were waited for; matrix products, arithmetic and copies ran while one was open for 3% of the time, Pallas kernels for 17%

profile of v2, /device:TPU:32, one launch (start us, length us, event | category | flops | bytes accessed | tf_op | source)
XLA Modules:
  0.0 123.2 jit_solution(2425055746024500100)
XLA Ops:
  0.6 1.7 %collective-permute-start = (bf16[1024,768]{1,0:T(8,128)(2,1)}, bf16[1024,768]{1,0:T(8,128)(2,1)S(1)}, u32[]{:S(2)}, u32[]{:S(2)}) collective-permute-start(bf16[1024,768]{1,0:T(8,128)(2,1)} %refs_0_.5), channel_id=1, source_target_pairs={{0,32},{32,64},{64,96},{96,0},{1,97},{33,1},{65,33},{97,65},{2,34}... | collective-permute-start | bytes 4718600 | tf_op jit(solution)/shard_map/ppermute | solution.py:208
  2.3 1.0 pad_select_fusion.refs_1_.refs_2_
  3.3 1.1 collective-permute-start.4
  4.4 1.1 collective-permute-done.4
  5.5 0.8 pad_maximum_fusion
  6.3 1.9 %collective-permute-start.5 = (bf16[256,768]{1,0:T(8,128)(2,1)}, bf16[256,768]{1,0:T(8,128)(2,1)}, u32[]{:S(2)}, u32[]{:S(2)}) collective-permute-start(bf16[256,768]{1,0:T(8,128)(2,1)} %pad_maximum_fusion), channel_id=1, source_target_pairs={{0,4},{4,8},{8,12},{12,16},{16,20},{20,24},{24,28},{28,0},{1,29},{... | collective-permute-start | bytes 1179656 | tf_op jit(solution)/shard_map/ppermute | solution.py:208
  8.2 14.3 %collective-permute-done.refs_0_.refs_1_ = bf16[1024,768]{1,0:T(8,128)(2,1)S(1)} collective-permute-done((bf16[1024,768]{1,0:T(8,128)(2,1)}, bf16[1024,768]{1,0:T(8,128)(2,1)S(1)}, u32[]{:S(2)}, u32[]{:S(2)}) %collective-permute-start) | collective-permute-done | bytes 1572896 | tf_op jit(solution)/shard_map/ppermute | solution.py:208
  22.5 0.0 collective-permute-start.1
  22.5 2.8 %collective-permute-start.8 = (bf16[128,768]{1,0:T(8,128)(2,1)S(1)}, bf16[128,768]{1,0:T(8,128)(2,1)S(1)}, u32[]{:S(2)}, u32[]{:S(2)}) collective-permute-start(bf16[128,768]{1,0:T(8,128)(2,1)S(1)} %pad_select_fusion.refs_1_.refs_2_), channel_id=1, source_target_pairs={{0,130},{130,0},{2,128},{128,2},{1,131},{131,1},{3,129},{129,3},{4... | collective-permute-start | bytes 589832 | tf_op jit(solution)/shard_map/ppermute | solution.py:202
  25.3 0.0 collective-permute-done.5.refs_3_.refs_4_
  25.3 1.9 %collective-permute-start.6 = (bf16[256,768]{1,0:T(8,128)(2,1)}, bf16[256,768]{1,0:T(8,128)(2,1)S(1)}, u32[]{:S(2)}, u32[]{:S(2)}) collective-permute-start(bf16[256,768]{1,0:T(8,128)(2,1)} %collective-permute-done.5.refs_3_.refs_4_), channel_id=1, source_target_pairs={{0,4},{4,8},{8,12},{12,16},{16,20},{20,24},{24,28},{28,0},{1,29},{... | collective-permute-start | bytes 1179656 | tf_op jit(solution)/shard_map/ppermute | solution.py:208
  27.2 0.1 constant_dynamic-slice_fusion
  27.3 0.4 collective-permute-start.2
  27.7 3.3 %collective-permute-done.8.refs_2_.refs_3_ = bf16[128,768]{1,0:T(8,128)(2,1)S(1)} collective-permute-done((bf16[128,768]{1,0:T(8,128)(2,1)S(1)}, bf16[128,768]{1,0:T(8,128)(2,1)S(1)}, u32[]{:S(2)}, u32[]{:S(2)}) %collective-permute-start.8) | collective-permute-done | bytes 196640 | tf_op jit(solution)/shard_map/ppermute | solution.py:202
  31.1 0.0 collective-permute-start.9
  31.1 1.4 %collective-permute-done.9 = bf16[128,768]{1,0:T(8,128)(2,1)S(1)} collective-permute-done((bf16[128,768]{1,0:T(8,128)(2,1)S(1)}, bf16[128,768]{1,0:T(8,128)(2,1)S(1)}, u32[]{:S(2)}, u32[]{:S(2)}) %collective-permute-start.9) | collective-permute-done | bytes 196640 | tf_op jit(solution)/shard_map/ppermute | solution.py:198
  32.5 2.0 %collective-permute-start.10 = (bf16[256,768]{1,0:T(8,128)(2,1)S(1)}, bf16[256,768]{1,0:T(8,128)(2,1)}, u32[]{:S(2)}, u32[]{:S(2)}) collective-permute-start(bf16[256,768]{1,0:T(8,128)(2,1)S(1)} %pad_maximum_fusion.1), channel_id=1, source_target_pairs={{0,4},{4,8},{8,12},{12,16},{16,20},{20,24},{24,28},{28,0},{1,29},{... | collective-permute-start | bytes 1179656 | tf_op jit(solution)/shard_map/ppermute | solution.py:208
  34.5 0.0 collective-permute-done.6.refs_4_.refs_6_
  34.5 1.9 %collective-permute-start.7 = (bf16[256,768]{1,0:T(8,128)(2,1)S(1)}, bf16[256,768]{1,0:T(8,128)(2,1)S(1)}, u32[]{:S(2)}, u32[]{:S(2)}) collective-permute-start(bf16[256,768]{1,0:T(8,128)(2,1)S(1)} %collective-permute-done.6.refs_4_.refs_6_), channel_id=1, source_target_pairs={{0,4},{4,8},{8,12},{12,16},{16,20},{20,24},{24,28},{28,0},{1,29},{... | collective-permute-start | bytes 1179656 | tf_op jit(solution)/shard_map/ppermute | solution.py:208
  36.5 4.0 %collective-permute-done.10.refs_3_.refs_5_ = bf16[256,768]{1,0:T(8,128)(2,1)} collective-permute-done((bf16[256,768]{1,0:T(8,128)(2,1)S(1)}, bf16[256,768]{1,0:T(8,128)(2,1)}, u32[]{:S(2)}, u32[]{:S(2)}) %collective-permute-start.10) | collective-permute-done | bytes 393248 | tf_op jit(solution)/shard_map/ppermute | solution.py:208
  40.5 1.9 %collective-permute-start.11 = (bf16[256,768]{1,0:T(8,128)(2,1)}, bf16[256,768]{1,0:T(8,128)(2,1)}, u32[]{:S(2)}, u32[]{:S(2)}) collective-permute-start(bf16[256,768]{1,0:T(8,128)(2,1)} %collective-permute-done.10.refs_3_.refs_5_), channel_id=1, source_target_pairs={{0,4},{4,8},{8,12},{12,16},{16,20},{20,24},{24,28},{28,0},{1,29},{... | collective-permute-start | bytes 1179656 | tf_op jit(solution)/shard_map/ppermute | solution.py:208
  42.4 2.2 %collective-permute-done.7.refs_5_ = bf16[256,768]{1,0:T(8,128)(2,1)S(1)} collective-permute-done((bf16[256,768]{1,0:T(8,128)(2,1)S(1)}, bf16[256,768]{1,0:T(8,128)(2,1)S(1)}, u32[]{:S(2)}, u32[]{:S(2)}) %collective-permute-start.7) | collective-permute-done | bytes 393248 | tf_op jit(solution)/shard_map/ppermute | solution.py:208
  44.6 0.7 slice.4
  45.3 0.8 copy-done.1
  46.1 1.9 %collective-permute-start.13 = (bf16[128,768]{1,0:T(8,128)(2,1)}, bf16[128,768]{1,0:T(8,128)(2,1)}, u32[]{:S(2)}, u32[]{:S(2)}) collective-permute-start(bf16[128,768]{1,0:T(8,128)(2,1)} %slice.4), channel_id=1, source_target_pairs={{0,4},{4,8},{8,12},{12,16},{16,20},{20,24},{24,28},{28,0},{1,29},{... | collective-permute-start | bytes 589832 | tf_op jit(solution)/shard_map/ppermute | solution.py:208
  48.0 0.0 collective-permute-done.2.refs_0_.refs_3_
  48.0 0.6 collective-permute-start.3
  48.6 0.4 multiply_reduce_fusion
  48.9 0.1 pad_add_fusion.place
  49.0 3.1 %shard_map.50.refs_9_ = f32[2,8,128]{2,1,0:T(8,128)S(1)} custom-call(bf16[1024,768]{1,0:T(8,128)(2,1)S(1)} %copy-done, bf16[128,768]{1,0:T(8,128)(2,1)S(1)} %pad_select_fusion.refs_1_.refs_2_, bf16[128,768]{1,0:T(8,128)(2,1)S(1)} %collective-permute-done.8.refs_2_.refs_3_, bf16[256,768]{1,0:T(8,128)(2,1)} %collective-permute-done.5.refs_3_.refs_4_), custom_call_target="tpu_custom_call" | custom-call | flops 805306368 | bytes 2359296 | tf_op jit(solution)/shard_map/pallas_call | solution.py:163
  52.1 0.0 collective-permute-done.11.refs_5_.refs_7_
  52.1 2.1 %collective-permute-start.12 = (bf16[256,768]{1,0:T(8,128)(2,1)}, bf16[256,768]{1,0:T(8,128)(2,1)S(1)}, u32[]{:S(2)}, u32[]{:S(2)}) collective-permute-start(bf16[256,768]{1,0:T(8,128)(2,1)} %collective-permute-done.11.refs_5_.refs_7_), channel_id=1, source_target_pairs={{0,4},{4,8},{8,12},{12,16},{16,20},{20,24},{24,28},{28,0},{1,29},{... | collective-permute-start | bytes 1179656 | tf_op jit(solution)/shard_map/ppermute | solution.py:208
  54.2 0.0 collective-permute-done.13.refs_7_
  54.2 2.8 %collective-permute-start.14 = (bf16[128,768]{1,0:T(8,128)(2,1)}, bf16[128,768]{1,0:T(8,128)(2,1)S(1)}, u32[]{:S(2)}, u32[]{:S(2)}) collective-permute-start(bf16[128,768]{1,0:T(8,128)(2,1)} %collective-permute-done.13.refs_7_), channel_id=1, source_target_pairs={{0,130},{130,0},{2,128},{128,2},{1,131},{131,1},{3,129},{129,3},{4... | collective-permute-start | bytes 589832 | tf_op jit(solution)/shard_map/ppermute | solution.py:202
  57.0 0.0 collective-permute-done.1.refs_1_.refs_2_
  57.0 7.9 %shard_map.52.refs_11_ = f32[2,24,128]{2,1,0:T(8,128)S(1)} custom-call(bf16[1024,768]{1,0:T(8,128)(2,1)S(1)} %copy-done, bf16[1024,768]{1,0:T(8,128)(2,1)S(1)} %collective-permute-done.refs_0_.refs_1_, bf16[1024,768]{1,0:T(8,128)(2,1)} %collective-permute-done.1.refs_1_.refs_2_, bf16[256,768]{1,0:T(8,128)(2,1)} %collective-permute-done.10.refs_3_.refs_5_, ...), custom_call_target="tpu_custom_call" | custom-call | flops 3623878656 | bytes 5898240 | tf_op jit(solution)/shard_map/pallas_call | solution.py:163
  64.9 4.8 %shard_map.51.refs_10_ = f32[2,16,128]{2,1,0:T(8,128)S(1)} custom-call(bf16[1024,768]{1,0:T(8,128)(2,1)S(1)} %collective-permute-done.refs_0_.refs_1_, bf16[1024,768]{1,0:T(8,128)(2,1)} %collective-permute-done.1.refs_1_.refs_2_, bf16[128,768]{1,0:T(8,128)(2,1)S(1)} %pad_select_fusion.refs_1_.refs_2_, ...), custom_call_target="tpu_custom_call" | custom-call | flops 1610612736 | bytes 3932160 | tf_op jit(solution)/shard_map/pallas_call | solution.py:163
  69.8 0.0 collective-permute-done.3.refs_1_.refs_4_
  69.8 5.6 %shard_map.53.refs_12_ = f32[2,8,128]{2,1,0:T(8,128)S(1)} custom-call(bf16[512,768]{1,0:T(8,128)(2,1)} %collective-permute-done.2.refs_0_.refs_3_, bf16[512,768]{1,0:T(8,128)(2,1)} %collective-permute-done.3.refs_1_.refs_4_, bf16[128,768]{1,0:T(8,128)(2,1)S(1)} %pad_select_fusion.refs_1_.refs_2_, ...), custom_call_target="tpu_custom_call" | custom-call | flops 2013265920 | bytes 3538944 | tf_op jit(solution)/shard_map/pallas_call | solution.py:163
  75.4 0.0 collective-permute-done.14.refs_8_
  75.4 12.0 %shard_map.54 = f32[16,2,8,128]{3,2,1,0:T(8,128)} custom-call(s32[2]{0:T(128)S(1)} %pad_add_fusion.place, bf16[1024,768]{1,0:T(8,128)(2,1)S(1)} %copy-done, bf16[1024,768]{1,0:T(8,128)(2,1)S(1)} %collective-permute-done.refs_0_.refs_1_, bf16[1024,768]{1,0:T(8,128)(2,1)} %collective-permute-done.1.refs_1_.refs_2_, ...), custom_call_target="tpu_custom_call" | custom-call | flops 4831838208 | bytes 7471104 | tf_op jit(solution)/shard_map/pallas_call | solution.py:165
  87.5 3.8 %all-to-all-start = ((f32[16,2,8,128]{3,2,1,0:T(8,128)}), f32[16,2,8,128]{3,2,1,0:T(8,128)S(1)}, u32[]{:S(2)}, u32[]{:S(2)}) async-start(f32[16,2,8,128]{3,2,1,0:T(8,128)} %shard_map.54), calls=%async_computation | async-start | bytes 262144 | tf_op jit(solution)/shard_map/all_to_all | solution.py:246
  91.3 0.6 multiply_bitcast_fusion.norms
  91.9 6.1 %all-to-all-done.got = f32[16,2,8,128]{3,2,1,0:T(8,128)S(1)} async-done(((f32[16,2,8,128]{3,2,1,0:T(8,128)}), f32[16,2,8,128]{3,2,1,0:T(8,128)S(1)}, u32[]{:S(2)}, u32[]{:S(2)}) %all-to-all-start) | async-done | bytes 131104 | tf_op jit(solution)/shard_map/all_to_all | solution.py:246
  98.0 0.6 copy-done.5
  98.6 1.8 %shard_map.55 = (f32[8,128]{1,0:T(8,128)}, f32[64,128]{1,0:T(8,128)}) custom-call(f32[16,2,8,128]{3,2,1,0:T(8,128)} %copy-done.5, f32[8,128]{1,0:T(8,128)} %multiply_bitcast_fusion.norms), custom_call_target="tpu_custom_call" | custom-call | tf_op jit(solution)/shard_map/pallas_call | solution.py:250
  100.4 21.2 %all_to_all.16 = f32[64,1,128]{2,1,0:T(1,128)} all-to-all(f32[64,1,128]{2,1,0:T(1,128)} %bitcast.11), channel_id=1, replica_groups=mesh['xh'=2,'y'=4,'z'=8,'xl'=2,'core'=2] {'xh','y','z'}, dimensions={0} | all-to-all | bytes 65536 | tf_op jit(solution)/shard_map/all_to_all | solution.py:256
  121.6 1.6 %shard_map.56 = f32[8,128]{1,0:T(8,128)} custom-call(f32[8,128]{1,0:T(8,128)} %get-tuple-element.4.ratio, f32[64,128]{1,0:T(8,128)} %bitcast.10), custom_call_target="tpu_custom_call" | custom-call | tf_op jit(solution)/shard_map/pallas_call | solution.py:257
  (13 shorter events, 0.1 us)
Async XLA Ops:
  0.6 21.9 %collective-permute-start = (bf16[1024,768]{1,0:T(8,128)(2,1)}, bf16[1024,768]{1,0:T(8,128)(2,1)S(1)}, u32[]{:S(2)}, u32[]{:S(2)}) collective-permute-start(bf16[1024,768]{1,0:T(8,128)(2,1)} %refs_0_.5), channel_id=1, source_target_pairs={{0,32},{32,64},{64,96},{96,0},{1,97},{33,1},{65,33},{97,65},{2,34}... | collective-permute-start | bytes 4718600 | tf_op jit(solution)/shard_map/ppermute | solution.py:208
  3.3 2.1 %collective-permute-start.4 = (bf16[128,768]{1,0:T(8,128)(2,1)S(1)}, bf16[128,768]{1,0:T(8,128)(2,1)S(1)}, u32[]{:S(2)}, u32[]{:S(2)}) collective-permute-start(bf16[128,768]{1,0:T(8,128)(2,1)S(1)} %pad_select_fusion.refs_1_.refs_2_), channel_id=1, source_target_pairs={{0,1},{1,0},{2,3},{3,2},{4,5},{5,4},{6,7},{7,6},{8,9},{9,8},{10,11... | collective-permute-start | bytes 589832 | tf_op jit(solution)/shard_map/ppermute | solution.py:198
  6.3 42.3 %copy-start = (bf16[1024,768]{1,0:T(8,128)(2,1)S(1)}, bf16[1024,768]{1,0:T(8,128)(2,1)}, u32[]{:S(2)}) copy-start(bf16[1024,768]{1,0:T(8,128)(2,1)} %refs_0_.5) | copy-start | bytes 4718596
  6.3 19.0 %collective-permute-start.5 = (bf16[256,768]{1,0:T(8,128)(2,1)}, bf16[256,768]{1,0:T(8,128)(2,1)}, u32[]{:S(2)}, u32[]{:S(2)}) collective-permute-start(bf16[256,768]{1,0:T(8,128)(2,1)} %pad_maximum_fusion), channel_id=1, source_target_pairs={{0,4},{4,8},{8,12},{12,16},{16,20},{20,24},{24,28},{28,0},{1,29},{... | collective-permute-start | bytes 1179656 | tf_op jit(solution)/shard_map/ppermute | solution.py:208
  22.5 34.4 %collective-permute-start.1 = (bf16[1024,768]{1,0:T(8,128)(2,1)S(1)}, bf16[1024,768]{1,0:T(8,128)(2,1)}, u32[]{:S(2)}, u32[]{:S(2)}) collective-permute-start(bf16[1024,768]{1,0:T(8,128)(2,1)S(1)} %collective-permute-done.refs_0_.refs_1_), channel_id=1, source_target_pairs={{0,1},{1,0},{2,3},{3,2},{4,5},{5,4},{6,7},{7,6},{8,9},{9,8},{10,11... | collective-permute-start | bytes 4718600 | tf_op jit(solution)/shard_map/ppermute | solution.py:198
  22.5 8.5 %collective-permute-start.8 = (bf16[128,768]{1,0:T(8,128)(2,1)S(1)}, bf16[128,768]{1,0:T(8,128)(2,1)S(1)}, u32[]{:S(2)}, u32[]{:S(2)}) collective-permute-start(bf16[128,768]{1,0:T(8,128)(2,1)S(1)} %pad_select_fusion.refs_1_.refs_2_), channel_id=1, source_target_pairs={{0,130},{130,0},{2,128},{128,2},{1,131},{131,1},{3,129},{129,3},{4... | collective-permute-start | bytes 589832 | tf_op jit(solution)/shard_map/ppermute | solution.py:202
  25.3 9.2 %collective-permute-start.6 = (bf16[256,768]{1,0:T(8,128)(2,1)}, bf16[256,768]{1,0:T(8,128)(2,1)S(1)}, u32[]{:S(2)}, u32[]{:S(2)}) collective-permute-start(bf16[256,768]{1,0:T(8,128)(2,1)} %collective-permute-done.5.refs_3_.refs_4_), channel_id=1, source_target_pairs={{0,4},{4,8},{8,12},{12,16},{16,20},{20,24},{24,28},{28,0},{1,29},{... | collective-permute-start | bytes 1179656 | tf_op jit(solution)/shard_map/ppermute | solution.py:208
  27.3 20.7 %collective-permute-start.2 = (bf16[512,768]{1,0:T(8,128)(2,1)S(1)}, bf16[512,768]{1,0:T(8,128)(2,1)}, u32[]{:S(2)}, u32[]{:S(2)}) collective-permute-start(bf16[512,768]{1,0:T(8,128)(2,1)S(1)} %constant_dynamic-slice_fusion), channel_id=1, source_target_pairs={{0,32},{32,64},{64,96},{96,0},{1,97},{33,1},{65,33},{97,65},{2,34}... | collective-permute-start | bytes 2359304 | tf_op jit(solution)/shard_map/ppermute | solution.py:208
  31.1 1.4 %collective-permute-start.9 = (bf16[128,768]{1,0:T(8,128)(2,1)S(1)}, bf16[128,768]{1,0:T(8,128)(2,1)S(1)}, u32[]{:S(2)}, u32[]{:S(2)}) collective-permute-start(bf16[128,768]{1,0:T(8,128)(2,1)S(1)} %collective-permute-done.8.refs_2_.refs_3_), channel_id=1, source_target_pairs={{0,1},{1,0},{2,3},{3,2},{4,5},{5,4},{6,7},{7,6},{8,9},{9,8},{10,11... | collective-permute-start | bytes 589832 | tf_op jit(solution)/shard_map/ppermute | solution.py:198
  32.5 8.0 %collective-permute-start.10 = (bf16[256,768]{1,0:T(8,128)(2,1)S(1)}, bf16[256,768]{1,0:T(8,128)(2,1)}, u32[]{:S(2)}, u32[]{:S(2)}) collective-permute-start(bf16[256,768]{1,0:T(8,128)(2,1)S(1)} %pad_maximum_fusion.1), channel_id=1, source_target_pairs={{0,4},{4,8},{8,12},{12,16},{16,20},{20,24},{24,28},{28,0},{1,29},{... | collective-permute-start | bytes 1179656 | tf_op jit(solution)/shard_map/ppermute | solution.py:208
  34.5 10.8 %copy-start.3 = (bf16[256,768]{1,0:T(8,128)(2,1)}, bf16[256,768]{1,0:T(8,128)(2,1)S(1)}, u32[]{:S(2)}) copy-start(bf16[256,768]{1,0:T(8,128)(2,1)S(1)} %collective-permute-done.6.refs_4_.refs_6_) | copy-start | bytes 1179652
  34.5 10.1 %collective-permute-start.7 = (bf16[256,768]{1,0:T(8,128)(2,1)S(1)}, bf16[256,768]{1,0:T(8,128)(2,1)S(1)}, u32[]{:S(2)}, u32[]{:S(2)}) collective-permute-start(bf16[256,768]{1,0:T(8,128)(2,1)S(1)} %collective-permute-done.6.refs_4_.refs_6_), channel_id=1, source_target_pairs={{0,4},{4,8},{8,12},{12,16},{16,20},{20,24},{24,28},{28,0},{1,29},{... | collective-permute-start | bytes 1179656 | tf_op jit(solution)/shard_map/ppermute | solution.py:208
  40.5 11.6 %collective-permute-start.11 = (bf16[256,768]{1,0:T(8,128)(2,1)}, bf16[256,768]{1,0:T(8,128)(2,1)}, u32[]{:S(2)}, u32[]{:S(2)}) collective-permute-start(bf16[256,768]{1,0:T(8,128)(2,1)} %collective-permute-done.10.refs_3_.refs_5_), channel_id=1, source_target_pairs={{0,4},{4,8},{8,12},{12,16},{16,20},{20,24},{24,28},{28,0},{1,29},{... | collective-permute-start | bytes 1179656 | tf_op jit(solution)/shard_map/ppermute | solution.py:208
  45.3 0.8 copy-start.1
  46.1 8.2 %collective-permute-start.13 = (bf16[128,768]{1,0:T(8,128)(2,1)}, bf16[128,768]{1,0:T(8,128)(2,1)}, u32[]{:S(2)}, u32[]{:S(2)}) collective-permute-start(bf16[128,768]{1,0:T(8,128)(2,1)} %slice.4), channel_id=1, source_target_pairs={{0,4},{4,8},{8,12},{12,16},{16,20},{20,24},{24,28},{28,0},{1,29},{... | collective-permute-start | bytes 589832 | tf_op jit(solution)/shard_map/ppermute | solution.py:208
  48.0 21.8 %collective-permute-start.3 = (bf16[512,768]{1,0:T(8,128)(2,1)}, bf16[512,768]{1,0:T(8,128)(2,1)}, u32[]{:S(2)}, u32[]{:S(2)}) collective-permute-start(bf16[512,768]{1,0:T(8,128)(2,1)} %collective-permute-done.2.refs_0_.refs_3_), channel_id=1, source_target_pairs={{0,1},{1,0},{2,3},{3,2},{4,5},{5,4},{6,7},{7,6},{8,9},{9,8},{10,11... | collective-permute-start | bytes 2359304 | tf_op jit(solution)/shard_map/ppermute | solution.py:198
  48.9 8.0 %copy-start.4 = (bf16[256,768]{1,0:T(8,128)(2,1)S(1)}, bf16[256,768]{1,0:T(8,128)(2,1)}, u32[]{:S(2)}) copy-start(bf16[256,768]{1,0:T(8,128)(2,1)} %copy-done.3) | copy-start | bytes 1179652
  52.1 23.3 %collective-permute-start.12 = (bf16[256,768]{1,0:T(8,128)(2,1)}, bf16[256,768]{1,0:T(8,128)(2,1)S(1)}, u32[]{:S(2)}, u32[]{:S(2)}) collective-permute-start(bf16[256,768]{1,0:T(8,128)(2,1)} %collective-permute-done.11.refs_5_.refs_7_), channel_id=1, source_target_pairs={{0,4},{4,8},{8,12},{12,16},{16,20},{20,24},{24,28},{28,0},{1,29},{... | collective-permute-start | bytes 1179656 | tf_op jit(solution)/shard_map/ppermute | solution.py:208
  54.2 21.2 %collective-permute-start.14 = (bf16[128,768]{1,0:T(8,128)(2,1)}, bf16[128,768]{1,0:T(8,128)(2,1)S(1)}, u32[]{:S(2)}, u32[]{:S(2)}) collective-permute-start(bf16[128,768]{1,0:T(8,128)(2,1)} %collective-permute-done.13.refs_7_), channel_id=1, source_target_pairs={{0,130},{130,0},{2,128},{128,2},{1,131},{131,1},{3,129},{129,3},{4... | collective-permute-start | bytes 589832 | tf_op jit(solution)/shard_map/ppermute | solution.py:202
  69.7 5.7 %copy-start.2 = (bf16[256,768]{1,0:T(8,128)(2,1)S(1)}, bf16[256,768]{1,0:T(8,128)(2,1)}, u32[]{:S(2)}) copy-start(bf16[256,768]{1,0:T(8,128)(2,1)} %copy-done.1) | copy-start | bytes 1179652
  87.5 10.5 %all-to-all-start = ((f32[16,2,8,128]{3,2,1,0:T(8,128)}), f32[16,2,8,128]{3,2,1,0:T(8,128)S(1)}, u32[]{:S(2)}, u32[]{:S(2)}) async-start(f32[16,2,8,128]{3,2,1,0:T(8,128)} %shard_map.54), calls=%async_computation | async-start | bytes 262144 | tf_op jit(solution)/shard_map/all_to_all | solution.py:246
  98.0 0.6 copy-start.5

commit v3 on v2

--- a/solution.py
+++ b/solution.py
@@ -11,6 +11,8 @@
 KERNEL_GAIN = 30.0
 TILE = 256
 CHUNK = 384
+STRAIGHT = 5
+TOGETHER = 2
 SIZES = {"xh": 2, "y": 4, "z": 8, "xl": 2, "core": 2}
 ROW_GROUP = ("y", "xl", "core")
 BLK = ("xh", "y", "z")
@@ -86,12 +88,22 @@
     for copy in pool_copies[1:]:
         copy.wait()
 
-    def pair(i, _):
+    def pair(i):
         step(2 * i + 1, bufs[1], tops[1], 2 * i, bufs[0], tops[0])
         step(2 * i + 2, bufs[0], tops[0], 2 * i + 1, bufs[1], tops[1])
+
+    pairs = tiles // 2 - 1
+    straight = pairs if pairs <= STRAIGHT else pairs % TOGETHER
+    for i in range(straight):
+        pair(i)
+
+    def several(j, _):
+        for k in range(TOGETHER):
+            pair(straight + j * TOGETHER + k)
         return 0
 
-    lax.fori_loop(0, tiles // 2 - 1, pair, 0)
+    if pairs > straight:
+        lax.fori_loop(0, (pairs - straight) // TOGETHER, several, 0)
     step(tiles - 1, bufs[1], tops[1], tiles - 2, bufs[0], tops[0])
     step(None, None, None, tiles - 1, bufs[1], tops[1])
 
@@ -109,14 +121,12 @@
 
 def last_kernel(n_pools, n_samples, each, scale, place, *refs):
     pools, samples = refs[:n_pools], refs[n_pools : n_pools + n_samples]
-    alone, first, second, third, out_ref, last = refs[n_pools + n_samples : n_pools + n_samples + 6]
-    joined, half_norm, pool_all, buf0, buf1, top0, top1, sems = refs[n_pools + n_samples + 6 :]
+    own, beside, swapped, second, third, out_ref, last = refs[n_pools + n_samples : n_pools + n_samples + 7]
+    joined, half_norm, pool_all, buf0, buf1, top0, top1, sems = refs[n_pools + n_samples + 7 :]
     lse_tiles(pools, samples, each, scale, last, joined, half_norm, pool_all, (buf0, buf1), (top0, top1), sems)
     y, core = place[0], place[1]
-    n = alone.shape[1]
+    n = own.shape[1]
     rest = add_exp(second[...], last[:, : 3 * n, :])
-    own = add_exp(alone[...], rest[:, :n, :])
-    near = add_exp(first[...], rest[:, n:, :])
     far = add_exp(third[...], last[:, 3 * n :, :])
 
     def put(owner, value, swapped):
@@ -129,9 +139,8 @@
             else:
                 out_ref[at, :, :, :] = value
 
-    put(y, own, False)
-    put(y + 3 - 2 * core, near[:, :n, :], False)
-    put(y + 1 + 2 * core, near[:, n:, :], False)
+    for i, (owner, part) in enumerate(((y, own), (y + 3 - 2 * core, beside), (y + 1 + 2 * core, swapped))):
+        put(owner, add_exp(part[...], rest[:, i * n : (i + 1) * n, :]), False)
     put(y + 2, far, True)
 
 
@@ -231,17 +240,18 @@
     zx2 = both_ways(zx1, "z")
     z3 = both_ways(z2, "z")
     zx3 = both_ways(zx2, "z")
-    z4 = both_ways(z3[: 2 * each], "z")
+    last = both_ways(jnp.concatenate([z3[: 2 * each], zx3[: 2 * each]], axis=0), "z")
     across = both_ways(lax.dynamic_slice_in_dim(beside, core * half, half, 0), "y")
-    near = [beside, swap_core(beside)]
+    swapped = swap_core(beside)
     far = [across, swap_core(across)]
-    earliest, early = [own, other, z1], [zx1, z2, zx2]
-    late = [z3, zx3, z4, swap_x(z4)]
-    alone = lse_call([pool_embeds], earliest, each, scale)
-    first = lse_call(near, earliest, each, scale)
-    second = lse_call([pool_embeds] + near, early, each, scale)
-    third = lse_call(far, earliest + early, each, scale)
-    send = lse_call([pool_embeds] + near + far, late, each, scale, (alone, first, second, third), place)
+    earliest, early, late = [own, other, z1], [zx1, z2, zx2], [z3, zx3, last]
+    parts = []
+    for block in (pool_embeds, beside, swapped):
+        parts.append(lse_call([block], earliest, each, scale))
+    near = [pool_embeds, beside, swapped]
+    parts.append(lse_call(near, early, each, scale))
+    parts.append(lse_call(far, earliest + early, each, scale))
+    send = lse_call(near + far, late, each, scale, parts, place)
 
     got = lax.all_to_all(send, ROW_GROUP, 0, 0)
     pool_norms = jnp.sum(jnp.square(pool_embeds.astype(jnp.float32)), axis=1) * (KERNEL_GAIN / depth)

time: 125 us -> 128 us (1.024)
  waiting for transfers between devices: 32.5 us -> 40.1 us
  starting transfers between devices: 26.8 us -> 20.7 us
  blocking collectives: 21.2 us -> 23.6 us
  local copies, waits for them, and re-layouts: 2.15 us -> 0.74 us
    ppermute x9, waiting for transfers between devices: 20.6 us -> 28.5 us  [both_ways(): return lax.ppermute(value, (axis, 'core'), pairs)]
    ppermute x9, starting transfers between devices: 15.8 us -> 10.4 us  [both_ways(): return lax.ppermute(value, (axis, 'core'), pairs)]
    ppermute x2 -> x1, starting transfers between devices: 5.52 us -> 2.85 us  [swap_x(): return lax.ppermute(value, ('xh', 'xl'), [(0, 3), (3, 0), (1, 2), (2, 1)])]
    ppermute x4, waiting for transfers between devices: 2.51 us -> 0.01 us  [swap_core(): return lax.ppermute(value, 'core', [(0, 1), (1, 0)])]
    all_to_all x1, blocking collectives: 21.2 us -> 23.6 us  [body(): stats = lax.all_to_all(stats, BLK, 0, 0, tiled=True)]
    ppermute x2 -> x1, waiting for transfers between devices: 3.35 us -> 5.49 us  [swap_x(): return lax.ppermute(value, ('xh', 'xl'), [(0, 3), (3, 0), (1, 2), (2, 1)])]
    all_to_all x1, starting transfers between devices: 3.83 us -> 5.19 us  [body(): got = lax.all_to_all(send, ROW_GROUP, 0, 0)]
    pallas_call x4 -> x5, Pallas kernels: 21.5 us -> 22.4 us  [lse_call(): pl.pallas_call(kernel, out_shape=partial, in_specs=inputs, scratch_shapes...]
  transfers between devices with their start and end apart: 16 -> 15, of which waited for: 7 -> 9; matrix products, arithmetic and copies ran while one was open for 3% -> 3% of each run, Pallas kernels for 17% -> 18%
where the time goes in v3:
time: 128 us; the launch traced here: 126 us
  waiting for transfers between devices  40.1 us (31%)
  Pallas kernels  37.3 us (29%)
  blocking collectives  23.6 us (18%)
  starting transfers between devices  20.7 us (16%)
  other arithmetic  3.1 us (2%)
    ppermute x9, waiting for transfers between devices, both_ways(): return lax.ppermute(value, (axis, 'core'), pairs)  28.5 us
    all_to_all x1, blocking collectives, body(): stats = lax.all_to_all(stats, BLK, 0, 0, tiled=True)  23.6 us
    pallas_call x5, Pallas kernels, lse_call(): pl.pallas_call(kernel, out_shape=partial, in_specs=inputs, scratch_shapes...  22.4 us
    pallas_call x1, Pallas kernels, lse_call(): pl.pallas_call(kernel, out_shape=jax.ShapeDtypeStruct((16, 2, pools[0].sh...  11.5 us
    ppermute x9, starting transfers between devices, both_ways(): return lax.ppermute(value, (axis, 'core'), pairs)  10.4 us
    all_to_all x1, waiting for transfers between devices, body(): got = lax.all_to_all(send, ROW_GROUP, 0, 0)  6.07 us
    ppermute x1, waiting for transfers between devices, swap_x(): return lax.ppermute(value, ('xh', 'xl'), [(0, 3), (3, 0), (1, 2), (2, 1)])  5.49 us
    all_to_all x1, starting transfers between devices, body(): got = lax.all_to_all(send, ROW_GROUP, 0, 0)  5.19 us
  transfers between devices with their start and end apart: 15, of which 9 were waited for; matrix products, arithmetic and copies ran while one was open for 3% of the time, Pallas kernels for 18%

profile of v3, /device:TPU:32, one launch (start us, length us, event | category | flops | bytes accessed | tf_op | source)
XLA Modules:
  0.0 126.3 jit_solution(18117552345827684140)
XLA Ops:
  0.6 1.7 %collective-permute-start = (bf16[1024,768]{1,0:T(8,128)(2,1)}, bf16[1024,768]{1,0:T(8,128)(2,1)S(1)}, u32[]{:S(2)}, u32[]{:S(2)}) collective-permute-start(bf16[1024,768]{1,0:T(8,128)(2,1)} %refs_0_.5), channel_id=1, source_target_pairs={{0,32},{32,64},{64,96},{96,0},{1,97},{33,1},{65,33},{97,65},{2,34}... | collective-permute-start | bytes 4718600 | tf_op jit(solution)/shard_map/ppermute | solution.py:217
  2.3 1.0 pad_select_fusion.refs_1_.refs_2_
  3.3 2.8 %collective-permute-start.8 = (bf16[128,768]{1,0:T(8,128)(2,1)S(1)}, bf16[128,768]{1,0:T(8,128)(2,1)S(1)}, u32[]{:S(2)}, u32[]{:S(2)}) collective-permute-start(bf16[128,768]{1,0:T(8,128)(2,1)S(1)} %pad_select_fusion.refs_1_.refs_2_), channel_id=1, source_target_pairs={{0,130},{130,0},{2,128},{128,2},{1,131},{131,1},{3,129},{129,3},{4... | collective-permute-start | bytes 589832 | tf_op jit(solution)/shard_map/ppermute | solution.py:211
  6.2 0.7 collective-permute-start.4
  6.9 0.0 copy-start
  6.9 5.5 %collective-permute-done.8.refs_2_.refs_3_ = bf16[128,768]{1,0:T(8,128)(2,1)S(1)} collective-permute-done((bf16[128,768]{1,0:T(8,128)(2,1)S(1)}, bf16[128,768]{1,0:T(8,128)(2,1)S(1)}, u32[]{:S(2)}, u32[]{:S(2)}) %collective-permute-start.8) | collective-permute-done | bytes 196640 | tf_op jit(solution)/shard_map/ppermute | solution.py:211
  12.4 0.1 collective-permute-start.9
  12.5 10.0 %collective-permute-done.refs_0_.refs_1_ = bf16[1024,768]{1,0:T(8,128)(2,1)S(1)} collective-permute-done((bf16[1024,768]{1,0:T(8,128)(2,1)}, bf16[1024,768]{1,0:T(8,128)(2,1)S(1)}, u32[]{:S(2)}, u32[]{:S(2)}) %collective-permute-start) | collective-permute-done | bytes 1572896 | tf_op jit(solution)/shard_map/ppermute | solution.py:217
  22.5 0.1 constant_dynamic-slice_fusion
  22.6 0.4 collective-permute-start.2
  23.0 0.0 collective-permute-done.4
  23.0 1.0 pad_maximum_fusion
  24.0 2.0 %collective-permute-start.5 = (bf16[256,768]{1,0:T(8,128)(2,1)S(1)}, bf16[256,768]{1,0:T(8,128)(2,1)}, u32[]{:S(2)}, u32[]{:S(2)}) collective-permute-start(bf16[256,768]{1,0:T(8,128)(2,1)S(1)} %pad_maximum_fusion), channel_id=1, source_target_pairs={{0,4},{4,8},{8,12},{12,16},{16,20},{20,24},{24,28},{28,0},{1,29},{... | collective-permute-start | bytes 1179656 | tf_op jit(solution)/shard_map/ppermute | solution.py:217
  26.0 0.0 collective-permute-start.1
  26.0 0.0 collective-permute-done.9
  26.0 2.0 %collective-permute-start.10 = (bf16[256,768]{1,0:T(8,128)(2,1)S(1)}, bf16[256,768]{1,0:T(8,128)(2,1)}, u32[]{:S(2)}, u32[]{:S(2)}) collective-permute-start(bf16[256,768]{1,0:T(8,128)(2,1)S(1)} %pad_maximum_fusion.1), channel_id=1, source_target_pairs={{0,4},{4,8},{8,12},{12,16},{16,20},{20,24},{24,28},{28,0},{1,29},{... | collective-permute-start | bytes 1179656 | tf_op jit(solution)/shard_map/ppermute | solution.py:217
  28.0 3.9 %collective-permute-done.5.refs_3_.refs_4_ = bf16[256,768]{1,0:T(8,128)(2,1)} collective-permute-done((bf16[256,768]{1,0:T(8,128)(2,1)S(1)}, bf16[256,768]{1,0:T(8,128)(2,1)}, u32[]{:S(2)}, u32[]{:S(2)}) %collective-permute-start.5) | collective-permute-done | bytes 393248 | tf_op jit(solution)/shard_map/ppermute | solution.py:217
  32.0 1.9 %collective-permute-start.6 = (bf16[256,768]{1,0:T(8,128)(2,1)}, bf16[256,768]{1,0:T(8,128)(2,1)}, u32[]{:S(2)}, u32[]{:S(2)}) collective-permute-start(bf16[256,768]{1,0:T(8,128)(2,1)} %collective-permute-done.5.refs_3_.refs_4_), channel_id=1, source_target_pairs={{0,4},{4,8},{8,12},{12,16},{16,20},{20,24},{24,28},{28,0},{1,29},{... | collective-permute-start | bytes 1179656 | tf_op jit(solution)/shard_map/ppermute | solution.py:217
  33.9 2.9 %collective-permute-done.10.refs_3_.refs_5_ = bf16[256,768]{1,0:T(8,128)(2,1)} collective-permute-done((bf16[256,768]{1,0:T(8,128)(2,1)S(1)}, bf16[256,768]{1,0:T(8,128)(2,1)}, u32[]{:S(2)}, u32[]{:S(2)}) %collective-permute-start.10) | collective-permute-done | bytes 393248 | tf_op jit(solution)/shard_map/ppermute | solution.py:217
  36.8 1.3 %collective-permute-start.11 = (bf16[256,768]{1,0:T(8,128)(2,1)}, bf16[256,768]{1,0:T(8,128)(2,1)}, u32[]{:S(2)}, u32[]{:S(2)}) collective-permute-start(bf16[256,768]{1,0:T(8,128)(2,1)} %collective-permute-done.10.refs_3_.refs_5_), channel_id=1, source_target_pairs={{0,4},{4,8},{8,12},{12,16},{16,20},{20,24},{24,28},{28,0},{1,29},{... | collective-permute-start | bytes 1179656 | tf_op jit(solution)/shard_map/ppermute | solution.py:217
  38.1 0.0 collective-permute-done.2.refs_0_.refs_3_
  38.1 1.4 %collective-permute-start.3 = (bf16[512,768]{1,0:T(8,128)(2,1)}, bf16[512,768]{1,0:T(8,128)(2,1)}, u32[]{:S(2)}, u32[]{:S(2)}) collective-permute-start(bf16[512,768]{1,0:T(8,128)(2,1)} %collective-permute-done.2.refs_0_.refs_3_), channel_id=1, source_target_pairs={{0,1},{1,0},{2,3},{3,2},{4,5},{5,4},{6,7},{7,6},{8,9},{9,8},{10,11... | collective-permute-start | bytes 2359304 | tf_op jit(solution)/shard_map/ppermute | solution.py:207
  39.5 2.5 %collective-permute-done.6.refs_4_.refs_6_ = bf16[256,768]{1,0:T(8,128)(2,1)} collective-permute-done((bf16[256,768]{1,0:T(8,128)(2,1)}, bf16[256,768]{1,0:T(8,128)(2,1)}, u32[]{:S(2)}, u32[]{:S(2)}) %collective-permute-start.6) | collective-permute-done | bytes 393248 | tf_op jit(solution)/shard_map/ppermute | solution.py:217
  42.0 0.3 collective-permute-start.7
  42.3 3.9 %collective-permute-done.11.refs_5_.refs_7_ = bf16[256,768]{1,0:T(8,128)(2,1)} collective-permute-done((bf16[256,768]{1,0:T(8,128)(2,1)}, bf16[256,768]{1,0:T(8,128)(2,1)}, u32[]{:S(2)}, u32[]{:S(2)}) %collective-permute-start.11) | collective-permute-done | bytes 393248 | tf_op jit(solution)/shard_map/ppermute | solution.py:217
  46.2 0.3 collective-permute-start.12
  46.5 0.1 pad_add_fusion.place
  46.6 0.0 copy-done
  46.6 0.4 multiply_reduce_fusion
  47.0 3.1 %shard_map.50.refs_8_ = f32[2,8,128]{2,1,0:T(8,128)S(1)} custom-call(bf16[1024,768]{1,0:T(8,128)(2,1)S(1)} %copy-done, bf16[128,768]{1,0:T(8,128)(2,1)S(1)} %pad_select_fusion.refs_1_.refs_2_, bf16[128,768]{1,0:T(8,128)(2,1)S(1)} %collective-permute-done.8.refs_2_.refs_3_, bf16[256,768]{1,0:T(8,128)(2,1)} %collective-permute-done.5.refs_3_.refs_4_), custom_call_target="tpu_custom_call" | custom-call | flops 805306368 | bytes 2359296 | tf_op jit(solution)/shard_map/pallas_call | solution.py:172
  50.1 1.1 collective-permute-done.7.refs_5_
  51.2 4.2 %collective-permute-done.12.refs_6_ = bf16[256,768]{1,0:T(8,128)(2,1)S(1)} collective-permute-done((bf16[256,768]{1,0:T(8,128)(2,1)}, bf16[256,768]{1,0:T(8,128)(2,1)S(1)}, u32[]{:S(2)}, u32[]{:S(2)}) %collective-permute-start.12) | collective-permute-done | bytes 393248 | tf_op jit(solution)/shard_map/ppermute | solution.py:217
  55.4 0.4 collective-permute-start.13
  55.9 3.1 %shard_map.51.refs_9_ = f32[2,8,128]{2,1,0:T(8,128)S(1)} custom-call(bf16[1024,768]{1,0:T(8,128)(2,1)S(1)} %collective-permute-done.refs_0_.refs_1_, bf16[128,768]{1,0:T(8,128)(2,1)S(1)} %pad_select_fusion.refs_1_.refs_2_, bf16[128,768]{1,0:T(8,128)(2,1)S(1)} %collective-permute-done.8.refs_2_.refs_3_, bf16[256,768]{1,0:T(8,128)(2,1)} %collective-permute-done.5.refs_3_.refs_4_), custom_call_target="tpu_custom_call" | custom-call | flops 805306368 | bytes 2359296 | tf_op jit(solution)/shard_map/pallas_call | solution.py:172
  59.0 0.0 collective-permute-done.3.refs_1_.refs_4_
  59.0 5.5 %shard_map.54.refs_12_ = f32[2,8,128]{2,1,0:T(8,128)S(1)} custom-call(bf16[512,768]{1,0:T(8,128)(2,1)} %collective-permute-done.2.refs_0_.refs_3_, bf16[512,768]{1,0:T(8,128)(2,1)} %collective-permute-done.3.refs_1_.refs_4_, bf16[128,768]{1,0:T(8,128)(2,1)S(1)} %pad_select_fusion.refs_1_.refs_2_, ...), custom_call_target="tpu_custom_call" | custom-call | flops 2013265920 | bytes 3538944 | tf_op jit(solution)/shard_map/pallas_call | solution.py:172
  64.6 0.0 collective-permute-done.1.refs_0_.refs_2_
  64.6 3.5 %shard_map.52.refs_10_ = f32[2,8,128]{2,1,0:T(8,128)S(1)} custom-call(bf16[1024,768]{1,0:T(8,128)(2,1)} %collective-permute-done.1.refs_0_.refs_2_, bf16[128,768]{1,0:T(8,128)(2,1)S(1)} %pad_select_fusion.refs_1_.refs_2_, bf16[128,768]{1,0:T(8,128)(2,1)S(1)} %collective-permute-done.8.refs_2_.refs_3_, bf16[256,768]{1,0:T(8,128)(2,1)} %collective-permute-done.5.refs_3_.refs_4_), custom_call_target="tpu_custom_call" | custom-call | flops 805306368 | bytes 2359296 | tf_op jit(solution)/shard_map/pallas_call | solution.py:172
  68.1 7.2 %shard_map.53.refs_11_ = f32[2,24,128]{2,1,0:T(8,128)S(1)} custom-call(bf16[1024,768]{1,0:T(8,128)(2,1)S(1)} %copy-done, bf16[1024,768]{1,0:T(8,128)(2,1)S(1)} %collective-permute-done.refs_0_.refs_1_, bf16[1024,768]{1,0:T(8,128)(2,1)} %collective-permute-done.1.refs_0_.refs_2_, bf16[256,768]{1,0:T(8,128)(2,1)} %collective-permute-done.10.refs_3_.refs_5_, ...), custom_call_target="tpu_custom_call" | custom-call | flops 3623878656 | bytes 5898240 | tf_op jit(solution)/shard_map/pallas_call | solution.py:172
  75.3 0.0 collective-permute-done.13.refs_7_
  75.3 11.5 %shard_map.55 = f32[16,2,8,128]{3,2,1,0:T(8,128)} custom-call(s32[2]{0:T(128)S(1)} %pad_add_fusion.place, bf16[1024,768]{1,0:T(8,128)(2,1)S(1)} %copy-done, bf16[1024,768]{1,0:T(8,128)(2,1)S(1)} %collective-permute-done.refs_0_.refs_1_, bf16[1024,768]{1,0:T(8,128)(2,1)} %collective-permute-done.1.refs_0_.refs_2_, ...), custom_call_target="tpu_custom_call" | custom-call | flops 4831838208 | bytes 7471104 | tf_op jit(solution)/shard_map/pallas_call | solution.py:174
  86.8 5.2 %all-to-all-start = ((f32[16,2,8,128]{3,2,1,0:T(8,128)}), f32[16,2,8,128]{3,2,1,0:T(8,128)S(1)}, u32[]{:S(2)}, u32[]{:S(2)}) async-start(f32[16,2,8,128]{3,2,1,0:T(8,128)} %shard_map.55), calls=%async_computation | async-start | bytes 262144 | tf_op jit(solution)/shard_map/all_to_all | solution.py:256
  92.0 0.6 multiply_bitcast_fusion.norms
  92.6 6.1 %all-to-all-done.got = f32[16,2,8,128]{3,2,1,0:T(8,128)S(1)} async-done(((f32[16,2,8,128]{3,2,1,0:T(8,128)}), f32[16,2,8,128]{3,2,1,0:T(8,128)S(1)}, u32[]{:S(2)}, u32[]{:S(2)}) %all-to-all-start) | async-done | bytes 131104 | tf_op jit(solution)/shard_map/all_to_all | solution.py:256
  98.6 0.7 copy-done.1
  99.3 1.8 %shard_map.56 = (f32[8,128]{1,0:T(8,128)}, f32[64,128]{1,0:T(8,128)}) custom-call(f32[16,2,8,128]{3,2,1,0:T(8,128)} %copy-done.1, f32[8,128]{1,0:T(8,128)} %multiply_bitcast_fusion.norms), custom_call_target="tpu_custom_call" | custom-call | tf_op jit(solution)/shard_map/pallas_call | solution.py:260
  101.1 23.6 %all_to_all.16 = f32[64,1,128]{2,1,0:T(1,128)} all-to-all(f32[64,1,128]{2,1,0:T(1,128)} %bitcast.11), channel_id=1, replica_groups=mesh['xh'=2,'y'=4,'z'=8,'xl'=2,'core'=2] {'xh','y','z'}, dimensions={0} | all-to-all | bytes 65536 | tf_op jit(solution)/shard_map/all_to_all | solution.py:266
  124.7 1.6 %shard_map.57 = f32[8,128]{1,0:T(8,128)} custom-call(f32[8,128]{1,0:T(8,128)} %get-tuple-element.4.ratio, f32[64,128]{1,0:T(8,128)} %bitcast.10), custom_call_target="tpu_custom_call" | custom-call | tf_op jit(solution)/shard_map/pallas_call | solution.py:267
  (6 shorter events, 0.1 us)
Async XLA Ops:
  0.6 21.9 %collective-permute-start = (bf16[1024,768]{1,0:T(8,128)(2,1)}, bf16[1024,768]{1,0:T(8,128)(2,1)S(1)}, u32[]{:S(2)}, u32[]{:S(2)}) collective-permute-start(bf16[1024,768]{1,0:T(8,128)(2,1)} %refs_0_.5), channel_id=1, source_target_pairs={{0,32},{32,64},{64,96},{96,0},{1,97},{33,1},{65,33},{97,65},{2,34}... | collective-permute-start | bytes 4718600 | tf_op jit(solution)/shard_map/ppermute | solution.py:217
  3.3 9.0 %collective-permute-start.8 = (bf16[128,768]{1,0:T(8,128)(2,1)S(1)}, bf16[128,768]{1,0:T(8,128)(2,1)S(1)}, u32[]{:S(2)}, u32[]{:S(2)}) collective-permute-start(bf16[128,768]{1,0:T(8,128)(2,1)S(1)} %pad_select_fusion.refs_1_.refs_2_), channel_id=1, source_target_pairs={{0,130},{130,0},{2,128},{128,2},{1,131},{131,1},{3,129},{129,3},{4... | collective-permute-start | bytes 589832 | tf_op jit(solution)/shard_map/ppermute | solution.py:211
  6.2 16.9 %collective-permute-start.4 = (bf16[128,768]{1,0:T(8,128)(2,1)S(1)}, bf16[128,768]{1,0:T(8,128)(2,1)}, u32[]{:S(2)}, u32[]{:S(2)}) collective-permute-start(bf16[128,768]{1,0:T(8,128)(2,1)S(1)} %pad_select_fusion.refs_1_.refs_2_), channel_id=1, source_target_pairs={{0,1},{1,0},{2,3},{3,2},{4,5},{5,4},{6,7},{7,6},{8,9},{9,8},{10,11... | collective-permute-start | bytes 589832 | tf_op jit(solution)/shard_map/ppermute | solution.py:207
  6.9 39.7 %copy-start = (bf16[1024,768]{1,0:T(8,128)(2,1)S(1)}, bf16[1024,768]{1,0:T(8,128)(2,1)}, u32[]{:S(2)}) copy-start(bf16[1024,768]{1,0:T(8,128)(2,1)} %refs_0_.5) | copy-start | bytes 4718596
  12.4 13.6 %collective-permute-start.9 = (bf16[128,768]{1,0:T(8,128)(2,1)S(1)}, bf16[128,768]{1,0:T(8,128)(2,1)S(1)}, u32[]{:S(2)}, u32[]{:S(2)}) collective-permute-start(bf16[128,768]{1,0:T(8,128)(2,1)S(1)} %collective-permute-done.8.refs_2_.refs_3_), channel_id=1, source_target_pairs={{0,1},{1,0},{2,3},{3,2},{4,5},{5,4},{6,7},{7,6},{8,9},{9,8},{10,11... | collective-permute-start | bytes 589832 | tf_op jit(solution)/shard_map/ppermute | solution.py:207
  22.6 15.5 %collective-permute-start.2 = (bf16[512,768]{1,0:T(8,128)(2,1)S(1)}, bf16[512,768]{1,0:T(8,128)(2,1)}, u32[]{:S(2)}, u32[]{:S(2)}) collective-permute-start(bf16[512,768]{1,0:T(8,128)(2,1)S(1)} %constant_dynamic-slice_fusion), channel_id=1, source_target_pairs={{0,32},{32,64},{64,96},{96,0},{1,97},{33,1},{65,33},{97,65},{2,34}... | collective-permute-start | bytes 2359304 | tf_op jit(solution)/shard_map/ppermute | solution.py:217
  24.0 8.0 %collective-permute-start.5 = (bf16[256,768]{1,0:T(8,128)(2,1)S(1)}, bf16[256,768]{1,0:T(8,128)(2,1)}, u32[]{:S(2)}, u32[]{:S(2)}) collective-permute-start(bf16[256,768]{1,0:T(8,128)(2,1)S(1)} %pad_maximum_fusion), channel_id=1, source_target_pairs={{0,4},{4,8},{8,12},{12,16},{16,20},{20,24},{24,28},{28,0},{1,29},{... | collective-permute-start | bytes 1179656 | tf_op jit(solution)/shard_map/ppermute | solution.py:217
  26.0 38.6 %collective-permute-start.1 = (bf16[1024,768]{1,0:T(8,128)(2,1)S(1)}, bf16[1024,768]{1,0:T(8,128)(2,1)}, u32[]{:S(2)}, u32[]{:S(2)}) collective-permute-start(bf16[1024,768]{1,0:T(8,128)(2,1)S(1)} %collective-permute-done.refs_0_.refs_1_), channel_id=1, source_target_pairs={{0,1},{1,0},{2,3},{3,2},{4,5},{5,4},{6,7},{7,6},{8,9},{9,8},{10,11... | collective-permute-start | bytes 4718600 | tf_op jit(solution)/shard_map/ppermute | solution.py:207
  26.0 10.8 %collective-permute-start.10 = (bf16[256,768]{1,0:T(8,128)(2,1)S(1)}, bf16[256,768]{1,0:T(8,128)(2,1)}, u32[]{:S(2)}, u32[]{:S(2)}) collective-permute-start(bf16[256,768]{1,0:T(8,128)(2,1)S(1)} %pad_maximum_fusion.1), channel_id=1, source_target_pairs={{0,4},{4,8},{8,12},{12,16},{16,20},{20,24},{24,28},{28,0},{1,29},{... | collective-permute-start | bytes 1179656 | tf_op jit(solution)/shard_map/ppermute | solution.py:217
  32.0 10.0 %collective-permute-start.6 = (bf16[256,768]{1,0:T(8,128)(2,1)}, bf16[256,768]{1,0:T(8,128)(2,1)}, u32[]{:S(2)}, u32[]{:S(2)}) collective-permute-start(bf16[256,768]{1,0:T(8,128)(2,1)} %collective-permute-done.5.refs_3_.refs_4_), channel_id=1, source_target_pairs={{0,4},{4,8},{8,12},{12,16},{16,20},{20,24},{24,28},{28,0},{1,29},{... | collective-permute-start | bytes 1179656 | tf_op jit(solution)/shard_map/ppermute | solution.py:217
  36.8 9.4 %collective-permute-start.11 = (bf16[256,768]{1,0:T(8,128)(2,1)}, bf16[256,768]{1,0:T(8,128)(2,1)}, u32[]{:S(2)}, u32[]{:S(2)}) collective-permute-start(bf16[256,768]{1,0:T(8,128)(2,1)} %collective-permute-done.10.refs_3_.refs_5_), channel_id=1, source_target_pairs={{0,4},{4,8},{8,12},{12,16},{16,20},{20,24},{24,28},{28,0},{1,29},{... | collective-permute-start | bytes 1179656 | tf_op jit(solution)/shard_map/ppermute | solution.py:217
  38.1 20.9 %collective-permute-start.3 = (bf16[512,768]{1,0:T(8,128)(2,1)}, bf16[512,768]{1,0:T(8,128)(2,1)}, u32[]{:S(2)}, u32[]{:S(2)}) collective-permute-start(bf16[512,768]{1,0:T(8,128)(2,1)} %collective-permute-done.2.refs_0_.refs_3_), channel_id=1, source_target_pairs={{0,1},{1,0},{2,3},{3,2},{4,5},{5,4},{6,7},{7,6},{8,9},{9,8},{10,11... | collective-permute-start | bytes 2359304 | tf_op jit(solution)/shard_map/ppermute | solution.py:207
  42.0 9.2 %collective-permute-start.7 = (bf16[256,768]{1,0:T(8,128)(2,1)}, bf16[256,768]{1,0:T(8,128)(2,1)S(1)}, u32[]{:S(2)}, u32[]{:S(2)}) collective-permute-start(bf16[256,768]{1,0:T(8,128)(2,1)} %collective-permute-done.6.refs_4_.refs_6_), channel_id=1, source_target_pairs={{0,4},{4,8},{8,12},{12,16},{16,20},{20,24},{24,28},{28,0},{1,29},{... | collective-permute-start | bytes 1179656 | tf_op jit(solution)/shard_map/ppermute | solution.py:217
  46.2 9.2 %collective-permute-start.12 = (bf16[256,768]{1,0:T(8,128)(2,1)}, bf16[256,768]{1,0:T(8,128)(2,1)S(1)}, u32[]{:S(2)}, u32[]{:S(2)}) collective-permute-start(bf16[256,768]{1,0:T(8,128)(2,1)} %collective-permute-done.11.refs_5_.refs_7_), channel_id=1, source_target_pairs={{0,4},{4,8},{8,12},{12,16},{16,20},{20,24},{24,28},{28,0},{1,29},{... | collective-permute-start | bytes 1179656 | tf_op jit(solution)/shard_map/ppermute | solution.py:217
  55.4 19.8 %collective-permute-start.13 = (bf16[256,768]{1,0:T(8,128)(2,1)S(1)}, bf16[256,768]{1,0:T(8,128)(2,1)S(1)}, u32[]{:S(2)}, u32[]{:S(2)}) collective-permute-start(bf16[256,768]{1,0:T(8,128)(2,1)S(1)} %pad_maximum_fusion.2), channel_id=1, source_target_pairs={{0,4},{4,8},{8,12},{12,16},{16,20},{20,24},{24,28},{28,0},{1,29},{... | collective-permute-start | bytes 1179656 | tf_op jit(solution)/shard_map/ppermute | solution.py:217
  86.8 11.9 %all-to-all-start = ((f32[16,2,8,128]{3,2,1,0:T(8,128)}), f32[16,2,8,128]{3,2,1,0:T(8,128)S(1)}, u32[]{:S(2)}, u32[]{:S(2)}) async-start(f32[16,2,8,128]{3,2,1,0:T(8,128)} %shard_map.55), calls=%async_computation | async-start | bytes 262144 | tf_op jit(solution)/shard_map/all_to_all | solution.py:256
  98.6 0.7 copy-start.1

commit v4 on v3

--- a/solution.py
+++ b/solution.py
@@ -19,12 +19,12 @@
 VMEM = pl.BlockSpec(memory_space=pltpu.VMEM)
 
 
-def lse_tiles(pools, samples, each, scale, out_ref, joined, half_norm, pool_all, bufs, tops, sems):
+def lse_tiles(pools, samples, used, each, scale, out_ref, joined, half_norm, pool_all, bufs, tops, sems):
     rows = joined.shape[0]
     member = rows // 2
     sample_copies, pool_copies = [], []
-    for ref in samples:
-        for unit in range(0, ref.shape[0], 2 * each):
+    for ref, taken in zip(samples, used):
+        for unit in range(0, taken, 2 * each):
             n = len(sample_copies)
             at = n // 2 * each
             for m in range(2):
@@ -108,10 +108,10 @@
     step(None, None, None, tiles - 1, bufs[1], tops[1])
 
 
-def partial_kernel(n_pools, n_samples, each, scale, *refs):
+def partial_kernel(n_pools, n_samples, used, each, scale, *refs):
     pools, samples, out_ref = refs[:n_pools], refs[n_pools : n_pools + n_samples], refs[n_pools + n_samples]
     joined, half_norm, pool_all, buf0, buf1, top0, top1, sems = refs[n_pools + n_samples + 1 :]
-    lse_tiles(pools, samples, each, scale, out_ref, joined, half_norm, pool_all, (buf0, buf1), (top0, top1), sems)
+    lse_tiles(pools, samples, used, each, scale, out_ref, joined, half_norm, pool_all, (buf0, buf1), (top0, top1), sems)
 
 
 def add_exp(a, b):
@@ -119,12 +119,12 @@
     return high + jnp.log(jnp.exp(a - high) + jnp.exp(b - high))
 
 
-def last_kernel(n_pools, n_samples, each, scale, place, *refs):
+def last_kernel(n_pools, n_samples, used, each, scale, *refs):
     pools, samples = refs[:n_pools], refs[n_pools : n_pools + n_samples]
     own, beside, swapped, second, third, out_ref, last = refs[n_pools + n_samples : n_pools + n_samples + 7]
     joined, half_norm, pool_all, buf0, buf1, top0, top1, sems = refs[n_pools + n_samples + 7 :]
-    lse_tiles(pools, samples, each, scale, last, joined, half_norm, pool_all, (buf0, buf1), (top0, top1), sems)
-    y, core = place[0], place[1]
+    lse_tiles(pools, samples, used, each, scale, last, joined, half_norm, pool_all, (buf0, buf1), (top0, top1), sems)
+    y, core = lax.axis_index("y"), lax.axis_index("core")
     n = own.shape[1]
     rest = add_exp(second[...], last[:, : 3 * n, :])
     far = add_exp(third[...], last[:, 3 * n :, :])
@@ -144,9 +144,10 @@
     put(y + 2, far, True)
 
 
-def lse_call(pools, samples, each, scale, earlier=None, place=None):
+def lse_call(pools, samples, each, scale, earlier=None, used=None):
+    used = used or tuple(s.shape[0] for s in samples)
     count = sum(p.shape[0] for p in pools)
-    rows = sum(s.shape[0] for s in samples)
+    rows = sum(used)
     depth = pools[0].shape[1]
     scratch = [
         pltpu.VMEM((rows, depth), jnp.bfloat16),
@@ -168,24 +169,24 @@
     )
     inputs = [pl.BlockSpec(memory_space=pl.ANY)] * (len(pools) + len(samples))
     if earlier is None:
-        kernel = functools.partial(partial_kernel, len(pools), len(samples), each, scale)
+        kernel = functools.partial(partial_kernel, len(pools), len(samples), used, each, scale)
         return pl.pallas_call(kernel, out_shape=partial, in_specs=inputs, scratch_shapes=scratch, **common)(*pools, *samples)
-    kernel = functools.partial(last_kernel, len(pools), len(samples), each, scale)
+    kernel = functools.partial(last_kernel, len(pools), len(samples), used, each, scale)
     return pl.pallas_call(
         kernel,
         out_shape=jax.ShapeDtypeStruct((16, 2, pools[0].shape[0] // 128, 128), jnp.float32),
-        in_specs=[pl.BlockSpec(memory_space=pltpu.SMEM)] + inputs + [VMEM] * len(earlier),
+        in_specs=inputs + [VMEM] * len(earlier),
         scratch_shapes=[pltpu.VMEM(partial.shape, jnp.float32)] + scratch,
         **common,
-    )(place, *pools, *samples, *earlier)
-
-
-def merge_kernel(got, norms, ratio_ref, stats_ref):
+    )(*pools, *samples, *earlier)
+
+
+def merge_kernel(norm_scale, got, norms, ratio_ref, stats_ref):
     value = got[...]
     high = jnp.max(value, axis=0)
     total = high + jnp.log(jnp.sum(jnp.exp(value - high[None]), axis=0))
-    log_target = total[0] - norms[...]
-    log_ref = total[1] - norms[...]
+    log_target = total[0] - norms[...] * norm_scale
+    log_ref = total[1] - norms[...] * norm_scale
     ratio = log_target - log_ref
     ratio_ref[...] = ratio
     count = ratio.shape[0] * ratio.shape[1]
@@ -223,7 +224,6 @@
     core = lax.axis_index("core")
     each = target_samples.shape[0]
     scale = 2.0 * KERNEL_GAIN / depth
-    place = jnp.stack([lax.axis_index("y"), core]).astype(jnp.int32)
 
     own = jnp.where(
         lax.broadcasted_iota(jnp.int32, (2 * each, depth), 0) < each,
@@ -231,6 +231,7 @@
         jnp.pad(reference_samples, ((each, 0), (0, 0))),
     )
     beside = both_ways(pool_embeds, "y")
+    pool_norms = jnp.sum(jnp.square(pool_embeds.astype(jnp.float32)), axis=1)
     other = swap_x(own)
     block = jnp.concatenate([own, swap_core(own)], axis=0)
     z1 = both_ways(block, "z")
@@ -240,25 +241,25 @@
     zx2 = both_ways(zx1, "z")
     z3 = both_ways(z2, "z")
     zx3 = both_ways(zx2, "z")
-    last = both_ways(jnp.concatenate([z3[: 2 * each], zx3[: 2 * each]], axis=0), "z")
+    z4, zx4 = both_ways(z3, "z"), both_ways(zx3, "z")
     across = both_ways(lax.dynamic_slice_in_dim(beside, core * half, half, 0), "y")
     swapped = swap_core(beside)
     far = [across, swap_core(across)]
-    earliest, early, late = [own, other, z1], [zx1, z2, zx2], [z3, zx3, last]
+    earliest, early, late = [own, other, z1], [zx1, z2, zx2], [z3, zx3, z4, zx4]
     parts = []
     for block in (pool_embeds, beside, swapped):
         parts.append(lse_call([block], earliest, each, scale))
     near = [pool_embeds, beside, swapped]
     parts.append(lse_call(near, early, each, scale))
     parts.append(lse_call(far, earliest + early, each, scale))
-    send = lse_call(near + far, late, each, scale, parts, place)
+    used = (4 * each, 4 * each, 2 * each, 2 * each)
+    send = lse_call(near + far, late, each, scale, parts, used)
 
     got = lax.all_to_all(send, ROW_GROUP, 0, 0)
-    pool_norms = jnp.sum(jnp.square(pool_embeds.astype(jnp.float32)), axis=1) * (KERNEL_GAIN / depth)
     dense = (count // 128, 128)
     blocks = lax.axis_size(BLK)
     log_ratio, stats = pl.pallas_call(
-        merge_kernel,
+        functools.partial(merge_kernel, KERNEL_GAIN / depth),
         out_shape=(jax.ShapeDtypeStruct(dense, jnp.float32), jax.ShapeDtypeStruct((blocks, 128), jnp.float32)),
         in_specs=[VMEM, VMEM],
         out_specs=(VMEM, VMEM),

time: 128 us -> 125 us (0.977)
  starting transfers between devices: 20.7 us -> 23.6 us
  waiting for transfers between devices: 40.1 us -> 37.9 us
  Pallas kernels: 37.3 us -> 35.5 us
    ppermute x9 -> x10, starting transfers between devices: 10.4 us -> 14.3 us  [both_ways(): return lax.ppermute(value, (axis, 'core'), pairs)]
    ppermute x9 -> x10, waiting for transfers between devices: 28.5 us -> 26.7 us  [both_ways(): return lax.ppermute(value, (axis, 'core'), pairs)]
    pallas_call x1, Pallas kernels: 11.5 us -> 10.1 us  [lse_call(): pl.pallas_call(kernel, out_shape=jax.ShapeDtypeStruct((16, 2, pools[0].sh...]
  transfers between devices with their start and end apart: 15 -> 16, of which waited for: 9 -> 9; matrix products, arithmetic and copies ran while one was open for 3% -> 2% of each run, Pallas kernels for 18% -> 18%
where the time goes in v4:
time: 125 us; the launch traced here: 124 us
  waiting for transfers between devices  37.9 us (30%)
  Pallas kernels  35.5 us (28%)
  starting transfers between devices  23.6 us (19%)
  blocking collectives  22.6 us (18%)
  other arithmetic  2.99 us (2%)
    ppermute x10, waiting for transfers between devices, both_ways(): return lax.ppermute(value, (axis, 'core'), pairs)  26.7 us
    all_to_all x1, blocking collectives, body(): stats = lax.all_to_all(stats, BLK, 0, 0, tiled=True)  22.6 us
    pallas_call x5, Pallas kernels, lse_call(): pl.pallas_call(kernel, out_shape=partial, in_specs=inputs, scratch_shapes...  22 us
    ppermute x10, starting transfers between devices, both_ways(): return lax.ppermute(value, (axis, 'core'), pairs)  14.3 us
    pallas_call x1, Pallas kernels, lse_call(): pl.pallas_call(kernel, out_shape=jax.ShapeDtypeStruct((16, 2, pools[0].sh...  10.1 us
    all_to_all x1, waiting for transfers between devices, body(): got = lax.all_to_all(send, ROW_GROUP, 0, 0)  5.7 us
    ppermute x1, waiting for transfers between devices, swap_x(): return lax.ppermute(value, ('xh', 'xl'), [(0, 3), (3, 0), (1, 2), (2, 1)])  5.49 us
    all_to_all x1, starting transfers between devices, body(): got = lax.all_to_all(send, ROW_GROUP, 0, 0)  4.18 us
  transfers between devices with their start and end apart: 16, of which 9 were waited for; matrix products, arithmetic and copies ran while one was open for 2% of the time, Pallas kernels for 18%

profile of v4, /device:TPU:32, one launch (start us, length us, event | category | flops | bytes accessed | tf_op | source)
XLA Modules:
  0.0 124.1 jit_solution(5020663077710365219)
XLA Ops:
  0.6 1.7 %collective-permute-start = (bf16[1024,768]{1,0:T(8,128)(2,1)}, bf16[1024,768]{1,0:T(8,128)(2,1)S(1)}, u32[]{:S(2)}, u32[]{:S(2)}) collective-permute-start(bf16[1024,768]{1,0:T(8,128)(2,1)} %refs_0_.5), channel_id=1, source_target_pairs={{0,32},{32,64},{64,96},{96,0},{1,97},{33,1},{65,33},{97,65},{2,34}... | collective-permute-start | bytes 4718600 | tf_op jit(solution)/shard_map/ppermute | solution.py:218
  2.3 1.0 pad_select_fusion.refs_1_.refs_2_
  3.3 2.8 %collective-permute-start.8 = (bf16[128,768]{1,0:T(8,128)(2,1)S(1)}, bf16[128,768]{1,0:T(8,128)(2,1)S(1)}, u32[]{:S(2)}, u32[]{:S(2)}) collective-permute-start(bf16[128,768]{1,0:T(8,128)(2,1)S(1)} %pad_select_fusion.refs_1_.refs_2_), channel_id=1, source_target_pairs={{0,130},{130,0},{2,128},{128,2},{1,131},{131,1},{3,129},{129,3},{4... | collective-permute-start | bytes 589832 | tf_op jit(solution)/shard_map/ppermute | solution.py:212
  6.2 0.7 collective-permute-start.4
  6.9 0.0 copy-start
  6.9 5.5 %collective-permute-done.8.refs_2_.refs_3_ = bf16[128,768]{1,0:T(8,128)(2,1)S(1)} collective-permute-done((bf16[128,768]{1,0:T(8,128)(2,1)S(1)}, bf16[128,768]{1,0:T(8,128)(2,1)S(1)}, u32[]{:S(2)}, u32[]{:S(2)}) %collective-permute-start.8) | collective-permute-done | bytes 196640 | tf_op jit(solution)/shard_map/ppermute | solution.py:212
  12.4 0.1 collective-permute-start.9
  12.5 10.0 %collective-permute-done.refs_0_.refs_1_ = bf16[1024,768]{1,0:T(8,128)(2,1)S(1)} collective-permute-done((bf16[1024,768]{1,0:T(8,128)(2,1)}, bf16[1024,768]{1,0:T(8,128)(2,1)S(1)}, u32[]{:S(2)}, u32[]{:S(2)}) %collective-permute-start) | collective-permute-done | bytes 1572896 | tf_op jit(solution)/shard_map/ppermute | solution.py:218
  22.5 0.1 constant_dynamic-slice_fusion
  22.6 0.4 collective-permute-start.2
  23.0 1.1 collective-permute-start.1
  24.1 0.0 collective-permute-done.4
  24.1 1.0 pad_maximum_fusion
  25.1 2.0 %collective-permute-start.5 = (bf16[256,768]{1,0:T(8,128)(2,1)S(1)}, bf16[256,768]{1,0:T(8,128)(2,1)S(1)}, u32[]{:S(2)}, u32[]{:S(2)}) collective-permute-start(bf16[256,768]{1,0:T(8,128)(2,1)S(1)} %pad_maximum_fusion), channel_id=1, source_target_pairs={{0,4},{4,8},{8,12},{12,16},{16,20},{20,24},{24,28},{28,0},{1,29},{... | collective-permute-start | bytes 1179656 | tf_op jit(solution)/shard_map/ppermute | solution.py:218
  27.1 0.0 collective-permute-done.9
  27.1 2.0 %collective-permute-start.10 = (bf16[256,768]{1,0:T(8,128)(2,1)S(1)}, bf16[256,768]{1,0:T(8,128)(2,1)S(1)}, u32[]{:S(2)}, u32[]{:S(2)}) collective-permute-start(bf16[256,768]{1,0:T(8,128)(2,1)S(1)} %pad_maximum_fusion.1), channel_id=1, source_target_pairs={{0,4},{4,8},{8,12},{12,16},{16,20},{20,24},{24,28},{28,0},{1,29},{... | collective-permute-start | bytes 1179656 | tf_op jit(solution)/shard_map/ppermute | solution.py:218
  29.1 3.8 %collective-permute-done.5.refs_3_.refs_4_ = bf16[256,768]{1,0:T(8,128)(2,1)S(1)} collective-permute-done((bf16[256,768]{1,0:T(8,128)(2,1)S(1)}, bf16[256,768]{1,0:T(8,128)(2,1)S(1)}, u32[]{:S(2)}, u32[]{:S(2)}) %collective-permute-start.5) | collective-permute-done | bytes 393248 | tf_op jit(solution)/shard_map/ppermute | solution.py:218
  32.9 1.9 %collective-permute-start.6 = (bf16[256,768]{1,0:T(8,128)(2,1)S(1)}, bf16[256,768]{1,0:T(8,128)(2,1)S(1)}, u32[]{:S(2)}, u32[]{:S(2)}) collective-permute-start(bf16[256,768]{1,0:T(8,128)(2,1)S(1)} %collective-permute-done.5.refs_3_.refs_4_), channel_id=1, source_target_pairs={{0,4},{4,8},{8,12},{12,16},{16,20},{20,24},{24,28},{28,0},{1,29},{... | collective-permute-start | bytes 1179656 | tf_op jit(solution)/shard_map/ppermute | solution.py:218
  34.8 2.3 %collective-permute-done.10.refs_3_.refs_5_ = bf16[256,768]{1,0:T(8,128)(2,1)S(1)} collective-permute-done((bf16[256,768]{1,0:T(8,128)(2,1)S(1)}, bf16[256,768]{1,0:T(8,128)(2,1)S(1)}, u32[]{:S(2)}, u32[]{:S(2)}) %collective-permute-start.10) | collective-permute-done | bytes 393248 | tf_op jit(solution)/shard_map/ppermute | solution.py:218
  37.1 1.9 %collective-permute-start.11 = (bf16[256,768]{1,0:T(8,128)(2,1)S(1)}, bf16[256,768]{1,0:T(8,128)(2,1)S(1)}, u32[]{:S(2)}, u32[]{:S(2)}) collective-permute-start(bf16[256,768]{1,0:T(8,128)(2,1)S(1)} %collective-permute-done.10.refs_3_.refs_5_), channel_id=1, source_target_pairs={{0,4},{4,8},{8,12},{12,16},{16,20},{20,24},{24,28},{28,0},{1,29},{... | collective-permute-start | bytes 1179656 | tf_op jit(solution)/shard_map/ppermute | solution.py:218
  39.0 0.0 collective-permute-done.2.refs_0_.refs_3_
  39.0 0.4 collective-permute-start.3
  39.5 3.1 %collective-permute-done.6.refs_4_.refs_6_ = bf16[256,768]{1,0:T(8,128)(2,1)S(1)} collective-permute-done((bf16[256,768]{1,0:T(8,128)(2,1)S(1)}, bf16[256,768]{1,0:T(8,128)(2,1)S(1)}, u32[]{:S(2)}, u32[]{:S(2)}) %collective-permute-start.6) | collective-permute-done | bytes 393248 | tf_op jit(solution)/shard_map/ppermute | solution.py:218
  42.6 0.6 collective-permute-start.7
  43.3 3.6 %collective-permute-done.11.refs_5_.refs_7_ = bf16[256,768]{1,0:T(8,128)(2,1)S(1)} collective-permute-done((bf16[256,768]{1,0:T(8,128)(2,1)S(1)}, bf16[256,768]{1,0:T(8,128)(2,1)S(1)}, u32[]{:S(2)}, u32[]{:S(2)}) %collective-permute-start.11) | collective-permute-done | bytes 393248 | tf_op jit(solution)/shard_map/ppermute | solution.py:218
  46.8 0.6 collective-permute-start.12
  47.5 0.0 copy-done
  47.5 2.7 %shard_map.50.refs_9_ = f32[2,8,128]{2,1,0:T(8,128)S(1)} custom-call(bf16[1024,768]{1,0:T(8,128)(2,1)S(1)} %copy-done, bf16[128,768]{1,0:T(8,128)(2,1)S(1)} %pad_select_fusion.refs_1_.refs_2_, bf16[128,768]{1,0:T(8,128)(2,1)S(1)} %collective-permute-done.8.refs_2_.refs_3_, bf16[256,768]{1,0:T(8,128)(2,1)S(1)} %collective-permute-done.5.refs_3_.refs_4_), custom_call_target="tpu_custom_call" | custom-call | flops 805306368 | bytes 2359296 | tf_op jit(solution)/shard_map/pallas_call | solution.py:173
  50.2 1.4 %collective-permute-done.7.refs_5_ = bf16[256,768]{1,0:T(8,128)(2,1)S(1)} collective-permute-done((bf16[256,768]{1,0:T(8,128)(2,1)S(1)}, bf16[256,768]{1,0:T(8,128)(2,1)S(1)}, u32[]{:S(2)}, u32[]{:S(2)}) %collective-permute-start.7) | collective-permute-done | bytes 393248 | tf_op jit(solution)/shard_map/ppermute | solution.py:218
  51.6 1.8 %collective-permute-start.13 = (bf16[256,768]{1,0:T(8,128)(2,1)S(1)}, bf16[256,768]{1,0:T(8,128)(2,1)S(1)}, u32[]{:S(2)}, u32[]{:S(2)}) collective-permute-start(bf16[256,768]{1,0:T(8,128)(2,1)S(1)} %collective-permute-done.7.refs_5_), channel_id=1, source_target_pairs={{0,4},{4,8},{8,12},{12,16},{16,20},{20,24},{24,28},{28,0},{1,29},{... | collective-permute-start | bytes 1179656 | tf_op jit(solution)/shard_map/ppermute | solution.py:218
  53.4 2.4 %collective-permute-done.12.refs_6_ = bf16[256,768]{1,0:T(8,128)(2,1)S(1)} collective-permute-done((bf16[256,768]{1,0:T(8,128)(2,1)S(1)}, bf16[256,768]{1,0:T(8,128)(2,1)S(1)}, u32[]{:S(2)}, u32[]{:S(2)}) %collective-permute-start.12) | collective-permute-done | bytes 393248 | tf_op jit(solution)/shard_map/ppermute | solution.py:218
  55.8 1.3 %collective-permute-start.14 = (bf16[256,768]{1,0:T(8,128)(2,1)S(1)}, bf16[256,768]{1,0:T(8,128)(2,1)S(1)}, u32[]{:S(2)}, u32[]{:S(2)}) collective-permute-start(bf16[256,768]{1,0:T(8,128)(2,1)S(1)} %collective-permute-done.12.refs_6_), channel_id=1, source_target_pairs={{0,4},{4,8},{8,12},{12,16},{16,20},{20,24},{24,28},{28,0},{1,29},{... | collective-permute-start | bytes 1179656 | tf_op jit(solution)/shard_map/ppermute | solution.py:218
  57.1 2.7 %shard_map.51.refs_10_ = f32[2,8,128]{2,1,0:T(8,128)S(1)} custom-call(bf16[1024,768]{1,0:T(8,128)(2,1)S(1)} %collective-permute-done.refs_0_.refs_1_, bf16[128,768]{1,0:T(8,128)(2,1)S(1)} %pad_select_fusion.refs_1_.refs_2_, bf16[128,768]{1,0:T(8,128)(2,1)S(1)} %collective-permute-done.8.refs_2_.refs_3_, ...), custom_call_target="tpu_custom_call" | custom-call | flops 805306368 | bytes 2359296 | tf_op jit(solution)/shard_map/pallas_call | solution.py:173
  59.8 0.0 collective-permute-done.3.refs_1_.refs_4_
  59.8 6.2 %shard_map.54.refs_13_ = f32[2,8,128]{2,1,0:T(8,128)S(1)} custom-call(bf16[512,768]{1,0:T(8,128)(2,1)S(1)} %collective-permute-done.2.refs_0_.refs_3_, bf16[512,768]{1,0:T(8,128)(2,1)S(1)} %collective-permute-done.3.refs_1_.refs_4_, bf16[128,768]{1,0:T(8,128)(2,1)S(1)} %pad_select_fusion.refs_1_.refs_2_, ...), custom_call_target="tpu_custom_call" | custom-call | flops 2013265920 | bytes 3538944 | tf_op jit(solution)/shard_map/pallas_call | solution.py:173
  66.0 0.0 collective-permute-done.1.refs_0_.refs_2_
  66.0 2.7 %shard_map.52.refs_11_ = f32[2,8,128]{2,1,0:T(8,128)S(1)} custom-call(bf16[1024,768]{1,0:T(8,128)(2,1)S(1)} %collective-permute-done.1.refs_0_.refs_2_, bf16[128,768]{1,0:T(8,128)(2,1)S(1)} %pad_select_fusion.refs_1_.refs_2_, bf16[128,768]{1,0:T(8,128)(2,1)S(1)} %collective-permute-done.8.refs_2_.refs_3_, ...), custom_call_target="tpu_custom_call" | custom-call | flops 805306368 | bytes 2359296 | tf_op jit(solution)/shard_map/pallas_call | solution.py:173
  68.8 7.7 %shard_map.53.refs_12_ = f32[2,24,128]{2,1,0:T(8,128)S(1)} custom-call(bf16[1024,768]{1,0:T(8,128)(2,1)S(1)} %copy-done, bf16[1024,768]{1,0:T(8,128)(2,1)S(1)} %collective-permute-done.refs_0_.refs_1_, bf16[1024,768]{1,0:T(8,128)(2,1)S(1)} %collective-permute-done.1.refs_0_.refs_2_, bf16[256,768]{1,0:T(8,128)(2,1)S(1)} %collective-permute-done.10.refs_3_.refs_5_, ...), custom_call_target="tpu_custom_call" | custom-call | flops 3623878656 | bytes 5898240 | tf_op jit(solution)/shard_map/pallas_call | solution.py:173
  76.5 0.0 collective-permute-done.13.refs_7_
  76.5 0.0 collective-permute-done.14.refs_8_
  76.5 10.1 %shard_map.55 = f32[16,2,8,128]{3,2,1,0:T(8,128)} custom-call(bf16[1024,768]{1,0:T(8,128)(2,1)S(1)} %copy-done, bf16[1024,768]{1,0:T(8,128)(2,1)S(1)} %collective-permute-done.refs_0_.refs_1_, bf16[1024,768]{1,0:T(8,128)(2,1)S(1)} %collective-permute-done.1.refs_0_.refs_2_, bf16[512,768]{1,0:T(8,128)(2,1)S(1)} %collective-permute-done.2.refs_0_.refs_3_, ...), custom_call_target="tpu_custom_call" | custom-call | flops 4831838208 | bytes 7471104 | tf_op jit(solution)/shard_map/pallas_call | solution.py:175
  86.6 4.2 %all-to-all-start = ((f32[16,2,8,128]{3,2,1,0:T(8,128)}), f32[16,2,8,128]{3,2,1,0:T(8,128)S(1)}, u32[]{:S(2)}, u32[]{:S(2)}) async-start(f32[16,2,8,128]{3,2,1,0:T(8,128)} %shard_map.55), calls=%async_computation | async-start | bytes 262144 | tf_op jit(solution)/shard_map/all_to_all | solution.py:258
  90.8 1.0 multiply_reduce_fusion
  91.8 5.7 %all-to-all-done.got = f32[16,2,8,128]{3,2,1,0:T(8,128)S(1)} async-done(((f32[16,2,8,128]{3,2,1,0:T(8,128)}), f32[16,2,8,128]{3,2,1,0:T(8,128)S(1)}, u32[]{:S(2)}, u32[]{:S(2)}) %all-to-all-start) | async-done | bytes 131104 | tf_op jit(solution)/shard_map/all_to_all | solution.py:258
  97.5 0.7 copy-done.1
  98.1 1.8 %shard_map.56 = (f32[8,128]{1,0:T(8,128)}, f32[64,128]{1,0:T(8,128)}) custom-call(f32[16,2,8,128]{3,2,1,0:T(8,128)} %copy-done.1, f32[8,128]{1,0:T(8,128)} %bitcast.9), custom_call_target="tpu_custom_call" | custom-call | tf_op jit(solution)/shard_map/pallas_call | solution.py:261
  99.9 22.6 %all_to_all.16 = f32[64,1,128]{2,1,0:T(1,128)} all-to-all(f32[64,1,128]{2,1,0:T(1,128)} %bitcast.8), channel_id=1, replica_groups=mesh['xh'=2,'y'=4,'z'=8,'xl'=2,'core'=2] {'xh','y','z'}, dimensions={0} | all-to-all | bytes 65536 | tf_op jit(solution)/shard_map/all_to_all | solution.py:267
  122.5 1.6 %shard_map.57 = f32[8,128]{1,0:T(8,128)} custom-call(f32[8,128]{1,0:T(8,128)} %get-tuple-element.4.ratio, f32[64,128]{1,0:T(8,128)} %bitcast.7), custom_call_target="tpu_custom_call" | custom-call | tf_op jit(solution)/shard_map/pallas_call | solution.py:268
  (3 shorter events, 0.0 us)
Async XLA Ops:
  0.6 21.9 %collective-permute-start = (bf16[1024,768]{1,0:T(8,128)(2,1)}, bf16[1024,768]{1,0:T(8,128)(2,1)S(1)}, u32[]{:S(2)}, u32[]{:S(2)}) collective-permute-start(bf16[1024,768]{1,0:T(8,128)(2,1)} %refs_0_.5), channel_id=1, source_target_pairs={{0,32},{32,64},{64,96},{96,0},{1,97},{33,1},{65,33},{97,65},{2,34}... | collective-permute-start | bytes 4718600 | tf_op jit(solution)/shard_map/ppermute | solution.py:218
  3.3 9.0 %collective-permute-start.8 = (bf16[128,768]{1,0:T(8,128)(2,1)S(1)}, bf16[128,768]{1,0:T(8,128)(2,1)S(1)}, u32[]{:S(2)}, u32[]{:S(2)}) collective-permute-start(bf16[128,768]{1,0:T(8,128)(2,1)S(1)} %pad_select_fusion.refs_1_.refs_2_), channel_id=1, source_target_pairs={{0,130},{130,0},{2,128},{128,2},{1,131},{131,1},{3,129},{129,3},{4... | collective-permute-start | bytes 589832 | tf_op jit(solution)/shard_map/ppermute | solution.py:212
  6.2 17.9 %collective-permute-start.4 = (bf16[128,768]{1,0:T(8,128)(2,1)S(1)}, bf16[128,768]{1,0:T(8,128)(2,1)}, u32[]{:S(2)}, u32[]{:S(2)}) collective-permute-start(bf16[128,768]{1,0:T(8,128)(2,1)S(1)} %pad_select_fusion.refs_1_.refs_2_), channel_id=1, source_target_pairs={{0,1},{1,0},{2,3},{3,2},{4,5},{5,4},{6,7},{7,6},{8,9},{9,8},{10,11... | collective-permute-start | bytes 589832 | tf_op jit(solution)/shard_map/ppermute | solution.py:208
  6.9 40.6 %copy-start = (bf16[1024,768]{1,0:T(8,128)(2,1)S(1)}, bf16[1024,768]{1,0:T(8,128)(2,1)}, u32[]{:S(2)}) copy-start(bf16[1024,768]{1,0:T(8,128)(2,1)} %refs_0_.5) | copy-start | bytes 4718596
  12.4 14.7 %collective-permute-start.9 = (bf16[128,768]{1,0:T(8,128)(2,1)S(1)}, bf16[128,768]{1,0:T(8,128)(2,1)S(1)}, u32[]{:S(2)}, u32[]{:S(2)}) collective-permute-start(bf16[128,768]{1,0:T(8,128)(2,1)S(1)} %collective-permute-done.8.refs_2_.refs_3_), channel_id=1, source_target_pairs={{0,1},{1,0},{2,3},{3,2},{4,5},{5,4},{6,7},{7,6},{8,9},{9,8},{10,11... | collective-permute-start | bytes 589832 | tf_op jit(solution)/shard_map/ppermute | solution.py:208
  22.6 16.4 %collective-permute-start.2 = (bf16[512,768]{1,0:T(8,128)(2,1)S(1)}, bf16[512,768]{1,0:T(8,128)(2,1)S(1)}, u32[]{:S(2)}, u32[]{:S(2)}) collective-permute-start(bf16[512,768]{1,0:T(8,128)(2,1)S(1)} %constant_dynamic-slice_fusion), channel_id=1, source_target_pairs={{0,32},{32,64},{64,96},{96,0},{1,97},{33,1},{65,33},{97,65},{2,34}... | collective-permute-start | bytes 2359304 | tf_op jit(solution)/shard_map/ppermute | solution.py:218
  23.0 43.0 %collective-permute-start.1 = (bf16[1024,768]{1,0:T(8,128)(2,1)S(1)}, bf16[1024,768]{1,0:T(8,128)(2,1)S(1)}, u32[]{:S(2)}, u32[]{:S(2)}) collective-permute-start(bf16[1024,768]{1,0:T(8,128)(2,1)S(1)} %collective-permute-done.refs_0_.refs_1_), channel_id=1, source_target_pairs={{0,1},{1,0},{2,3},{3,2},{4,5},{5,4},{6,7},{7,6},{8,9},{9,8},{10,11... | collective-permute-start | bytes 4718600 | tf_op jit(solution)/shard_map/ppermute | solution.py:208
  25.1 7.9 %collective-permute-start.5 = (bf16[256,768]{1,0:T(8,128)(2,1)S(1)}, bf16[256,768]{1,0:T(8,128)(2,1)S(1)}, u32[]{:S(2)}, u32[]{:S(2)}) collective-permute-start(bf16[256,768]{1,0:T(8,128)(2,1)S(1)} %pad_maximum_fusion), channel_id=1, source_target_pairs={{0,4},{4,8},{8,12},{12,16},{16,20},{20,24},{24,28},{28,0},{1,29},{... | collective-permute-start | bytes 1179656 | tf_op jit(solution)/shard_map/ppermute | solution.py:218
  27.1 10.0 %collective-permute-start.10 = (bf16[256,768]{1,0:T(8,128)(2,1)S(1)}, bf16[256,768]{1,0:T(8,128)(2,1)S(1)}, u32[]{:S(2)}, u32[]{:S(2)}) collective-permute-start(bf16[256,768]{1,0:T(8,128)(2,1)S(1)} %pad_maximum_fusion.1), channel_id=1, source_target_pairs={{0,4},{4,8},{8,12},{12,16},{16,20},{20,24},{24,28},{28,0},{1,29},{... | collective-permute-start | bytes 1179656 | tf_op jit(solution)/shard_map/ppermute | solution.py:218
  32.9 9.7 %collective-permute-start.6 = (bf16[256,768]{1,0:T(8,128)(2,1)S(1)}, bf16[256,768]{1,0:T(8,128)(2,1)S(1)}, u32[]{:S(2)}, u32[]{:S(2)}) collective-permute-start(bf16[256,768]{1,0:T(8,128)(2,1)S(1)} %collective-permute-done.5.refs_3_.refs_4_), channel_id=1, source_target_pairs={{0,4},{4,8},{8,12},{12,16},{16,20},{20,24},{24,28},{28,0},{1,29},{... | collective-permute-start | bytes 1179656 | tf_op jit(solution)/shard_map/ppermute | solution.py:218
  37.1 9.7 %collective-permute-start.11 = (bf16[256,768]{1,0:T(8,128)(2,1)S(1)}, bf16[256,768]{1,0:T(8,128)(2,1)S(1)}, u32[]{:S(2)}, u32[]{:S(2)}) collective-permute-start(bf16[256,768]{1,0:T(8,128)(2,1)S(1)} %collective-permute-done.10.refs_3_.refs_5_), channel_id=1, source_target_pairs={{0,4},{4,8},{8,12},{12,16},{16,20},{20,24},{24,28},{28,0},{1,29},{... | collective-permute-start | bytes 1179656 | tf_op jit(solution)/shard_map/ppermute | solution.py:218
  39.0 20.7 %collective-permute-start.3 = (bf16[512,768]{1,0:T(8,128)(2,1)S(1)}, bf16[512,768]{1,0:T(8,128)(2,1)S(1)}, u32[]{:S(2)}, u32[]{:S(2)}) collective-permute-start(bf16[512,768]{1,0:T(8,128)(2,1)S(1)} %collective-permute-done.2.refs_0_.refs_3_), channel_id=1, source_target_pairs={{0,1},{1,0},{2,3},{3,2},{4,5},{5,4},{6,7},{7,6},{8,9},{9,8},{10,11... | collective-permute-start | bytes 2359304 | tf_op jit(solution)/shard_map/ppermute | solution.py:208
  42.6 9.0 %collective-permute-start.7 = (bf16[256,768]{1,0:T(8,128)(2,1)S(1)}, bf16[256,768]{1,0:T(8,128)(2,1)S(1)}, u32[]{:S(2)}, u32[]{:S(2)}) collective-permute-start(bf16[256,768]{1,0:T(8,128)(2,1)S(1)} %collective-permute-done.6.refs_4_.refs_6_), channel_id=1, source_target_pairs={{0,4},{4,8},{8,12},{12,16},{16,20},{20,24},{24,28},{28,0},{1,29},{... | collective-permute-start | bytes 1179656 | tf_op jit(solution)/shard_map/ppermute | solution.py:218
  46.8 9.0 %collective-permute-start.12 = (bf16[256,768]{1,0:T(8,128)(2,1)S(1)}, bf16[256,768]{1,0:T(8,128)(2,1)S(1)}, u32[]{:S(2)}, u32[]{:S(2)}) collective-permute-start(bf16[256,768]{1,0:T(8,128)(2,1)S(1)} %collective-permute-done.11.refs_5_.refs_7_), channel_id=1, source_target_pairs={{0,4},{4,8},{8,12},{12,16},{16,20},{20,24},{24,28},{28,0},{1,29},{... | collective-permute-start | bytes 1179656 | tf_op jit(solution)/shard_map/ppermute | solution.py:218
  51.6 24.9 %collective-permute-start.13 = (bf16[256,768]{1,0:T(8,128)(2,1)S(1)}, bf16[256,768]{1,0:T(8,128)(2,1)S(1)}, u32[]{:S(2)}, u32[]{:S(2)}) collective-permute-start(bf16[256,768]{1,0:T(8,128)(2,1)S(1)} %collective-permute-done.7.refs_5_), channel_id=1, source_target_pairs={{0,4},{4,8},{8,12},{12,16},{16,20},{20,24},{24,28},{28,0},{1,29},{... | collective-permute-start | bytes 1179656 | tf_op jit(solution)/shard_map/ppermute | solution.py:218
  55.8 20.7 %collective-permute-start.14 = (bf16[256,768]{1,0:T(8,128)(2,1)S(1)}, bf16[256,768]{1,0:T(8,128)(2,1)S(1)}, u32[]{:S(2)}, u32[]{:S(2)}) collective-permute-start(bf16[256,768]{1,0:T(8,128)(2,1)S(1)} %collective-permute-done.12.refs_6_), channel_id=1, source_target_pairs={{0,4},{4,8},{8,12},{12,16},{16,20},{20,24},{24,28},{28,0},{1,29},{... | collective-permute-start | bytes 1179656 | tf_op jit(solution)/shard_map/ppermute | solution.py:218
  86.6 10.9 %all-to-all-start = ((f32[16,2,8,128]{3,2,1,0:T(8,128)}), f32[16,2,8,128]{3,2,1,0:T(8,128)S(1)}, u32[]{:S(2)}, u32[]{:S(2)}) async-start(f32[16,2,8,128]{3,2,1,0:T(8,128)} %shard_map.55), calls=%async_computation | async-start | bytes 262144 | tf_op jit(solution)/shard_map/all_to_all | solution.py:258
  97.5 0.7 copy-start.1

commit v5 on v4

--- a/solution.py
+++ b/solution.py
@@ -241,7 +241,7 @@
     zx2 = both_ways(zx1, "z")
     z3 = both_ways(z2, "z")
     zx3 = both_ways(zx2, "z")
-    z4, zx4 = both_ways(z3, "z"), both_ways(zx3, "z")
+    z4, zx4 = both_ways(z3[: 2 * each], "z"), both_ways(zx3[: 2 * each], "z")
     across = both_ways(lax.dynamic_slice_in_dim(beside, core * half, half, 0), "y")
     swapped = swap_core(beside)
     far = [across, swap_core(across)]
@@ -252,8 +252,7 @@
     near = [pool_embeds, beside, swapped]
     parts.append(lse_call(near, early, each, scale))
     parts.append(lse_call(far, earliest + early, each, scale))
-    used = (4 * each, 4 * each, 2 * each, 2 * each)
-    send = lse_call(near + far, late, each, scale, parts, used)
+    send = lse_call(near + far, late, each, scale, parts)
 
     got = lax.all_to_all(send, ROW_GROUP, 0, 0)
     dense = (count // 128, 128)

time: 125 us -> 126 us (level)
  Pallas kernels: 35.5 us -> 37.5 us
  waiting for transfers between devices: 37.9 us -> 35.9 us
    ppermute x10, waiting for transfers between devices: 26.7 us -> 24.7 us  [both_ways(): return lax.ppermute(value, (axis, 'core'), pairs)]
    pallas_call x5, Pallas kernels: 22 us -> 23.6 us  [lse_call(): pl.pallas_call(kernel, out_shape=partial, in_specs=inputs, scratch_shapes...]
  transfers between devices with their start and end apart: 16 -> 16, of which waited for: 9 -> 9; matrix products, arithmetic and copies ran while one was open for 2% -> 3% of each run, Pallas kernels for 18% -> 19%
where the time goes in v5:
time: 126 us; the launch traced here: 125 us
  Pallas kernels  37.5 us (30%)
  waiting for transfers between devices  35.9 us (28%)
  starting transfers between devices  23.6 us (19%)
  blocking collectives  22.6 us (18%)
  other arithmetic  4.04 us (3%)
    ppermute x10, waiting for transfers between devices, both_ways(): return lax.ppermute(value, (axis, 'core'), pairs)  24.7 us
    pallas_call x5, Pallas kernels, lse_call(): pl.pallas_call(kernel, out_shape=partial, in_specs=inputs, scratch_shapes...  23.6 us
    all_to_all x1, blocking collectives, body(): stats = lax.all_to_all(stats, BLK, 0, 0, tiled=True)  22.6 us
    ppermute x10, starting transfers between devices, both_ways(): return lax.ppermute(value, (axis, 'core'), pairs)  14.6 us
    pallas_call x1, Pallas kernels, lse_call(): pl.pallas_call(kernel, out_shape=jax.ShapeDtypeStruct((16, 2, pools[0].sh...  10.5 us
    all_to_all x1, waiting for transfers between devices, body(): got = lax.all_to_all(send, ROW_GROUP, 0, 0)  5.7 us
    ppermute x1, waiting for transfers between devices, swap_x(): return lax.ppermute(value, ('xh', 'xl'), [(0, 3), (3, 0), (1, 2), (2, 1)])  5.49 us
    all_to_all x1, starting transfers between devices, body(): got = lax.all_to_all(send, ROW_GROUP, 0, 0)  4.29 us
  transfers between devices with their start and end apart: 16, of which 9 were waited for; matrix products, arithmetic and copies ran while one was open for 3% of the time, Pallas kernels for 19%

profile of v5, /device:TPU:32, one launch (start us, length us, event | category | flops | bytes accessed | tf_op | source)
XLA Modules:
  0.0 125.0 jit_solution(9911536855312413134)
XLA Ops:
  0.6 1.7 %collective-permute-start = (bf16[1024,768]{1,0:T(8,128)(2,1)}, bf16[1024,768]{1,0:T(8,128)(2,1)S(1)}, u32[]{:S(2)}, u32[]{:S(2)}) collective-permute-start(bf16[1024,768]{1,0:T(8,128)(2,1)} %refs_0_.5), channel_id=1, source_target_pairs={{0,32},{32,64},{64,96},{96,0},{1,97},{33,1},{65,33},{97,65},{2,34}... | collective-permute-start | bytes 4718600 | tf_op jit(solution)/shard_map/ppermute | solution.py:218
  2.3 1.0 pad_select_fusion.refs_1_.refs_2_
  3.3 2.8 %collective-permute-start.8 = (bf16[128,768]{1,0:T(8,128)(2,1)S(1)}, bf16[128,768]{1,0:T(8,128)(2,1)S(1)}, u32[]{:S(2)}, u32[]{:S(2)}) collective-permute-start(bf16[128,768]{1,0:T(8,128)(2,1)S(1)} %pad_select_fusion.refs_1_.refs_2_), channel_id=1, source_target_pairs={{0,130},{130,0},{2,128},{128,2},{1,131},{131,1},{3,129},{129,3},{4... | collective-permute-start | bytes 589832 | tf_op jit(solution)/shard_map/ppermute | solution.py:212
  6.2 0.7 collective-permute-start.4
  6.9 5.5 %collective-permute-done.8.refs_2_.refs_3_ = bf16[128,768]{1,0:T(8,128)(2,1)S(1)} collective-permute-done((bf16[128,768]{1,0:T(8,128)(2,1)S(1)}, bf16[128,768]{1,0:T(8,128)(2,1)S(1)}, u32[]{:S(2)}, u32[]{:S(2)}) %collective-permute-start.8) | collective-permute-done | bytes 196640 | tf_op jit(solution)/shard_map/ppermute | solution.py:212
  12.4 0.1 collective-permute-start.9
  12.5 10.0 %collective-permute-done.refs_0_.refs_1_ = bf16[1024,768]{1,0:T(8,128)(2,1)S(1)} collective-permute-done((bf16[1024,768]{1,0:T(8,128)(2,1)}, bf16[1024,768]{1,0:T(8,128)(2,1)S(1)}, u32[]{:S(2)}, u32[]{:S(2)}) %collective-permute-start) | collective-permute-done | bytes 1572896 | tf_op jit(solution)/shard_map/ppermute | solution.py:218
  22.5 0.0 collective-permute-start.1
  22.5 0.0 collective-permute-done.4
  22.6 1.1 pad_maximum_fusion
  23.6 2.0 %collective-permute-start.5 = (bf16[256,768]{1,0:T(8,128)(2,1)S(1)}, bf16[256,768]{1,0:T(8,128)(2,1)S(1)}, u32[]{:S(2)}, u32[]{:S(2)}) collective-permute-start(bf16[256,768]{1,0:T(8,128)(2,1)S(1)} %pad_maximum_fusion), channel_id=1, source_target_pairs={{0,4},{4,8},{8,12},{12,16},{16,20},{20,24},{24,28},{28,0},{1,29},{... | collective-permute-start | bytes 1179656 | tf_op jit(solution)/shard_map/ppermute | solution.py:218
  25.6 0.0 collective-permute-done.9
  25.6 1.0 pad_maximum_fusion.1
  26.6 2.0 %collective-permute-start.10 = (bf16[256,768]{1,0:T(8,128)(2,1)S(1)}, bf16[256,768]{1,0:T(8,128)(2,1)S(1)}, u32[]{:S(2)}, u32[]{:S(2)}) collective-permute-start(bf16[256,768]{1,0:T(8,128)(2,1)S(1)} %pad_maximum_fusion.1), channel_id=1, source_target_pairs={{0,4},{4,8},{8,12},{12,16},{16,20},{20,24},{24,28},{28,0},{1,29},{... | collective-permute-start | bytes 1179656 | tf_op jit(solution)/shard_map/ppermute | solution.py:218
  28.6 0.1 constant_dynamic-slice_fusion
  28.6 0.4 collective-permute-start.2
  29.1 2.4 %collective-permute-done.5.refs_3_.refs_4_ = bf16[256,768]{1,0:T(8,128)(2,1)S(1)} collective-permute-done((bf16[256,768]{1,0:T(8,128)(2,1)S(1)}, bf16[256,768]{1,0:T(8,128)(2,1)S(1)}, u32[]{:S(2)}, u32[]{:S(2)}) %collective-permute-start.5) | collective-permute-done | bytes 393248 | tf_op jit(solution)/shard_map/ppermute | solution.py:218
  31.5 1.9 %collective-permute-start.6 = (bf16[256,768]{1,0:T(8,128)(2,1)S(1)}, bf16[256,768]{1,0:T(8,128)(2,1)S(1)}, u32[]{:S(2)}, u32[]{:S(2)}) collective-permute-start(bf16[256,768]{1,0:T(8,128)(2,1)S(1)} %collective-permute-done.5.refs_3_.refs_4_), channel_id=1, source_target_pairs={{0,4},{4,8},{8,12},{12,16},{16,20},{20,24},{24,28},{28,0},{1,29},{... | collective-permute-start | bytes 1179656 | tf_op jit(solution)/shard_map/ppermute | solution.py:218
  33.4 2.3 %collective-permute-done.10.refs_3_.refs_5_ = bf16[256,768]{1,0:T(8,128)(2,1)S(1)} collective-permute-done((bf16[256,768]{1,0:T(8,128)(2,1)S(1)}, bf16[256,768]{1,0:T(8,128)(2,1)S(1)}, u32[]{:S(2)}, u32[]{:S(2)}) %collective-permute-start.10) | collective-permute-done | bytes 393248 | tf_op jit(solution)/shard_map/ppermute | solution.py:218
  35.7 1.9 %collective-permute-start.11 = (bf16[256,768]{1,0:T(8,128)(2,1)S(1)}, bf16[256,768]{1,0:T(8,128)(2,1)S(1)}, u32[]{:S(2)}, u32[]{:S(2)}) collective-permute-start(bf16[256,768]{1,0:T(8,128)(2,1)S(1)} %collective-permute-done.10.refs_3_.refs_5_), channel_id=1, source_target_pairs={{0,4},{4,8},{8,12},{12,16},{16,20},{20,24},{24,28},{28,0},{1,29},{... | collective-permute-start | bytes 1179656 | tf_op jit(solution)/shard_map/ppermute | solution.py:218
  37.6 3.6 %collective-permute-done.6.refs_4_.refs_6_ = bf16[256,768]{1,0:T(8,128)(2,1)S(1)} collective-permute-done((bf16[256,768]{1,0:T(8,128)(2,1)S(1)}, bf16[256,768]{1,0:T(8,128)(2,1)S(1)}, u32[]{:S(2)}, u32[]{:S(2)}) %collective-permute-start.6) | collective-permute-done | bytes 393248 | tf_op jit(solution)/shard_map/ppermute | solution.py:218
  41.2 0.6 collective-permute-start.7
  41.8 3.6 %collective-permute-done.11.refs_5_.refs_7_ = bf16[256,768]{1,0:T(8,128)(2,1)S(1)} collective-permute-done((bf16[256,768]{1,0:T(8,128)(2,1)S(1)}, bf16[256,768]{1,0:T(8,128)(2,1)S(1)}, u32[]{:S(2)}, u32[]{:S(2)}) %collective-permute-start.11) | collective-permute-done | bytes 393248 | tf_op jit(solution)/shard_map/ppermute | solution.py:218
  45.4 0.6 collective-permute-start.12
  46.0 0.0 collective-permute-done.2.refs_0_.refs_3_
  46.0 0.9 collective-permute-start.3
  47.0 0.0 copy-done
  47.0 2.7 %shard_map.50.refs_9_ = f32[2,8,128]{2,1,0:T(8,128)S(1)} custom-call(bf16[1024,768]{1,0:T(8,128)(2,1)S(1)} %copy-done, bf16[128,768]{1,0:T(8,128)(2,1)S(1)} %pad_select_fusion.refs_1_.refs_2_, bf16[128,768]{1,0:T(8,128)(2,1)S(1)} %collective-permute-done.8.refs_2_.refs_3_, bf16[256,768]{1,0:T(8,128)(2,1)S(1)} %collective-permute-done.5.refs_3_.refs_4_), custom_call_target="tpu_custom_call" | custom-call | flops 805306368 | bytes 2359296 | tf_op jit(solution)/shard_map/pallas_call | solution.py:173
  49.7 0.4 collective-permute-done.7.refs_5_
  50.2 1.8 %collective-permute-start.13 = (bf16[128,768]{1,0:T(8,128)(2,1)S(1)}, bf16[128,768]{1,0:T(8,128)(2,1)S(1)}, u32[]{:S(2)}, u32[]{:S(2)}) collective-permute-start(bf16[128,768]{1,0:T(8,128)(2,1)S(1)} %slice.8), channel_id=1, source_target_pairs={{0,4},{4,8},{8,12},{12,16},{16,20},{20,24},{24,28},{28,0},{1,29},{... | collective-permute-start | bytes 589832 | tf_op jit(solution)/shard_map/ppermute | solution.py:218
  52.0 2.4 %collective-permute-done.12.refs_6_ = bf16[256,768]{1,0:T(8,128)(2,1)S(1)} collective-permute-done((bf16[256,768]{1,0:T(8,128)(2,1)S(1)}, bf16[256,768]{1,0:T(8,128)(2,1)S(1)}, u32[]{:S(2)}, u32[]{:S(2)}) %collective-permute-start.12) | collective-permute-done | bytes 393248 | tf_op jit(solution)/shard_map/ppermute | solution.py:218
  54.4 1.6 %collective-permute-start.14 = (bf16[128,768]{1,0:T(8,128)(2,1)S(1)}, bf16[128,768]{1,0:T(8,128)(2,1)S(1)}, u32[]{:S(2)}, u32[]{:S(2)}) collective-permute-start(bf16[128,768]{1,0:T(8,128)(2,1)S(1)} %slice.9), channel_id=1, source_target_pairs={{0,4},{4,8},{8,12},{12,16},{16,20},{20,24},{24,28},{28,0},{1,29},{... | collective-permute-start | bytes 589832 | tf_op jit(solution)/shard_map/ppermute | solution.py:218
  56.0 2.7 %shard_map.51.refs_10_ = f32[2,8,128]{2,1,0:T(8,128)S(1)} custom-call(bf16[1024,768]{1,0:T(8,128)(2,1)S(1)} %collective-permute-done.refs_0_.refs_1_, bf16[128,768]{1,0:T(8,128)(2,1)S(1)} %pad_select_fusion.refs_1_.refs_2_, bf16[128,768]{1,0:T(8,128)(2,1)S(1)} %collective-permute-done.8.refs_2_.refs_3_, ...), custom_call_target="tpu_custom_call" | custom-call | flops 805306368 | bytes 2359296 | tf_op jit(solution)/shard_map/pallas_call | solution.py:173
  58.7 0.0 collective-permute-done.1.refs_0_.refs_2_
  58.7 8.2 %shard_map.53.refs_12_ = f32[2,24,128]{2,1,0:T(8,128)S(1)} custom-call(bf16[1024,768]{1,0:T(8,128)(2,1)S(1)} %copy-done, bf16[1024,768]{1,0:T(8,128)(2,1)S(1)} %collective-permute-done.refs_0_.refs_1_, bf16[1024,768]{1,0:T(8,128)(2,1)} %collective-permute-done.1.refs_0_.refs_2_, bf16[256,768]{1,0:T(8,128)(2,1)S(1)} %collective-permute-done.10.refs_3_.refs_5_, ...), custom_call_target="tpu_custom_call" | custom-call | flops 3623878656 | bytes 5898240 | tf_op jit(solution)/shard_map/pallas_call | solution.py:173
  66.9 3.8 %shard_map.52.refs_11_ = f32[2,8,128]{2,1,0:T(8,128)S(1)} custom-call(bf16[1024,768]{1,0:T(8,128)(2,1)} %collective-permute-done.1.refs_0_.refs_2_, bf16[128,768]{1,0:T(8,128)(2,1)S(1)} %pad_select_fusion.refs_1_.refs_2_, bf16[128,768]{1,0:T(8,128)(2,1)S(1)} %collective-permute-done.8.refs_2_.refs_3_, bf16[256,768]{1,0:T(8,128)(2,1)S(1)} %collective-permute-done.5.refs_3_.refs_4_), custom_call_target="tpu_custom_call" | custom-call | flops 805306368 | bytes 2359296 | tf_op jit(solution)/shard_map/pallas_call | solution.py:173
  70.7 0.0 collective-permute-done.3.refs_1_.refs_4_
  70.7 6.2 %shard_map.54.refs_13_ = f32[2,8,128]{2,1,0:T(8,128)S(1)} custom-call(bf16[512,768]{1,0:T(8,128)(2,1)S(1)} %collective-permute-done.2.refs_0_.refs_3_, bf16[512,768]{1,0:T(8,128)(2,1)S(1)} %collective-permute-done.3.refs_1_.refs_4_, bf16[128,768]{1,0:T(8,128)(2,1)S(1)} %pad_select_fusion.refs_1_.refs_2_, ...), custom_call_target="tpu_custom_call" | custom-call | flops 2013265920 | bytes 3538944 | tf_op jit(solution)/shard_map/pallas_call | solution.py:173
  76.9 0.0 collective-permute-done.13.refs_7_
  76.9 0.0 collective-permute-done.14.refs_8_
  76.9 10.5 %shard_map.55 = f32[16,2,8,128]{3,2,1,0:T(8,128)} custom-call(bf16[1024,768]{1,0:T(8,128)(2,1)S(1)} %copy-done, bf16[1024,768]{1,0:T(8,128)(2,1)S(1)} %collective-permute-done.refs_0_.refs_1_, bf16[1024,768]{1,0:T(8,128)(2,1)} %collective-permute-done.1.refs_0_.refs_2_, bf16[512,768]{1,0:T(8,128)(2,1)S(1)} %collective-permute-done.2.refs_0_.refs_3_, ...), custom_call_target="tpu_custom_call" | custom-call | flops 4831838208 | bytes 7471104 | tf_op jit(solution)/shard_map/pallas_call | solution.py:175
  87.4 4.3 %all-to-all-start = ((f32[16,2,8,128]{3,2,1,0:T(8,128)}), f32[16,2,8,128]{3,2,1,0:T(8,128)S(1)}, u32[]{:S(2)}, u32[]{:S(2)}) async-start(f32[16,2,8,128]{3,2,1,0:T(8,128)} %shard_map.55), calls=%async_computation | async-start | bytes 262144 | tf_op jit(solution)/shard_map/all_to_all | solution.py:257
  91.8 1.0 multiply_reduce_fusion
  92.7 5.7 %all-to-all-done.got = f32[16,2,8,128]{3,2,1,0:T(8,128)S(1)} async-done(((f32[16,2,8,128]{3,2,1,0:T(8,128)}), f32[16,2,8,128]{3,2,1,0:T(8,128)S(1)}, u32[]{:S(2)}, u32[]{:S(2)}) %all-to-all-start) | async-done | bytes 131104 | tf_op jit(solution)/shard_map/all_to_all | solution.py:257
  98.4 0.7 copy-done.1
  99.1 1.8 %shard_map.56 = (f32[8,128]{1,0:T(8,128)}, f32[64,128]{1,0:T(8,128)}) custom-call(f32[16,2,8,128]{3,2,1,0:T(8,128)} %copy-done.1, f32[8,128]{1,0:T(8,128)} %bitcast.9), custom_call_target="tpu_custom_call" | custom-call | tf_op jit(solution)/shard_map/pallas_call | solution.py:260
  100.9 22.6 %all_to_all.16 = f32[64,1,128]{2,1,0:T(1,128)} all-to-all(f32[64,1,128]{2,1,0:T(1,128)} %bitcast.8), channel_id=1, replica_groups=mesh['xh'=2,'y'=4,'z'=8,'xl'=2,'core'=2] {'xh','y','z'}, dimensions={0} | all-to-all | bytes 65536 | tf_op jit(solution)/shard_map/all_to_all | solution.py:266
  123.4 1.6 %shard_map.57 = f32[8,128]{1,0:T(8,128)} custom-call(f32[8,128]{1,0:T(8,128)} %get-tuple-element.4.ratio, f32[64,128]{1,0:T(8,128)} %bitcast.7), custom_call_target="tpu_custom_call" | custom-call | tf_op jit(solution)/shard_map/pallas_call | solution.py:267
  (5 shorter events, 0.0 us)
Async XLA Ops:
  0.6 21.9 %collective-permute-start = (bf16[1024,768]{1,0:T(8,128)(2,1)}, bf16[1024,768]{1,0:T(8,128)(2,1)S(1)}, u32[]{:S(2)}, u32[]{:S(2)}) collective-permute-start(bf16[1024,768]{1,0:T(8,128)(2,1)} %refs_0_.5), channel_id=1, source_target_pairs={{0,32},{32,64},{64,96},{96,0},{1,97},{33,1},{65,33},{97,65},{2,34}... | collective-permute-start | bytes 4718600 | tf_op jit(solution)/shard_map/ppermute | solution.py:218
  3.3 9.0 %collective-permute-start.8 = (bf16[128,768]{1,0:T(8,128)(2,1)S(1)}, bf16[128,768]{1,0:T(8,128)(2,1)S(1)}, u32[]{:S(2)}, u32[]{:S(2)}) collective-permute-start(bf16[128,768]{1,0:T(8,128)(2,1)S(1)} %pad_select_fusion.refs_1_.refs_2_), channel_id=1, source_target_pairs={{0,130},{130,0},{2,128},{128,2},{1,131},{131,1},{3,129},{129,3},{4... | collective-permute-start | bytes 589832 | tf_op jit(solution)/shard_map/ppermute | solution.py:212
  6.2 16.4 %collective-permute-start.4 = (bf16[128,768]{1,0:T(8,128)(2,1)S(1)}, bf16[128,768]{1,0:T(8,128)(2,1)}, u32[]{:S(2)}, u32[]{:S(2)}) collective-permute-start(bf16[128,768]{1,0:T(8,128)(2,1)S(1)} %pad_select_fusion.refs_1_.refs_2_), channel_id=1, source_target_pairs={{0,1},{1,0},{2,3},{3,2},{4,5},{5,4},{6,7},{7,6},{8,9},{9,8},{10,11... | collective-permute-start | bytes 589832 | tf_op jit(solution)/shard_map/ppermute | solution.py:208
  12.4 13.2 %collective-permute-start.9 = (bf16[128,768]{1,0:T(8,128)(2,1)S(1)}, bf16[128,768]{1,0:T(8,128)(2,1)}, u32[]{:S(2)}, u32[]{:S(2)}) collective-permute-start(bf16[128,768]{1,0:T(8,128)(2,1)S(1)} %collective-permute-done.8.refs_2_.refs_3_), channel_id=1, source_target_pairs={{0,1},{1,0},{2,3},{3,2},{4,5},{5,4},{6,7},{7,6},{8,9},{9,8},{10,11... | collective-permute-start | bytes 589832 | tf_op jit(solution)/shard_map/ppermute | solution.py:208
  22.5 36.1 %collective-permute-start.1 = (bf16[1024,768]{1,0:T(8,128)(2,1)S(1)}, bf16[1024,768]{1,0:T(8,128)(2,1)}, u32[]{:S(2)}, u32[]{:S(2)}) collective-permute-start(bf16[1024,768]{1,0:T(8,128)(2,1)S(1)} %collective-permute-done.refs_0_.refs_1_), channel_id=1, source_target_pairs={{0,1},{1,0},{2,3},{3,2},{4,5},{5,4},{6,7},{7,6},{8,9},{9,8},{10,11... | collective-permute-start | bytes 4718600 | tf_op jit(solution)/shard_map/ppermute | solution.py:208
  22.5 24.4 %copy-start = (bf16[1024,768]{1,0:T(8,128)(2,1)S(1)}, bf16[1024,768]{1,0:T(8,128)(2,1)}, u32[]{:S(2)}) copy-start(bf16[1024,768]{1,0:T(8,128)(2,1)} %refs_0_.5) | copy-start | bytes 4718596
  23.6 7.9 %collective-permute-start.5 = (bf16[256,768]{1,0:T(8,128)(2,1)S(1)}, bf16[256,768]{1,0:T(8,128)(2,1)S(1)}, u32[]{:S(2)}, u32[]{:S(2)}) collective-permute-start(bf16[256,768]{1,0:T(8,128)(2,1)S(1)} %pad_maximum_fusion), channel_id=1, source_target_pairs={{0,4},{4,8},{8,12},{12,16},{16,20},{20,24},{24,28},{28,0},{1,29},{... | collective-permute-start | bytes 1179656 | tf_op jit(solution)/shard_map/ppermute | solution.py:218
  26.6 9.1 %collective-permute-start.10 = (bf16[256,768]{1,0:T(8,128)(2,1)S(1)}, bf16[256,768]{1,0:T(8,128)(2,1)S(1)}, u32[]{:S(2)}, u32[]{:S(2)}) collective-permute-start(bf16[256,768]{1,0:T(8,128)(2,1)S(1)} %pad_maximum_fusion.1), channel_id=1, source_target_pairs={{0,4},{4,8},{8,12},{12,16},{16,20},{20,24},{24,28},{28,0},{1,29},{... | collective-permute-start | bytes 1179656 | tf_op jit(solution)/shard_map/ppermute | solution.py:218
  28.6 17.4 %collective-permute-start.2 = (bf16[512,768]{1,0:T(8,128)(2,1)S(1)}, bf16[512,768]{1,0:T(8,128)(2,1)S(1)}, u32[]{:S(2)}, u32[]{:S(2)}) collective-permute-start(bf16[512,768]{1,0:T(8,128)(2,1)S(1)} %constant_dynamic-slice_fusion), channel_id=1, source_target_pairs={{0,32},{32,64},{64,96},{96,0},{1,97},{33,1},{65,33},{97,65},{2,34}... | collective-permute-start | bytes 2359304 | tf_op jit(solution)/shard_map/ppermute | solution.py:218
  31.5 9.7 %collective-permute-start.6 = (bf16[256,768]{1,0:T(8,128)(2,1)S(1)}, bf16[256,768]{1,0:T(8,128)(2,1)S(1)}, u32[]{:S(2)}, u32[]{:S(2)}) collective-permute-start(bf16[256,768]{1,0:T(8,128)(2,1)S(1)} %collective-permute-done.5.refs_3_.refs_4_), channel_id=1, source_target_pairs={{0,4},{4,8},{8,12},{12,16},{16,20},{20,24},{24,28},{28,0},{1,29},{... | collective-permute-start | bytes 1179656 | tf_op jit(solution)/shard_map/ppermute | solution.py:218
  35.7 9.7 %collective-permute-start.11 = (bf16[256,768]{1,0:T(8,128)(2,1)S(1)}, bf16[256,768]{1,0:T(8,128)(2,1)S(1)}, u32[]{:S(2)}, u32[]{:S(2)}) collective-permute-start(bf16[256,768]{1,0:T(8,128)(2,1)S(1)} %collective-permute-done.10.refs_3_.refs_5_), channel_id=1, source_target_pairs={{0,4},{4,8},{8,12},{12,16},{16,20},{20,24},{24,28},{28,0},{1,29},{... | collective-permute-start | bytes 1179656 | tf_op jit(solution)/shard_map/ppermute | solution.py:218
  41.2 9.0 %collective-permute-start.7 = (bf16[256,768]{1,0:T(8,128)(2,1)S(1)}, bf16[256,768]{1,0:T(8,128)(2,1)S(1)}, u32[]{:S(2)}, u32[]{:S(2)}) collective-permute-start(bf16[256,768]{1,0:T(8,128)(2,1)S(1)} %collective-permute-done.6.refs_4_.refs_6_), channel_id=1, source_target_pairs={{0,4},{4,8},{8,12},{12,16},{16,20},{20,24},{24,28},{28,0},{1,29},{... | collective-permute-start | bytes 1179656 | tf_op jit(solution)/shard_map/ppermute | solution.py:218
  45.4 9.0 %collective-permute-start.12 = (bf16[256,768]{1,0:T(8,128)(2,1)S(1)}, bf16[256,768]{1,0:T(8,128)(2,1)S(1)}, u32[]{:S(2)}, u32[]{:S(2)}) collective-permute-start(bf16[256,768]{1,0:T(8,128)(2,1)S(1)} %collective-permute-done.11.refs_5_.refs_7_), channel_id=1, source_target_pairs={{0,4},{4,8},{8,12},{12,16},{16,20},{20,24},{24,28},{28,0},{1,29},{... | collective-permute-start | bytes 1179656 | tf_op jit(solution)/shard_map/ppermute | solution.py:218
  46.0 24.6 %collective-permute-start.3 = (bf16[512,768]{1,0:T(8,128)(2,1)S(1)}, bf16[512,768]{1,0:T(8,128)(2,1)S(1)}, u32[]{:S(2)}, u32[]{:S(2)}) collective-permute-start(bf16[512,768]{1,0:T(8,128)(2,1)S(1)} %collective-permute-done.2.refs_0_.refs_3_), channel_id=1, source_target_pairs={{0,1},{1,0},{2,3},{3,2},{4,5},{5,4},{6,7},{7,6},{8,9},{9,8},{10,11... | collective-permute-start | bytes 2359304 | tf_op jit(solution)/shard_map/ppermute | solution.py:208
  50.2 26.7 %collective-permute-start.13 = (bf16[128,768]{1,0:T(8,128)(2,1)S(1)}, bf16[128,768]{1,0:T(8,128)(2,1)S(1)}, u32[]{:S(2)}, u32[]{:S(2)}) collective-permute-start(bf16[128,768]{1,0:T(8,128)(2,1)S(1)} %slice.8), channel_id=1, source_target_pairs={{0,4},{4,8},{8,12},{12,16},{16,20},{20,24},{24,28},{28,0},{1,29},{... | collective-permute-start | bytes 589832 | tf_op jit(solution)/shard_map/ppermute | solution.py:218
  54.4 22.5 %collective-permute-start.14 = (bf16[128,768]{1,0:T(8,128)(2,1)S(1)}, bf16[128,768]{1,0:T(8,128)(2,1)S(1)}, u32[]{:S(2)}, u32[]{:S(2)}) collective-permute-start(bf16[128,768]{1,0:T(8,128)(2,1)S(1)} %slice.9), channel_id=1, source_target_pairs={{0,4},{4,8},{8,12},{12,16},{16,20},{20,24},{24,28},{28,0},{1,29},{... | collective-permute-start | bytes 589832 | tf_op jit(solution)/shard_map/ppermute | solution.py:218
  87.4 11.0 %all-to-all-start = ((f32[16,2,8,128]{3,2,1,0:T(8,128)}), f32[16,2,8,128]{3,2,1,0:T(8,128)S(1)}, u32[]{:S(2)}, u32[]{:S(2)}) async-start(f32[16,2,8,128]{3,2,1,0:T(8,128)} %shard_map.55), calls=%async_computation | async-start | bytes 262144 | tf_op jit(solution)/shard_map/all_to_all | solution.py:257
  98.4 0.7 copy-start.1
